TPU v7x, 128 devices: a whole 4x4x4 slice. The times are simulated.
128 devices in a mesh: brick: 16 (over z, y), narrow: 8 (over x, core).
Axes of the slice: x: 4, y: 4, z: 4, core: 2. Of those that a mesh axis runs over, the one named last changes fastest.
Arguments:
- potential: float32 [64, 32, 128], P('brick', 'narrow'), may hold values from -1 to 1
- functions: bfloat16 [16, 8, 64, 8, 8, 128], P('brick', 'narrow'), may hold values from -6 to 6
- kernel_store: bfloat16 [32768, 1152], P(('brick', 'narrow')), may hold values from -0.25 to 0.25
- owners: int32 [4096, 1], P(('brick', 'narrow')), may hold values from 0 to 127; in each aligned block of 32 rows (0 to 31, 32 to 63, ...) at most 2 rows name the same one
Outputs:
- pair_blocks: float32 [32768, 2, 1152], P(('brick', 'narrow'))
- gradients: bfloat16 [16, 8, 64, 8, 8, 128], P('brick', 'narrow')
Inputs may be any that keep to these rules, and one draw needn't show every extreme that they name: `owners`: no more than 2 atoms of one brick share an owner, and in every draw some brick has exactly 2 atoms with one owner.
All inputs are finite; a program needn't handle non-finite values.
Results may differ from a plain program's by a relative error of at most 0.001.
Values may be sent and summed in bfloat16 or wider, within the bound.
No kernel may reach another device: no remote copies, remote signals or barrier semaphores. Data moves between devices by JAX's collectives and lax.ppermute only.
A program may use at most 64 MiB of HBM per device.

v0:
```python
import jax
import jax.numpy as jnp
from jax import lax
from jax.sharding import PartitionSpec as P

OFFSETS = ((0, 0), (1, 0), (-1, 0), (0, 1), (0, -1), (1, 1), (1, -1), (-1, 1), (-1, -1))


def shifted(shard, axis, by):
    size = lax.axis_size(axis)
    return lax.ppermute(shard, axis, [(i, (i + by) % size) for i in range(size)])


def padded_2(block, sides, width):
    for axis, dim in sides:
        count = lax.axis_size(axis)
        forward = [(i, i + 1) for i in range(count - 1)]
        forward.append((count - 1, 0))
        backward = [(target, source) for source, target in forward]
        low = lax.ppermute(
            lax.slice_in_dim(block, block.shape[dim] - width, None, axis=dim), axis, forward
        )
        high = lax.ppermute(lax.slice_in_dim(block, 0, width, axis=dim), axis, backward)
        block = jnp.concatenate([low, block, high], axis=dim)
    return block


def apply_ham(values, box_pot):
    padded = jnp.pad(values, ((0, 0), (1, 1), (1, 1), (1, 1)))
    beside = padded[:, 2:, 1:-1, 1:-1] + padded[:, :-2, 1:-1, 1:-1]
    beside = beside + padded[:, 1:-1, 2:, 1:-1] + padded[:, 1:-1, :-2, 1:-1]
    beside = beside + padded[:, 1:-1, 1:-1, 2:] + padded[:, 1:-1, 1:-1, :-2]
    return (3.0 + box_pot)[None] * values - 0.5 * beside


def near_cut(step, extent, band_width):
    if step == 0:
        return slice(0, extent)
    if step == 1:
        return slice(extent - band_width, extent)
    return slice(0, band_width)


def far_cut(step, extent, band_width):
    if step == 1:
        return slice(0, band_width)
    return slice(extent - band_width, extent)


def cross_dot(left, right):
    return lax.dot_general(
        left, right, (((1,), (1,)), ((), ())), preferred_element_type=jnp.float32
    )


def wide_move(values, amount):
    return shifted(values, "brick", amount)


def narrow_move(values, amount):
    return shifted(values, "narrow", amount)


def body(potential, functions, kernel_store, owners):
    own_funcs = functions[0, 0]
    func_count, ext_x, ext_y, z_depth = own_funcs.shape
    margin = (ext_x - potential.shape[0]) // 2
    band_width = 2 * margin
    n_brick = lax.axis_size("brick")
    n_narrow = lax.axis_size("narrow")
    device_count = n_brick * n_narrow
    box_pot = padded_2(potential, (("brick", 0), ("narrow", 1)), margin)
    applied = apply_ham(own_funcs.astype(jnp.float32), box_pot).astype(jnp.bfloat16)
    owner_col = owners[:, 0]
    atom_count = owner_col.shape[0]
    slot_count = kernel_store.shape[0]
    slot_cap = slot_count // device_count
    row_width = kernel_store.shape[1]
    atom_order = jnp.arange(atom_count, dtype=jnp.int32)
    earlier = (owner_col[:, None] == owner_col[None, :]) & (
        atom_order[None, :] < atom_order[:, None]
    )
    atom_rank = jnp.sum(earlier.astype(jnp.int32), axis=1)
    slot_of = owner_col * slot_cap + atom_rank
    kernel_in = lax.all_to_all(
        kernel_store, ("brick", "narrow"), split_axis=0, concat_axis=0, tiled=True
    )
    kernel_mat = jnp.take(kernel_in, slot_of, axis=0).reshape(func_count, 9, func_count)
    from_x = {
        1: wide_move(own_funcs[:, :band_width], -1),
        -1: wide_move(own_funcs[:, ext_x - band_width :], 1),
    }
    pieces = {(0, 0): own_funcs, (1, 0): from_x[1], (-1, 0): from_x[-1]}
    for step_y in (1, -1):
        cut_y = far_cut(step_y, ext_y, band_width)
        pieces[0, step_y] = narrow_move(own_funcs[:, :, cut_y], -step_y)
    for step_x in (1, -1):
        for step_y in (1, -1):
            cut_y = far_cut(step_y, ext_y, band_width)
            pieces[step_x, step_y] = shifted(from_x[step_x][:, :, cut_y], "narrow", -step_y)
    cell_volume = 1.0 / (ext_x * ext_y * z_depth)
    s_parts = []
    h_parts = []
    mixed = jnp.zeros(own_funcs.shape, jnp.float32)
    for position, (step_x, step_y) in enumerate(OFFSETS):
        cut_x = near_cut(step_x, ext_x, band_width)
        cut_y = near_cut(step_y, ext_y, band_width)
        far_piece = pieces[step_x, step_y]
        far_flat = far_piece.reshape(func_count, -1)
        near_flat = own_funcs[:, cut_x, cut_y].reshape(func_count, -1)
        applied_flat = applied[:, cut_x, cut_y].reshape(func_count, -1)
        s_parts.append(cross_dot(near_flat, far_flat) * cell_volume)
        h_parts.append(cross_dot(applied_flat, far_flat) * cell_volume)
        added = jnp.dot(kernel_mat[:, position], far_flat, preferred_element_type=jnp.float32)
        mixed = mixed.at[:, cut_x, cut_y].add(added.reshape(far_piece.shape))
    gradient = apply_ham(mixed, box_pot).astype(jnp.bfloat16)
    intersection_rows = jnp.stack(s_parts, axis=1).reshape(atom_count, row_width)
    ham_rows = jnp.stack(h_parts, axis=1).reshape(atom_count, row_width)
    pair_rows = jnp.stack([intersection_rows, ham_rows], axis=1)
    slot_index = jnp.arange(slot_count, dtype=jnp.int32)
    matches = slot_of[None, :] == slot_index[:, None]
    slot_used = jnp.any(matches, axis=1)
    slot_atom = jnp.sum(matches.astype(jnp.int32) * atom_order[None, :], axis=1)
    outgoing = jnp.where(slot_used[:, None, None], jnp.take(pair_rows, slot_atom, axis=0), 0.0)
    blocks = lax.all_to_all(outgoing, ("brick", "narrow"), split_axis=0, concat_axis=0, tiled=True)
    return (blocks, gradient[None, None])


def solution(mesh):
    in_specs = (
        P("brick", "narrow", None),
        P("brick", "narrow", None, None, None, None),
        P(("brick", "narrow"), None),
        P(("brick", "narrow"), None),
    )
    out_specs = (P(("brick", "narrow"), None, None), P("brick", "narrow", None, None, None, None))
    return jax.shard_map(body, mesh=mesh, in_specs=in_specs, out_specs=out_specs, check_vma=False)
```

profile of v0, /device:TPU:1, one launch (start us, length us, event | category | flops | bytes accessed | tf_op | source)
XLA Modules:
  0.0 169.4 jit_solution(17293976905414493529)
XLA Ops:
  0.6 2.7 %all_to_all.12 = bf16[128,2,1152]{2,1,0:T(2,128)(2,1)} reshape(bf16[256,1152]{1,0:T(8,128)(2,1)} %param.26) | data formatting | bytes 1179648 | tf_op jit(solution)/shard_map/all_to_all | solution.py:85
  3.3 11.9 %all-to-all-start.1 = ((bf16[128,2,1152]{2,1,0:T(2,128)(2,1)}), bf16[128,2,1152]{2,1,0:T(2,128)(2,1)}, u32[]{:S(2)}, u32[]{:S(2)}) async-start(bf16[128,2,1152]{2,1,0:T(2,128)(2,1)} %all_to_all.12), calls=%async_computation.1 | async-start | bytes 1179648 | tf_op jit(solution)/shard_map/all_to_all | solution.py:85
  15.3 2.0 %copy_bitcast_fusion = (bf16[64,8,8,128]{3,0,2,1:T(8,128)(2,1)S(1)}, f32[64,8,8,128]{3,0,2,1:T(8,128)}) fusion(bf16[1,1,64,8,8,128]{5,4,3,2,1,0:T(8,128)(2,1)S(1)} %copy-done.3), kind=kLoop, calls=%fused_computation.123 | loop fusion | flops 524288 | bytes 4194304 | tf_op jit(solution)/shard_map/reshape.395
  18.4 5.6 %collective-permute-start = (bf16[64,4,8,128]{3,0,2,1:T(8,128)(2,1)}, bf16[64,4,8,128]{3,0,2,1:T(8,128)(2,1)S(1)}, u32[]{:S(2)}, u32[]{:S(2)}) collective-permute-start(bf16[64,4,8,128]{3,0,2,1:T(8,128)(2,1)} %get-tuple-element.129), channel_id=1, source_target_pairs={{0,120},{8,0},{16,8},{24,16},{32,24},{40,32},{48,40},{56,48},{64,5... | collective-permute-start | bytes 1572872 | tf_op jit(solution)/shard_map/ppermute | solution.py:11
  26.8 1.8 %fusion.53 = f32[64,9,64]{2,0,1:T(8,128)} fusion(bf16[1,1,64,8,8,128]{5,4,3,2,1,0:T(8,128)(2,1)S(1)} %copy-done.3), kind=kOutput, calls=%fused_computation.94 | convolution fusion | flops 67112960 | bytes 1081344 | tf_op jit(solution)/shard_map/dot_general | solution.py:51
  31.4 9.0 %collective-permute-done.8 = f32[2,4,128]{2,1,0:T(4,128)S(1)} collective-permute-done((f32[2,4,128]{2,1,0:T(4,128)S(1)}, f32[2,4,128]{2,1,0:T(4,128)S(1)}, u32[]{:S(2)}, u32[]{:S(2)}) %collective-permute-start.8) | collective-permute-done | bytes 4128 | tf_op jit(solution)/shard_map/ppermute | solution.py:20
  40.4 2.4 %collective-permute-done.9 = f32[2,4,128]{2,1,0:T(4,128)S(1)} collective-permute-done((f32[2,4,128]{2,1,0:T(4,128)S(1)}, f32[2,4,128]{2,1,0:T(4,128)S(1)}, u32[]{:S(2)}, u32[]{:S(2)}) %collective-permute-start.9) | collective-permute-done | bytes 4128 | tf_op jit(solution)/shard_map/ppermute | solution.py:23
  42.9 3.8 %collective-permute-start.10 = (f32[8,2,128]{2,1,0:T(2,128)S(1)}, f32[8,2,128]{2,1,0:T(2,128)S(1)}, u32[]{:S(2)}, u32[]{:S(2)}) collective-permute-start(f32[8,2,128]{2,1,0:T(2,128)S(1)} %get-tuple-element.138), channel_id=1, source_target_pairs={{0,1},{1,2},{2,3},{3,4},{4,5},{5,6},{6,7},{7,0},{8,9},{9,10},{10,1... | collective-permute-start | bytes 24584 | tf_op jit(solution)/shard_map/ppermute | solution.py:20
  47.4 2.4 %collective-permute-start.11 = (f32[8,2,128]{2,1,0:T(2,128)S(1)}, f32[8,2,128]{2,1,0:T(2,128)S(1)}, u32[]{:S(2)}, u32[]{:S(2)}) collective-permute-start(f32[8,2,128]{2,1,0:T(2,128)S(1)} %get-tuple-element.139), channel_id=1, source_target_pairs={{1,0},{2,1},{3,2},{4,3},{5,4},{6,5},{7,6},{0,7},{9,8},{10,9},{11,1... | collective-permute-start | bytes 24584 | tf_op jit(solution)/shard_map/ppermute | solution.py:23
  56.6 1.4 copy.45
  59.6 1.4 copy.47
  63.5 1.7 %collective-permute-start.5 = (bf16[64,4,4,128]{3,0,2,1:T(8,128)(2,1)}, bf16[64,4,4,128]{3,0,2,1:T(8,128)(2,1)}, u32[]{:S(2)}, u32[]{:S(2)}) collective-permute-start(bf16[64,4,4,128]{3,0,2,1:T(8,128)(2,1)} %get-tuple-element.134), channel_id=1, source_target_pairs={{0,1},{1,2},{2,3},{3,4},{4,5},{5,6},{6,7},{7,0},{8,9},{9,10},{10,1... | collective-permute-start | bytes 786440 | tf_op jit(solution)/shard_map/ppermute | solution.py:11
  66.0 1.7 %collective-permute-start.7 = (bf16[64,4,4,128]{3,0,2,1:T(8,128)(2,1)}, bf16[64,4,4,128]{3,0,2,1:T(8,128)(2,1)}, u32[]{:S(2)}, u32[]{:S(2)}) collective-permute-start(bf16[64,4,4,128]{3,0,2,1:T(8,128)(2,1)} %get-tuple-element.132), channel_id=1, source_target_pairs={{0,1},{1,2},{2,3},{3,4},{4,5},{5,6},{6,7},{7,0},{8,9},{9,10},{10,1... | collective-permute-start | bytes 786440 | tf_op jit(solution)/shard_map/ppermute | solution.py:11
  69.9 2.2 %fusion.33 = f32[64,9,64]{2,0,1:T(8,128)} fusion(f32[64,9,64]{2,0,1:T(8,128)} %fusion.30, bf16[64,8,4,128]{3,0,2,1:T(8,128)(2,1)} %collective-permute-done.2, bf16[1,1,64,8,8,128]{5,4,3,2,1,0:T(8,128)(2,1)S(1)} %copy-done.3), kind=kOutput, calls=%fused_computation.64 | convolution fusion | flops 33558528 | bytes 1605632 | tf_op jit(solution)/shard_map/dot_general | solution.py:51
  72.0 2.2 %fusion.36 = f32[64,9,64]{2,0,1:T(8,128)} fusion(f32[64,9,64]{2,0,1:T(8,128)} %fusion.33, bf16[64,8,4,128]{3,0,2,1:T(8,128)(2,1)} %collective-permute-done.3, bf16[1,1,64,8,8,128]{5,4,3,2,1,0:T(8,128)(2,1)S(1)} %copy-done.3), kind=kOutput, calls=%fused_computation.67 | convolution fusion | flops 33558528 | bytes 1605632 | tf_op jit(solution)/shard_map/dot_general | solution.py:51
  74.2 2.2 %all_to_all.14 = bf16[256,1152]{1,0:T(8,128)(2,1)S(1)} reshape(bf16[128,2,1152]{2,1,0:T(2,128)(2,1)} %all-to-all-done.1) | data formatting | bytes 1179648 | tf_op jit(solution)/shard_map/all_to_all | solution.py:85
  77.3 2.2 %fusion.80 = f32[64,8,8,128]{3,0,2,1:T(8,128)S(1)} fusion(bf16[8,8,128,64]{2,1,0,3:T(8,128)(2,1)} %bitcast.416, bf16[64,9,64]{2,0,1:T(8,128)(2,1)S(1)} %copy_select_fusion), kind=kOutput, calls=%fused_computation.121 | convolution fusion | flops 67108864 | bytes 3162112 | tf_op jit(solution)/shard_map/dot_general | solution.py:114
  85.8 1.9 %copy.51 = bf16[64,4,4,128]{3,2,1,0:T(4,128)(2,1)} copy(bf16[64,4,4,128]{3,0,2,1:T(8,128)(2,1)} %collective-permute-done.5) | data formatting | bytes 524288 | tf_op jit(solution)/shard_map/ppermute | solution.py:11
  89.6 1.8 %copy.53 = bf16[64,4,4,128]{3,2,1,0:T(4,128)(2,1)} copy(bf16[64,4,4,128]{3,0,2,1:T(8,128)(2,1)} %collective-permute-done.6) | data formatting | bytes 524288 | tf_op jit(solution)/shard_map/ppermute | solution.py:11
  93.5 1.8 %copy.55 = bf16[64,4,4,128]{3,2,1,0:T(4,128)(2,1)} copy(bf16[64,4,4,128]{3,0,2,1:T(8,128)(2,1)} %collective-permute-done.7) | data formatting | bytes 524288 | tf_op jit(solution)/shard_map/ppermute | solution.py:11
  98.6 1.3 fusion.23
  100.0 2.0 %fusion.22 = f32[64,8,8,128]{3,0,2,1:T(8,128)S(1)} fusion(f32[64,8,8,128]{3,0,2,1:T(8,128)S(1)} %fusion.23, s32[]{:T(128)} %bitcast.87, s32[]{:T(128)} %bitcast.88, bf16[4,4,128,64]{2,1,0,3:T(4,128)(2,1)S(1)} %copy-done.12, pred[]{:T(512)} %and_reduce_fusion, bf16[64,9,64]{2,0,1:T(8,128)(2,1)S(1)} %copy_select_fusion), kind=kOutput, calls=%fused_computation.43 | convolution fusion | flops 17039360 | bytes 1327113 | tf_op jit(solution)/shard_map/dot_general | solution.py:114
  102.2 3.9 %fusion.82 = (bf16[1,1,64,8,8,128]{5,2,4,3,1,0:T(8,128)(2,1)}, bf16[64,8,8,128]{3,0,2,1:T(8,128)(2,1)S(1)}) fusion(f32[64,8,8,128]{3,0,2,1:T(8,128)S(1)} %fusion.20, f32[8,8,128]{2,1,0:T(8,128)S(1)} %copy-done.15, f32[64,8,8,128]{3,0,2,1:T(8,128)S(1)} %copy-done), kind=kLoop, calls=%fused_computation.124 | loop fusion | flops 9437184 | bytes 6324224 | tf_op jit(solution)/shard_map/broadcast_in_dim | solution.py:126
  108.8 1.3 fusion.45
  110.1 1.3 fusion.48
  112.9 1.3 fusion.74
  120.4 3.4 %gather_fusion = f32[256,2,1152]{2,1,0:T(2,128)S(1)} fusion(f32[32,2,1152]{2,1,0:T(2,128)S(1)} %pad_maximum_fusion, s32[1024]{0:T(1024)} %pad_clamp_fusion.1), kind=kCustom, calls=%fused_computation | custom fusion | bytes 4719616 | tf_op jit(solution)/shard_map/jit(_take)/gather | solution.py:124
  123.8 3.3 %select_select_fusion = f32[256,2,1152]{2,1,0:T(2,128)} fusion(f32[256,2,1152]{2,1,0:T(2,128)S(1)} %gather_fusion, pred[256]{0:T(512)(128)(4,1)S(1)} %copy-done.19, pred[256]{0:T(512)(128)(4,1)S(1)} %copy-done.18), kind=kLoop, calls=%fused_computation.14 | loop fusion | flops 1179648 | bytes 4719104 | tf_op jit(solution)/shard_map/jit(_where)/select_n | solution.py:124
  127.1 7.7 %all-to-all-start = ((f32[256,2,1152]{2,1,0:T(2,128)}), f32[256,2,1152]{2,1,0:T(2,128)S(1)}, u32[]{:S(2)}, u32[]{:S(2)}) async-start(f32[256,2,1152]{2,1,0:T(2,128)} %select_select_fusion), calls=%async_computation | async-start | bytes 4718592 | tf_op jit(solution)/shard_map/all_to_all | solution.py:125
  134.8 1.6 copy.57
  136.5 31.6 %all-to-all-done = f32[256,2,1152]{2,1,0:T(2,128)S(1)} async-done(((f32[256,2,1152]{2,1,0:T(2,128)}), f32[256,2,1152]{2,1,0:T(2,128)S(1)}, u32[]{:S(2)}, u32[]{:S(2)}) %all-to-all-start) | async-done | bytes 2359328 | tf_op jit(solution)/shard_map/all_to_all | solution.py:125
  168.0 1.4 copy.156
  (134 shorter events, 45.9 us)
Async XLA Ops:
  0.6 14.6 %copy-start.3 = (bf16[1,1,64,8,8,128]{5,4,3,2,1,0:T(8,128)(2,1)S(1)}, bf16[1,1,64,8,8,128]{5,4,3,2,1,0:T(8,128)(2,1)}, u32[]{:S(2)}) copy-start(bf16[1,1,64,8,8,128]{5,4,3,2,1,0:T(8,128)(2,1)} %param.25) | copy-start | bytes 3145732
  3.3 70.8 %all-to-all-start.1 = ((bf16[128,2,1152]{2,1,0:T(2,128)(2,1)}), bf16[128,2,1152]{2,1,0:T(2,128)(2,1)}, u32[]{:S(2)}, u32[]{:S(2)}) async-start(bf16[128,2,1152]{2,1,0:T(2,128)(2,1)} %all_to_all.12), calls=%async_computation.1 | async-start | bytes 1179648 | tf_op jit(solution)/shard_map/all_to_all | solution.py:85
  17.3 9.5 %copy-start.16 = (f32[4,4,128]{2,1,0:T(4,128)S(1)}, f32[4,4,128]{2,1,0:T(4,128)}, u32[]{:S(2)}) copy-start(f32[4,4,128]{2,1,0:T(4,128)} %param.24) | copy-start | bytes 24580
  18.4 10.3 %copy-start.20 = (s32[32,1]{0,1:T(1,128)S(1)}, s32[32,1]{0,1:T(1,128)}, u32[]{:S(2)}) copy-start(s32[32,1]{0,1:T(1,128)} %param.27) | copy-start | bytes 388
  18.4 11.7 %copy-start.21 = (s32[4]{0:T(128)S(1)}, s32[4]{0:T(128)}, u32[]{:S(2)}) copy-start(s32[4]{0:T(128)} %constant.300.clone.1) | copy-start | bytes 52
  18.4 35.3 %collective-permute-start = (bf16[64,4,8,128]{3,0,2,1:T(8,128)(2,1)}, bf16[64,4,8,128]{3,0,2,1:T(8,128)(2,1)S(1)}, u32[]{:S(2)}, u32[]{:S(2)}) collective-permute-start(bf16[64,4,8,128]{3,0,2,1:T(8,128)(2,1)} %get-tuple-element.129), channel_id=1, source_target_pairs={{0,120},{8,0},{16,8},{24,16},{32,24},{40,32},{48,40},{56,48},{64,5... | collective-permute-start | bytes 1572872 | tf_op jit(solution)/shard_map/ppermute | solution.py:11
  23.9 31.2 %collective-permute-start.1 = (bf16[64,4,8,128]{3,0,2,1:T(8,128)(2,1)}, bf16[64,4,8,128]{3,0,2,1:T(8,128)(2,1)S(1)}, u32[]{:S(2)}, u32[]{:S(2)}) collective-permute-start(bf16[64,4,8,128]{3,0,2,1:T(8,128)(2,1)} %get-tuple-element.128), channel_id=1, source_target_pairs={{0,8},{8,16},{16,24},{24,32},{32,40},{40,48},{48,56},{56,64},{64,7... | collective-permute-start | bytes 1572872 | tf_op jit(solution)/shard_map/ppermute | solution.py:11
  25.0 31.5 %collective-permute-start.2 = (bf16[64,8,4,128]{3,0,2,1:T(8,128)(2,1)}, bf16[64,8,4,128]{3,0,2,1:T(8,128)(2,1)}, u32[]{:S(2)}, u32[]{:S(2)}) collective-permute-start(bf16[64,8,4,128]{3,0,2,1:T(8,128)(2,1)} %get-tuple-element.127), channel_id=1, source_target_pairs={{0,7},{1,0},{2,1},{3,2},{4,3},{5,4},{6,5},{7,6},{8,15},{9,8},{10,9... | collective-permute-start | bytes 1572872 | tf_op jit(solution)/shard_map/ppermute | solution.py:11
  25.7 33.9 %collective-permute-start.3 = (bf16[64,8,4,128]{3,0,2,1:T(8,128)(2,1)}, bf16[64,8,4,128]{3,0,2,1:T(8,128)(2,1)}, u32[]{:S(2)}, u32[]{:S(2)}) collective-permute-start(bf16[64,8,4,128]{3,0,2,1:T(8,128)(2,1)} %get-tuple-element.126), channel_id=1, source_target_pairs={{0,1},{1,2},{2,3},{3,4},{4,5},{5,6},{6,7},{7,0},{8,9},{9,10},{10,1... | collective-permute-start | bytes 1572872 | tf_op jit(solution)/shard_map/ppermute | solution.py:11
  26.8 13.6 %collective-permute-start.8 = (f32[2,4,128]{2,1,0:T(4,128)S(1)}, f32[2,4,128]{2,1,0:T(4,128)S(1)}, u32[]{:S(2)}, u32[]{:S(2)}) collective-permute-start(f32[2,4,128]{2,1,0:T(4,128)S(1)} %get-tuple-element.141), channel_id=1, source_target_pairs={{0,8},{8,16},{16,24},{24,32},{32,40},{40,48},{48,56},{56,64},{64,7... | collective-permute-start | bytes 12296 | tf_op jit(solution)/shard_map/ppermute | solution.py:20
  40.4 2.5 %collective-permute-start.9 = (f32[2,4,128]{2,1,0:T(4,128)S(1)}, f32[2,4,128]{2,1,0:T(4,128)S(1)}, u32[]{:S(2)}, u32[]{:S(2)}) collective-permute-start(f32[2,4,128]{2,1,0:T(4,128)S(1)} %get-tuple-element.140), channel_id=1, source_target_pairs={{8,0},{16,8},{24,16},{32,24},{40,32},{48,40},{56,48},{64,56},{72,6... | collective-permute-start | bytes 12296 | tf_op jit(solution)/shard_map/ppermute | solution.py:23
  42.9 4.5 %collective-permute-start.10 = (f32[8,2,128]{2,1,0:T(2,128)S(1)}, f32[8,2,128]{2,1,0:T(2,128)S(1)}, u32[]{:S(2)}, u32[]{:S(2)}) collective-permute-start(f32[8,2,128]{2,1,0:T(2,128)S(1)} %get-tuple-element.138), channel_id=1, source_target_pairs={{0,1},{1,2},{2,3},{3,4},{4,5},{5,6},{6,7},{7,0},{8,9},{9,10},{10,1... | collective-permute-start | bytes 24584 | tf_op jit(solution)/shard_map/ppermute | solution.py:20
  47.4 5.6 %collective-permute-start.11 = (f32[8,2,128]{2,1,0:T(2,128)S(1)}, f32[8,2,128]{2,1,0:T(2,128)S(1)}, u32[]{:S(2)}, u32[]{:S(2)}) collective-permute-start(f32[8,2,128]{2,1,0:T(2,128)S(1)} %get-tuple-element.139), channel_id=1, source_target_pairs={{1,0},{2,1},{3,2},{4,3},{5,4},{6,5},{7,6},{0,7},{9,8},{10,9},{11,1... | collective-permute-start | bytes 24584 | tf_op jit(solution)/shard_map/ppermute | solution.py:23
  50.9 3.3 %copy-start.1 = (bf16[64,8192]{1,0:T(8,128)(2,1)}, bf16[64,8192]{1,0:T(8,128)(2,1)S(1)}, u32[]{:S(2)}) copy-start(bf16[64,8192]{1,0:T(8,128)(2,1)S(1)} %reshape_squeeze.4) | copy-start | bytes 3145732
  63.5 18.7 %collective-permute-start.4 = (bf16[64,4,4,128]{3,0,2,1:T(8,128)(2,1)}, bf16[64,4,4,128]{3,0,2,1:T(8,128)(2,1)S(1)}, u32[]{:S(2)}, u32[]{:S(2)}) collective-permute-start(bf16[64,4,4,128]{3,0,2,1:T(8,128)(2,1)} %get-tuple-element.135), channel_id=1, source_target_pairs={{0,7},{1,0},{2,1},{3,2},{4,3},{5,4},{6,5},{7,6},{8,15},{9,8},{10,9... | collective-permute-start | bytes 786440 | tf_op jit(solution)/shard_map/ppermute | solution.py:11
  63.5 22.3 %collective-permute-start.5 = (bf16[64,4,4,128]{3,0,2,1:T(8,128)(2,1)}, bf16[64,4,4,128]{3,0,2,1:T(8,128)(2,1)}, u32[]{:S(2)}, u32[]{:S(2)}) collective-permute-start(bf16[64,4,4,128]{3,0,2,1:T(8,128)(2,1)} %get-tuple-element.134), channel_id=1, source_target_pairs={{0,1},{1,2},{2,3},{3,4},{4,5},{5,6},{6,7},{7,0},{8,9},{9,10},{10,1... | collective-permute-start | bytes 786440 | tf_op jit(solution)/shard_map/ppermute | solution.py:11
  66.0 23.6 %collective-permute-start.6 = (bf16[64,4,4,128]{3,0,2,1:T(8,128)(2,1)}, bf16[64,4,4,128]{3,0,2,1:T(8,128)(2,1)}, u32[]{:S(2)}, u32[]{:S(2)}) collective-permute-start(bf16[64,4,4,128]{3,0,2,1:T(8,128)(2,1)} %get-tuple-element.133), channel_id=1, source_target_pairs={{0,7},{1,0},{2,1},{3,2},{4,3},{5,4},{6,5},{7,6},{8,15},{9,8},{10,9... | collective-permute-start | bytes 786440 | tf_op jit(solution)/shard_map/ppermute | solution.py:11
  66.0 27.4 %collective-permute-start.7 = (bf16[64,4,4,128]{3,0,2,1:T(8,128)(2,1)}, bf16[64,4,4,128]{3,0,2,1:T(8,128)(2,1)}, u32[]{:S(2)}, u32[]{:S(2)}) collective-permute-start(bf16[64,4,4,128]{3,0,2,1:T(8,128)(2,1)} %get-tuple-element.132), channel_id=1, source_target_pairs={{0,1},{1,2},{2,3},{3,4},{4,5},{5,6},{6,7},{7,0},{8,9},{9,10},{10,1... | collective-permute-start | bytes 786440 | tf_op jit(solution)/shard_map/ppermute | solution.py:11
  72.0 5.2 %copy-start.17 = (pred[64]{0:T(512)(128)(4,1)S(1)}, pred[64]{0:T(512)(128)(4,1)}, u32[]{:S(2)}) copy-start(pred[64]{0:T(512)(128)(4,1)} %broadcast_in_dim.53) | copy-start | bytes 196
  77.2 2.3 %copy-start.6 = (bf16[8,8,32,128]{3,2,1,0:T(8,128)(2,1)S(1)}, bf16[8,8,32,128]{3,2,1,0:T(8,128)(2,1)}, u32[]{:S(2)}) copy-start(bf16[8,8,32,128]{3,2,1,0:T(8,128)(2,1)} %copy.87) | copy-start | bytes 1572868
  79.5 1.5 copy-start.8
  97.3 2.6 %copy-start.12 = (bf16[4,4,128,64]{2,1,0,3:T(4,128)(2,1)S(1)}, bf16[4,4,128,64]{2,1,0,3:T(4,128)(2,1)}, u32[]{:S(2)}) copy-start(bf16[4,4,128,64]{2,1,0,3:T(4,128)(2,1)} %dot_general.157) | copy-start | bytes 786436
  97.3 4.6 %copy-start.13 = (bf16[4,4,128,64]{2,1,0,3:T(4,128)(2,1)S(1)}, bf16[4,4,128,64]{2,1,0,3:T(4,128)(2,1)}, u32[]{:S(2)}) copy-start(bf16[4,4,128,64]{2,1,0,3:T(4,128)(2,1)} %dot_general.160) | copy-start | bytes 786436
  98.6 3.6 %copy-start = (f32[64,8,8,128]{3,0,2,1:T(8,128)S(1)}, f32[64,8,8,128]{3,0,2,1:T(8,128)}, u32[]{:S(2)}) copy-start(f32[64,8,8,128]{3,0,2,1:T(8,128)} %get-tuple-element.131) | copy-start | bytes 6291460
  98.6 3.6 %copy-start.15 = (f32[8,8,128]{2,1,0:T(8,128)S(1)}, f32[8,8,128]{2,1,0:T(8,128)}, u32[]{:S(2)}) copy-start(f32[8,8,128]{2,1,0:T(8,128)} %maximum_add_fusion) | copy-start | bytes 98308
  108.5 3.0 %copy-start.11 = (bf16[64,4,4,128]{3,0,2,1:T(8,128)(2,1)S(1)}, bf16[64,4,4,128]{3,0,2,1:T(8,128)(2,1)}, u32[]{:S(2)}) copy-start(bf16[64,4,4,128]{3,0,2,1:T(8,128)(2,1)} %copy-done.10) | copy-start | bytes 786436
  112.9 2.9 %copy-start.4 = (bf16[1,1,64,8,8,128]{5,4,3,2,1,0:T(8,128)(2,1)S(1)}, bf16[1,1,64,8,8,128]{5,4,3,2,1,0:T(8,128)(2,1)}, u32[]{:S(2)}) copy-start(bf16[1,1,64,8,8,128]{5,4,3,2,1,0:T(8,128)(2,1)} %param.25) | copy-start | bytes 3145732
  112.9 2.9 %copy-start.14 = (f32[64,9,64]{2,0,1:T(8,128)S(1)}, f32[64,9,64]{2,0,1:T(8,128)}, u32[]{:S(2)}) copy-start(f32[64,9,64]{2,0,1:T(8,128)} %fusion.36) | copy-start | bytes 442372
  120.4 3.4 %copy-start.18 = (pred[256]{0:T(512)(128)(4,1)S(1)}, pred[256]{0:T(512)(128)(4,1)}, u32[]{:S(2)}) copy-start(pred[256]{0:T(512)(128)(4,1)} %fusion.91) | copy-start | bytes 772
  120.4 3.4 %copy-start.19 = (pred[256]{0:T(512)(128)(4,1)S(1)}, pred[256]{0:T(512)(128)(4,1)}, u32[]{:S(2)}) copy-start(pred[256]{0:T(512)(128)(4,1)} %compare_and_fusion) | copy-start | bytes 772
  127.1 7.7 %copy-start.5 = (bf16[1,1,64,8,8,128]{5,2,4,3,1,0:T(8,128)(2,1)S(1)}, bf16[1,1,64,8,8,128]{5,2,4,3,1,0:T(8,128)(2,1)}, u32[]{:S(2)}) copy-start(bf16[1,1,64,8,8,128]{5,2,4,3,1,0:T(8,128)(2,1)} %get-tuple-element.136) | copy-start | bytes 3145732
  127.1 40.9 %all-to-all-start = ((f32[256,2,1152]{2,1,0:T(2,128)}), f32[256,2,1152]{2,1,0:T(2,128)S(1)}, u32[]{:S(2)}, u32[]{:S(2)}) async-start(f32[256,2,1152]{2,1,0:T(2,128)} %select_select_fusion), calls=%async_computation | async-start | bytes 4718592 | tf_op jit(solution)/shard_map/all_to_all | solution.py:125
  (4 other events, 4.1 us)
where the time goes:
time: 171 us; the launch traced here: 169 us
  local copies, waits for them, and re-layouts  46 us (27%)
  waiting for transfers between devices  43.8 us (26%)
  starting transfers between devices  36.5 us (21%)
  matrix products  28.9 us (17%)
  other arithmetic  13 us (8%)
    all_to_all x1, waiting for transfers between devices, body(): lax.all_to_all(outgoing, ('brick', 'narrow'), split_axis=0, concat_axis=0...  31.6 us
    dot_general x18, matrix products, cross_dot(): lax.dot_general(left, right, (((1,), (1,)), ((), ())), preferred_element_...  20 us
    all_to_all x1, starting transfers between devices, body(): lax.all_to_all(kernel_store, ('brick', 'narrow'), split_axis=0, concat_ax...  11.9 us
    ppermute x8, starting transfers between devices, shifted(): lax.ppermute(shard, axis, [(i, (i + by) % size) for i in range(size)])  10.8 us
    ppermute x8, local copies, waits for them, and re-layouts, shifted(): lax.ppermute(shard, axis, [(i, (i + by) % size) for i in range(size)])  10 us
    ppermute x2, waiting for transfers between devices, padded_2(): lax.ppermute(lax.slice_in_dim(block, block.shape[dim] - width, None, axis...  9.77 us
    dot_general x9, matrix products, body(): jnp.dot(kernel_mat[:, position], far_flat, preferred_element_type=jnp.flo...  8.86 us
    unnamed x53, local copies, waits for them, and re-layouts  8.51 us
  transfers between devices with their start and end apart: 14, of which 4 were waited for; matrix products, arithmetic and copies ran while one was open for 28% of the time, Pallas kernels for 0%

commit v1 on v0

v1 whole, which is shorter than its diff:
```python
import functools

import jax
import jax.numpy as jnp
from jax import lax
from jax.experimental import pallas as pl
from jax.experimental.pallas import tpu as pltpu
from jax.sharding import PartitionSpec as P

AT_X = {1: 1, 0: 2}
AT_Y = {1: 3, 0: 4}
AT_XY = {(1, 1): 5, (1, 0): 6, (0, 1): 7, (0, 0): 8}
SIDES = ((0, 0), (0, 1), (1, 0), (1, 1))
HEADROOM = 14
VMEM = pl.BlockSpec(memory_space=pltpu.VMEM)
SMEM = pl.BlockSpec(memory_space=pltpu.SMEM)


def shifted(shard, axis, by):
    size = lax.axis_size(axis)
    return lax.ppermute(shard, axis, [(i, (i + by) % size) for i in range(size)])


def params(mib=48):
    return pltpu.CompilerParams(vmem_limit_bytes=mib << 20)


def split_kernel(half, f_ref, x0_ref, x1_ref, y0_ref, y1_ref):
    for x in range(2 * half):
        rows = jnp.swapaxes(f_ref[:, x], 0, 1)
        side_x, at = divmod(x, half)
        for side_y in (0, 1):
            part = rows[side_y * half : (side_y + 1) * half]
            (x0_ref, x1_ref)[side_x][side_y, at] = part
            (y0_ref, y1_ref)[side_y][side_x, at] = part


def pair_kernel(k_ref, o_ref):
    o_ref[...] = k_ref[...].reshape(o_ref.shape)


def stencil(cell, potential_row, half, x, y, zero_low, zero_high):
    value = cell(x, y)
    beside = jnp.where(zero_high, 0.0, pltpu.roll(value, value.shape[1] - 1, 1)) + jnp.where(
        zero_low, 0.0, pltpu.roll(value, 1, 1)
    )
    for near_x, near_y in ((x + 1, y), (x - 1, y), (x, y + 1), (x, y - 1)):
        if 0 <= near_x < 2 * half and 0 <= near_y < 2 * half:
            beside = beside + cell(near_x, near_y)
    return (3.0 + potential_row(x, y)) * value - 0.5 * beside


def potential_rows(low_ref, mid_ref, high_ref):
    margin = low_ref.shape[1]
    inner = mid_ref.shape[1]

    def row(x, y):
        if y < margin:
            return low_ref[x, y : y + 1]
        if y < margin + inner:
            return mid_ref[x, y - margin : y - margin + 1]
        return high_ref[x, y - margin - inner : y - margin - inner + 1]

    return row


def edges(func_count, depth):
    lane = lax.broadcasted_iota(jnp.int32, (func_count, depth), 1)
    return lane == 0, lane == depth - 1


def ranks(owner_ref, count_ref):
    def clear(i, carry):
        count_ref[owner_ref[i]] = 0
        return carry

    lax.fori_loop(0, owner_ref.shape[0], clear, 0)
    found = []
    for a in range(owner_ref.shape[0]):
        owner = owner_ref[a]
        rank = count_ref[owner]
        count_ref[owner] = rank + 1
        found.append((owner, rank))
    return found


def pairs_kernel(half, cap, owner_ref, *refs):
    own, from_x, from_y, from_xy = refs[0:2], refs[2:4], refs[4:6], refs[6:10]
    row_of = potential_rows(*refs[10:13])
    out_ref, sums_ref, count_ref = refs[13:16]
    func_count, depth = own[0].shape[-2:]
    atoms = owner_ref.shape[0]
    low_edge, high_edge = edges(func_count, depth)

    def cell(x, y):
        side_x, at_x = divmod(x, half)
        side_y, at_y = divmod(y, half)
        return own[side_x][side_y, at_x, at_y].astype(jnp.float32)

    out_ref[...] = jnp.zeros(out_ref.shape, out_ref.dtype)
    block = {}
    for number, (side_x, side_y) in enumerate(SIDES):
        total = jnp.zeros((2 * func_count, 4 * func_count), jnp.float32)
        for at_x in range(half):
            left, right = [], []
            for at_y in range(half):
                near = own[side_x][side_y, at_x, at_y]
                applied = stencil(
                    cell, row_of, half, side_x * half + at_x, side_y * half + at_y, low_edge, high_edge
                ).astype(jnp.bfloat16)
                left.append(jnp.concatenate([near, applied], axis=0))
                right.append(
                    jnp.concatenate(
                        [
                            near,
                            from_x[side_x][side_y, at_x, at_y],
                            from_y[side_y][side_x, at_x, at_y],
                            from_xy[number][at_x, at_y],
                        ],
                        axis=0,
                    )
                )
            total = total + lax.dot_general(
                jnp.concatenate(left, axis=1),
                jnp.concatenate(right, axis=1),
                (((1,), (1,)), ((), ())),
                preferred_element_type=jnp.float32,
            )
        block[side_x, side_y] = total

    def columns(part, *sides):
        return functools.reduce(
            jnp.add, [block[s][:, part * func_count : (part + 1) * func_count] for s in sides]
        )

    parts = [columns(0, *SIDES)] + [None] * 8
    for side in (0, 1):
        parts[AT_X[side]] = columns(1, (side, 0), (side, 1))
        parts[AT_Y[side]] = columns(2, (0, side), (1, side))
    for sides in SIDES:
        parts[AT_XY[sides]] = columns(3, sides)
    width = 9 * func_count
    volume = 1.0 / (4 * half * half * depth)
    sums = jnp.concatenate(parts, axis=1) * volume
    for t in range(0, width, depth):
        sums_ref[t // depth, :, : min(depth, width - t)] = sums[:, t : t + depth]

    def atom_rows(start):
        picked = []
        for i in (0, 1):
            tiles = [sums_ref[t, pl.ds(start + i, atoms, stride=2), :] for t in range(sums_ref.shape[0])]
            picked.append(jnp.concatenate(tiles, axis=1)[:, :width])
        return jnp.concatenate(picked, axis=1)

    rows = [atom_rows(0), atom_rows(func_count)]
    largest = jnp.maximum(
        jnp.max(jnp.abs(rows[0]), axis=1, keepdims=True), jnp.max(jnp.abs(rows[1]), axis=1, keepdims=True)
    )
    power = jnp.ceil(jnp.log2(jnp.maximum(largest, 1e-33))) - HEADROOM
    scale = jnp.exp2(-power)
    tail = jnp.broadcast_to(power, (atoms, depth))
    rows = [jnp.concatenate([r * scale, tail], axis=1) for r in rows]
    for a, (owner, rank) in enumerate(ranks(owner_ref, count_ref)):
        slot = owner * cap + rank
        out_ref[slot, 0:1, :] = rows[0][a : a + 1]
        out_ref[slot, 1:2, :] = rows[1][a : a + 1]


def mix_kernel(half, owner_ref, kernel_ref, *refs):
    own, from_x, from_y, from_xy = refs[0:2], refs[2:4], refs[4:6], refs[6:10]
    row_of = potential_rows(*refs[10:13])
    out_ref, rows_ref, mixed_ref, count_ref = refs[13:17]
    func_count, depth = own[0].shape[-2:]
    atoms = owner_ref.shape[0]
    low_edge, high_edge = edges(func_count, depth)
    for a, (owner, rank) in enumerate(ranks(owner_ref, count_ref)):
        both = kernel_ref[owner].astype(jnp.float32)
        rows_ref[a : a + 1, :] = jnp.where(rank == 0, both[0:1], both[1:2])
    width = 9 * func_count
    matrix = jnp.concatenate([rows_ref[:, :width], rows_ref[:, width:]], axis=0)
    for number, (side_x, side_y) in enumerate(SIDES):
        at = (0, AT_X[side_x], AT_Y[side_y], AT_XY[side_x, side_y])
        left = jnp.concatenate(
            [matrix[:, k * func_count : (k + 1) * func_count] for k in at], axis=1
        ).astype(jnp.bfloat16)
        for at_x in range(half):
            for at_y in range(0, half, 2):
                right = jnp.concatenate(
                    [
                        jnp.concatenate(
                            [
                                own[side_x][side_y, at_x, y],
                                from_x[side_x][side_y, at_x, y],
                                from_y[side_y][side_x, at_x, y],
                                from_xy[number][at_x, y],
                            ],
                            axis=0,
                        )
                        for y in (at_y, at_y + 1)
                    ],
                    axis=1,
                )
                got = jnp.dot(left, right, preferred_element_type=jnp.float32)
                for i in (0, 1):
                    mixed_ref[side_x * half + at_x, side_y * half + at_y + i] = got[
                        :, i * depth : (i + 1) * depth
                    ]

    def cell(x, y):
        return mixed_ref[x, y]

    for x in range(2 * half):
        made = [
            stencil(cell, row_of, half, x, y, low_edge, high_edge) for y in range(2 * half)
        ]
        for odd in (0, 1):
            stacked = jnp.stack([m[odd * atoms : (odd + 1) * atoms] for m in made], axis=0)
            out_ref[:, odd, x] = jnp.swapaxes(stacked, 0, 1).astype(out_ref.dtype)


def body(potential, functions, kernel_store, owners):
    own_funcs = functions[0, 0]
    func_count, ext_x, ext_y, depth = own_funcs.shape
    half = ext_x // 2
    margin = (ext_x - potential.shape[0]) // 2
    device_count = lax.axis_size("brick") * lax.axis_size("narrow")
    owner_col = owners[:, 0]
    atoms = owner_col.shape[0]
    slot_count, row_width = kernel_store.shape
    slot_cap = slot_count // device_count
    bf16 = jnp.bfloat16
    struct = jax.ShapeDtypeStruct

    band = struct((2, half, half, func_count, depth), bf16)
    own_x0, own_x1, own_y0, own_y1 = pl.pallas_call(
        functools.partial(split_kernel, half),
        out_shape=(band,) * 4,
        in_specs=[VMEM],
        out_specs=(VMEM,) * 4,
        compiler_params=params(),
        cost_estimate=pl.CostEstimate(flops=0, transcendentals=0, bytes_accessed=3 << 20),
    )(own_funcs)

    from_x = (shifted(own_x1, "brick", 1), shifted(own_x0, "brick", -1))
    from_y = (shifted(own_y1, "narrow", 1), shifted(own_y0, "narrow", -1))
    from_xy = [shifted(from_x[sx][1 - sy], "narrow", -1 if sy else 1) for sx, sy in SIDES]

    low = shifted(potential[-margin:], "brick", 1)
    high = shifted(potential[:margin], "brick", -1)
    middle = jnp.concatenate([low, potential, high], axis=0)
    low = shifted(middle[:, -margin:], "narrow", 1)
    high = shifted(middle[:, :margin], "narrow", -1)
    pots = (low, middle, high)

    kernel_out = pl.pallas_call(
        pair_kernel,
        out_shape=struct((device_count, slot_cap, row_width), bf16),
        in_specs=[VMEM],
        out_specs=VMEM,
        compiler_params=params(),
        cost_estimate=pl.CostEstimate(flops=0, transcendentals=0, bytes_accessed=1 << 20),
    )(kernel_store)
    kernel_in = lax.all_to_all(
        kernel_out, ("brick", "narrow"), split_axis=0, concat_axis=0, tiled=True
    )

    boxes = (own_x0, own_x1, *from_x, *from_y, *from_xy)
    cells = ext_x * ext_y * depth
    outgoing = pl.pallas_call(
        functools.partial(pairs_kernel, half, slot_cap),
        out_shape=struct((slot_count, 2, row_width + depth), jnp.float32),
        in_specs=[SMEM] + [VMEM] * 13,
        out_specs=VMEM,
        scratch_shapes=[
            pltpu.VMEM((pl.cdiv(9 * func_count, depth), 2 * func_count, depth), jnp.float32),
            pltpu.SMEM((device_count,), jnp.int32),
        ],
        compiler_params=params(),
        cost_estimate=pl.CostEstimate(
            flops=16 * func_count * func_count * cells, transcendentals=0, bytes_accessed=7 << 20
        ),
    )(owner_col, *boxes, *pots)
    blocks = lax.all_to_all(
        outgoing.astype(jnp.float16), ("brick", "narrow"), split_axis=0, concat_axis=0, tiled=True
    )
    power = blocks[:, :, row_width : row_width + 1].astype(jnp.float32)
    blocks = blocks[:, :, :row_width].astype(jnp.float32) * jnp.exp2(power)

    gradient = pl.pallas_call(
        functools.partial(mix_kernel, half),
        out_shape=struct((atoms, 2, ext_x, ext_y, depth), bf16),
        in_specs=[SMEM] + [VMEM] * 14,
        out_specs=VMEM,
        scratch_shapes=[
            pltpu.VMEM((atoms, row_width), jnp.float32),
            pltpu.VMEM((ext_x, ext_y, func_count, depth), jnp.float32),
            pltpu.SMEM((device_count,), jnp.int32),
        ],
        compiler_params=params(),
        cost_estimate=pl.CostEstimate(
            flops=8 * func_count * func_count * cells, transcendentals=0, bytes_accessed=7 << 20
        ),
    )(owner_col, kernel_in, *boxes, *pots)
    return (blocks, gradient.reshape(functions.shape))


def solution(mesh):
    in_specs = (
        P("brick", "narrow", None),
        P("brick", "narrow", None, None, None, None),
        P(("brick", "narrow"), None),
        P(("brick", "narrow"), None),
    )
    out_specs = (P(("brick", "narrow"), None, None), P("brick", "narrow", None, None, None, None))
    return jax.shard_map(body, mesh=mesh, in_specs=in_specs, out_specs=out_specs, check_vma=False)
```

time: 171 us -> 93.5 us (0.55)
  local copies, waits for them, and re-layouts: 46 us -> 6.14 us
  matrix products: 28.9 us -> 0 us
  waiting for transfers between devices: 43.8 us -> 31.5 us
  Pallas kernels: 0 us -> 9.4 us
  other arithmetic: 13 us -> 8.38 us
    dot_general x27 -> x0, matrix products: 28.9 us -> none  [the longest x18 20 us: cross_dot(): lax.dot_general(left, right, (((1,), (1,)), ((), ())), preferred_element_...]
    all_to_all x2, waiting for transfers between devices: 31.6 us -> 14.3 us  [the longest x1 14.3 us: body(): lax.all_to_all(outgoing.astype(jnp.float16), ('brick', 'narrow'), split_a...]
    ppermute x8 -> x12, waiting for transfers between devices: 0.02 us -> 17.1 us  [shifted(): lax.ppermute(shard, axis, [(i, (i + by) % size) for i in range(size)])]
    ppermute x4 -> x0, waiting for transfers between devices: 12.2 us -> none  [the longest x2 9.77 us: padded_2(): lax.ppermute(lax.slice_in_dim(block, block.shape[dim] - width, None, axis...]
    ppermute x8 -> x12, starting transfers between devices: 10.8 us -> 22.7 us  [shifted(): lax.ppermute(shard, axis, [(i, (i + by) % size) for i in range(size)])]
    ppermute x8 -> x0, local copies, waits for them, and re-layouts: 10 us -> none  [shifted(): lax.ppermute(shard, axis, [(i, (i + by) % size) for i in range(size)])]
    pallas_call x0 -> x4, Pallas kernels: none -> 9.4 us  [the longest x1 4.37 us: body(): pl.pallas_call(functools.partial(pairs_kernel, half, slot_cap), out_shape...]
    ppermute x4 -> x0, starting transfers between devices: 6.17 us -> none  [the longest x2 3.75 us: padded_2(): lax.ppermute(lax.slice_in_dim(block, block.shape[dim] - width, None, axis...]
  transfers between devices with their start and end apart: 14 -> 14, of which waited for: 4 -> 5; matrix products, arithmetic and copies ran while one was open for 28% -> 4% of each run, Pallas kernels for 0% -> 10%
where the time goes in v1:
time: 93.5 us; the launch traced here: 92.9 us
  starting transfers between devices  36.8 us (39%)
  waiting for transfers between devices  31.5 us (34%)
  Pallas kernels  9.4 us (10%)
  other arithmetic  8.38 us (9%)
  local copies, waits for them, and re-layouts  6.14 us (7%)
    ppermute x12, starting transfers between devices, shifted(): lax.ppermute(shard, axis, [(i, (i + by) % size) for i in range(size)])  22.7 us
    ppermute x12, waiting for transfers between devices, shifted(): lax.ppermute(shard, axis, [(i, (i + by) % size) for i in range(size)])  17.1 us
    all_to_all x1, waiting for transfers between devices, body(): lax.all_to_all(outgoing.astype(jnp.float16), ('brick', 'narrow'), split_a...  14.3 us
    all_to_all x1, starting transfers between devices, body(): lax.all_to_all(outgoing.astype(jnp.float16), ('brick', 'narrow'), split_a...  7.59 us
    all_to_all x1, starting transfers between devices, body(): lax.all_to_all(kernel_out, ('brick', 'narrow'), split_axis=0, concat_axis...  6.48 us
    unnamed x26, local copies, waits for them, and re-layouts  4.98 us
    pallas_call x1, Pallas kernels, body(): pl.pallas_call(functools.partial(pairs_kernel, half, slot_cap), out_shape...  4.37 us
    convert_element_type x1, other arithmetic, body(): outgoing.astype(jnp.float16)  3.7 us
  transfers between devices with their start and end apart: 14, of which 5 were waited for; matrix products, arithmetic and copies ran while one was open for 4% of the time, Pallas kernels for 10%

profile of v1, /device:TPU:1, one launch (start us, length us, event | category | flops | bytes accessed | tf_op | source)
XLA Modules:
  0.0 92.9 jit_solution(1202128052029343946)
XLA Ops:
  0.6 0.8 fusion.1
  1.4 2.1 %collective-permute-start.8 = (f32[2,4,128]{2,1,0:T(4,128)S(1)}, f32[2,4,128]{2,1,0:T(4,128)S(1)}, u32[]{:S(2)}, u32[]{:S(2)}) collective-permute-start(f32[2,4,128]{2,1,0:T(4,128)S(1)} %get-tuple-element.17), channel_id=1, source_target_pairs={{0,8},{8,16},{16,24},{24,32},{32,40},{40,48},{48,56},{56,64},{64,7... | collective-permute-start | bytes 12296 | tf_op jit(solution)/shard_map/ppermute | solution.py:21
  3.6 4.9 %collective-permute-start.9 = (f32[2,4,128]{2,1,0:T(4,128)S(1)}, f32[2,4,128]{2,1,0:T(4,128)S(1)}, u32[]{:S(2)}, u32[]{:S(2)}) collective-permute-start(f32[2,4,128]{2,1,0:T(4,128)S(1)} %get-tuple-element.16), channel_id=1, source_target_pairs={{0,120},{8,0},{16,8},{24,16},{32,24},{40,32},{48,40},{56,48},{64,5... | collective-permute-start | bytes 12296 | tf_op jit(solution)/shard_map/ppermute | solution.py:21
  8.5 1.1 %copy-done.9 = bf16[256,1152]{1,0:T(8,128)(2,1)S(1)} copy-done((bf16[256,1152]{1,0:T(8,128)(2,1)S(1)}, bf16[256,1152]{1,0:T(8,128)(2,1)}, u32[]{:S(2)}) %copy-start.9) | copy-done | bytes 589848
  9.5 0.9 shard_map.61
  10.5 6.5 %all-to-all-start.1 = ((bf16[128,2,1152]{2,1,0:T(2,128)(2,1)}), bf16[128,2,1152]{2,1,0:T(2,128)(2,1)S(1)}, u32[]{:S(2)}, u32[]{:S(2)}) async-start(bf16[128,2,1152]{2,1,0:T(2,128)(2,1)} %shard_map.61), calls=%async_computation.1 | async-start | bytes 1179648 | tf_op jit(solution)/shard_map/all_to_all | solution.py:263
  17.0 0.5 shard_map.59
  17.4 1.6 %collective-permute-start.2 = (bf16[2,4,4,64,128]{4,3,2,1,0:T(8,128)(2,1)S(1)}, bf16[2,4,4,64,128]{4,3,2,1,0:T(8,128)(2,1)S(1)}, u32[]{:S(2)}, u32[]{:S(2)}) collective-permute-start(bf16[2,4,4,64,128]{4,3,2,1,0:T(8,128)(2,1)S(1)} %get-tuple-element.8), channel_id=1, source_target_pairs={{0,1},{1,2},{2,3},{3,4},{4,5},{5,6},{6,7},{7,0},{8,9},{9,10},{10,1... | collective-permute-start | bytes 1572872 | tf_op jit(solution)/shard_map/ppermute | solution.py:21
  19.1 0.0 collective-permute-start.3
  19.1 5.4 %collective-permute-start.1 = (bf16[2,4,4,64,128]{4,3,2,1,0:T(8,128)(2,1)S(1)}, bf16[2,4,4,64,128]{4,3,2,1,0:T(8,128)(2,1)S(1)}, u32[]{:S(2)}, u32[]{:S(2)}) collective-permute-start(bf16[2,4,4,64,128]{4,3,2,1,0:T(8,128)(2,1)S(1)} %get-tuple-element.6.refs_0_), channel_id=1, source_target_pairs={{0,120},{8,0},{16,8},{24,16},{32,24},{40,32},{48,40},{56,48},{64,5... | collective-permute-start | bytes 1572872 | tf_op jit(solution)/shard_map/ppermute | solution.py:21
  24.5 2.2 %collective-permute-start.11 = (f32[8,2,128]{2,1,0:T(2,128)S(1)}, f32[8,2,128]{2,1,0:T(2,128)S(1)}, u32[]{:S(2)}, u32[]{:S(2)}) collective-permute-start(f32[8,2,128]{2,1,0:T(2,128)S(1)} %get-tuple-element.14), channel_id=1, source_target_pairs={{0,7},{1,0},{2,1},{3,2},{4,3},{5,4},{6,5},{7,6},{8,15},{9,8},{10,9... | collective-permute-start | bytes 24584 | tf_op jit(solution)/shard_map/ppermute | solution.py:21
  26.7 9.6 %collective-permute-done.1.refs_3_ = bf16[2,4,4,64,128]{4,3,2,1,0:T(8,128)(2,1)S(1)} collective-permute-done((bf16[2,4,4,64,128]{4,3,2,1,0:T(8,128)(2,1)S(1)}, bf16[2,4,4,64,128]{4,3,2,1,0:T(8,128)(2,1)S(1)}, u32[]{:S(2)}, u32[]{:S(2)}) %collective-permute-start.1) | collective-permute-done | bytes 524320 | tf_op jit(solution)/shard_map/ppermute | solution.py:21
  36.2 1.7 %collective-permute-start.10 = (f32[8,2,128]{2,1,0:T(2,128)S(1)}, f32[8,2,128]{2,1,0:T(2,128)S(1)}, u32[]{:S(2)}, u32[]{:S(2)}) collective-permute-start(f32[8,2,128]{2,1,0:T(2,128)S(1)} %get-tuple-element.15), channel_id=1, source_target_pairs={{0,1},{1,2},{2,3},{3,4},{4,5},{5,6},{6,7},{7,0},{8,9},{9,10},{10,1... | collective-permute-start | bytes 24584 | tf_op jit(solution)/shard_map/ppermute | solution.py:21
  38.0 2.2 %collective-permute-done.refs_2_ = bf16[2,4,4,64,128]{4,3,2,1,0:T(8,128)(2,1)S(1)} collective-permute-done((bf16[2,4,4,64,128]{4,3,2,1,0:T(8,128)(2,1)S(1)}, bf16[2,4,4,64,128]{4,3,2,1,0:T(8,128)(2,1)S(1)}, u32[]{:S(2)}, u32[]{:S(2)}) %collective-permute-start) | collective-permute-done | bytes 524320 | tf_op jit(solution)/shard_map/ppermute | solution.py:21
  40.2 2.5 %collective-permute-start.7 = (bf16[4,4,64,128]{3,2,1,0:T(8,128)(2,1)S(1)}, bf16[4,4,64,128]{3,2,1,0:T(8,128)(2,1)S(1)}, u32[]{:S(2)}, u32[]{:S(2)}) collective-permute-start(bf16[4,4,64,128]{3,2,1,0:T(8,128)(2,1)S(1)} %get-tuple-element.10), channel_id=1, source_target_pairs={{0,7},{1,0},{2,1},{3,2},{4,3},{5,4},{6,5},{7,6},{8,15},{9,8},{10,9... | collective-permute-start | bytes 786440 | tf_op jit(solution)/shard_map/ppermute | solution.py:21
  42.8 0.5 collective-permute-start.6
  43.3 1.7 %collective-permute-start.4 = (bf16[4,4,64,128]{3,2,1,0:T(8,128)(2,1)S(1)}, bf16[4,4,64,128]{3,2,1,0:T(8,128)(2,1)S(1)}, u32[]{:S(2)}, u32[]{:S(2)}) collective-permute-start(bf16[4,4,64,128]{3,2,1,0:T(8,128)(2,1)S(1)} %get-tuple-element.13), channel_id=1, source_target_pairs={{0,1},{1,2},{2,3},{3,4},{4,5},{5,6},{6,7},{7,0},{8,9},{9,10},{10,1... | collective-permute-start | bytes 786440 | tf_op jit(solution)/shard_map/ppermute | solution.py:21
  45.1 2.5 %collective-permute-done.7.refs_9_ = bf16[4,4,64,128]{3,2,1,0:T(8,128)(2,1)S(1)} collective-permute-done((bf16[4,4,64,128]{3,2,1,0:T(8,128)(2,1)S(1)}, bf16[4,4,64,128]{3,2,1,0:T(8,128)(2,1)S(1)}, u32[]{:S(2)}, u32[]{:S(2)}) %collective-permute-start.7) | collective-permute-done | bytes 262176 | tf_op jit(solution)/shard_map/ppermute | solution.py:21
  47.6 2.8 %collective-permute-done.5.refs_7_ = bf16[4,4,64,128]{3,2,1,0:T(8,128)(2,1)S(1)} collective-permute-done((bf16[4,4,64,128]{3,2,1,0:T(8,128)(2,1)S(1)}, bf16[4,4,64,128]{3,2,1,0:T(8,128)(2,1)S(1)}, u32[]{:S(2)}, u32[]{:S(2)}) %collective-permute-start.5) | collective-permute-done | bytes 262176 | tf_op jit(solution)/shard_map/ppermute | solution.py:21
  50.4 4.4 %shard_map.60 = f32[256,2,1280]{2,1,0:T(2,128)} custom-call(s32[32]{0:T(128)S(1)} %bitcast.13, bf16[2,4,4,64,128]{4,3,2,1,0:T(8,128)(2,1)S(1)} %get-tuple-element.6.refs_0_, bf16[2,4,4,64,128]{4,3,2,1,0:T(8,128)(2,1)S(1)} %get-tuple-element.7.refs_1_, bf16[2,4,4,64,128]{4,3,2,1,0:T(8,128)(2,1)S(1)} %collective-permute-done.refs_2_, ...), custom_call_target="tpu_custom_call" | custom-call | flops 536870912 | bytes 7340032 | tf_op jit(solution)/shard_map/pallas_call | solution.py:269
  54.8 3.7 %convert_element_type.9 = f16[256,2,1280]{2,1,0:T(2,128)(2,1)} convert(f32[256,2,1280]{2,1,0:T(2,128)} %shard_map.60) | non-fusion elementwise | flops 655360 | bytes 3932160 | tf_op jit(solution)/shard_map/convert_element_type | solution.py:284
  58.5 7.6 %all-to-all-start = ((f16[256,2,1280]{2,1,0:T(2,128)(2,1)}), f16[256,2,1280]{2,1,0:T(2,128)(2,1)}, u32[]{:S(2)}, u32[]{:S(2)}) async-start(f16[256,2,1280]{2,1,0:T(2,128)(2,1)} %convert_element_type.9), calls=%async_computation | async-start | bytes 2621440 | tf_op jit(solution)/shard_map/all_to_all | solution.py:283
  66.1 1.0 %copy-done.1 = bf16[2,4,4,64,128]{4,3,2,1,0:T(8,128)(2,1)S(1)} copy-done((bf16[2,4,4,64,128]{4,3,2,1,0:T(8,128)(2,1)S(1)}, bf16[2,4,4,64,128]{4,3,2,1,0:T(8,128)(2,1)}, u32[]{:S(2)}) %copy-start.1) | copy-done | bytes 524312
  67.2 0.9 %copy-done.3 = bf16[4,4,64,128]{3,2,1,0:T(8,128)(2,1)S(1)} copy-done((bf16[4,4,64,128]{3,2,1,0:T(8,128)(2,1)S(1)}, bf16[4,4,64,128]{3,2,1,0:T(8,128)(2,1)}, u32[]{:S(2)}) %copy-start.3) | copy-done | bytes 262168
  68.1 0.9 %copy-done.5 = bf16[4,4,64,128]{3,2,1,0:T(8,128)(2,1)S(1)} copy-done((bf16[4,4,64,128]{3,2,1,0:T(8,128)(2,1)S(1)}, bf16[4,4,64,128]{3,2,1,0:T(8,128)(2,1)}, u32[]{:S(2)}) %copy-start.5) | copy-done | bytes 262168
  69.1 0.9 %copy-done.7 = bf16[4,4,64,128]{3,2,1,0:T(8,128)(2,1)S(1)} copy-done((bf16[4,4,64,128]{3,2,1,0:T(8,128)(2,1)S(1)}, bf16[4,4,64,128]{3,2,1,0:T(8,128)(2,1)}, u32[]{:S(2)}) %copy-start.7) | copy-done | bytes 262168
  70.0 3.7 %shard_map.62 = bf16[32,2,8,8,128]{4,3,2,1,0:T(8,128)(2,1)} custom-call(s32[32]{0:T(128)S(1)} %bitcast.14, bf16[128,2,1152]{2,1,0:T(2,128)(2,1)S(1)} %all-to-all-done.1.kernel_ref, bf16[2,4,4,64,128]{4,3,2,1,0:T(8,128)(2,1)S(1)} %get-tuple-element.6.refs_0_, bf16[2,4,4,64,128]{4,3,2,1,0:T(8,128)(2,1)S(1)} %get-tuple-element.7.refs_1_, ...), custom_call_target="tpu_custom_call" | custom-call | flops 268435456 | bytes 7340032 | tf_op jit(solution)/shard_map/pallas_call | solution.py:289
  73.7 14.3 %all-to-all-done = f16[256,2,1280]{2,1,0:T(2,128)(2,1)} async-done(((f16[256,2,1280]{2,1,0:T(2,128)(2,1)}), f16[256,2,1280]{2,1,0:T(2,128)(2,1)}, u32[]{:S(2)}, u32[]{:S(2)}) %all-to-all-start) | async-done | bytes 1310752 | tf_op jit(solution)/shard_map/all_to_all | solution.py:283
  88.0 1.1 %multiply_exponential_fusion = f32[256,2,1]{2,1,0:T(2,128)S(1)} fusion(f16[256,2,1280]{2,1,0:T(2,128)(2,1)} %all-to-all-done), kind=kLoop, calls=%fused_computation.5 | loop fusion | flops 1024 | bytes 3072 | tf_op jit(solution)/shard_map/exp2 | solution.py:287
  89.1 0.1 copy.8
  89.2 0.1 copy.9
  89.3 3.6 %convert_multiply_fusion = f32[256,2,1152]{2,1,0:T(2,128)} fusion(f16[256,2,1280]{2,1,0:T(2,128)(2,1)} %all-to-all-done, f32[256,2]{1,0:T(8,128)S(1)} %copy.9), kind=kLoop, calls=%fused_computation | loop fusion | flops 1179648 | bytes 3540992 | tf_op jit(solution)/shard_map/mul | solution.py:287
  (36 shorter events, 0.2 us)
Async XLA Ops:
  0.6 16.3 %copy-start.8 = (bf16[1,1,64,8,8,128]{5,4,3,2,1,0:T(8,128)(2,1)S(1)}, bf16[1,1,64,8,8,128]{5,4,3,2,1,0:T(8,128)(2,1)}, u32[]{:S(2)}) copy-start(bf16[1,1,64,8,8,128]{5,4,3,2,1,0:T(8,128)(2,1)} %param.5) | copy-start | bytes 3145732
  1.4 23.0 %collective-permute-start.8 = (f32[2,4,128]{2,1,0:T(4,128)S(1)}, f32[2,4,128]{2,1,0:T(4,128)S(1)}, u32[]{:S(2)}, u32[]{:S(2)}) collective-permute-start(f32[2,4,128]{2,1,0:T(4,128)S(1)} %get-tuple-element.17), channel_id=1, source_target_pairs={{0,8},{8,16},{16,24},{24,32},{32,40},{40,48},{48,56},{56,64},{64,7... | collective-permute-start | bytes 12296 | tf_op jit(solution)/shard_map/ppermute | solution.py:21
  3.6 20.9 %collective-permute-start.9 = (f32[2,4,128]{2,1,0:T(4,128)S(1)}, f32[2,4,128]{2,1,0:T(4,128)S(1)}, u32[]{:S(2)}, u32[]{:S(2)}) collective-permute-start(f32[2,4,128]{2,1,0:T(4,128)S(1)} %get-tuple-element.16), channel_id=1, source_target_pairs={{0,120},{8,0},{16,8},{24,16},{32,24},{40,32},{48,40},{56,48},{64,5... | collective-permute-start | bytes 12296 | tf_op jit(solution)/shard_map/ppermute | solution.py:21
  8.5 1.1 %copy-start.9 = (bf16[256,1152]{1,0:T(8,128)(2,1)S(1)}, bf16[256,1152]{1,0:T(8,128)(2,1)}, u32[]{:S(2)}) copy-start(bf16[256,1152]{1,0:T(8,128)(2,1)} %k_ref.1) | copy-start | bytes 1769476
  9.5 14.9 %copy-start.11 = (f32[4,4,128]{2,1,0:T(4,128)S(1)}, f32[4,4,128]{2,1,0:T(4,128)}, u32[]{:S(2)}) copy-start(f32[4,4,128]{2,1,0:T(4,128)} %param.4) | copy-start | bytes 24580
  10.5 40.0 %copy-start.10 = (s32[32,1]{0,1:T(1,128)S(1)}, s32[32,1]{0,1:T(1,128)}, u32[]{:S(2)}) copy-start(s32[32,1]{0,1:T(1,128)} %param.7) | copy-start | bytes 388
  10.5 48.1 %all-to-all-start.1 = ((bf16[128,2,1152]{2,1,0:T(2,128)(2,1)}), bf16[128,2,1152]{2,1,0:T(2,128)(2,1)S(1)}, u32[]{:S(2)}, u32[]{:S(2)}) async-start(bf16[128,2,1152]{2,1,0:T(2,128)(2,1)} %shard_map.61), calls=%async_computation.1 | async-start | bytes 1179648 | tf_op jit(solution)/shard_map/all_to_all | solution.py:263
  17.4 25.9 %collective-permute-start.2 = (bf16[2,4,4,64,128]{4,3,2,1,0:T(8,128)(2,1)S(1)}, bf16[2,4,4,64,128]{4,3,2,1,0:T(8,128)(2,1)S(1)}, u32[]{:S(2)}, u32[]{:S(2)}) collective-permute-start(bf16[2,4,4,64,128]{4,3,2,1,0:T(8,128)(2,1)S(1)} %get-tuple-element.8), channel_id=1, source_target_pairs={{0,1},{1,2},{2,3},{3,4},{4,5},{5,6},{6,7},{7,0},{8,9},{9,10},{10,1... | collective-permute-start | bytes 1572872 | tf_op jit(solution)/shard_map/ppermute | solution.py:21
  19.1 26.0 %collective-permute-start.3 = (bf16[2,4,4,64,128]{4,3,2,1,0:T(8,128)(2,1)S(1)}, bf16[2,4,4,64,128]{4,3,2,1,0:T(8,128)(2,1)S(1)}, u32[]{:S(2)}, u32[]{:S(2)}) collective-permute-start(bf16[2,4,4,64,128]{4,3,2,1,0:T(8,128)(2,1)S(1)} %get-tuple-element.9), channel_id=1, source_target_pairs={{0,7},{1,0},{2,1},{3,2},{4,3},{5,4},{6,5},{7,6},{8,15},{9,8},{10,9... | collective-permute-start | bytes 1572872 | tf_op jit(solution)/shard_map/ppermute | solution.py:21
  19.1 17.2 %collective-permute-start.1 = (bf16[2,4,4,64,128]{4,3,2,1,0:T(8,128)(2,1)S(1)}, bf16[2,4,4,64,128]{4,3,2,1,0:T(8,128)(2,1)S(1)}, u32[]{:S(2)}, u32[]{:S(2)}) collective-permute-start(bf16[2,4,4,64,128]{4,3,2,1,0:T(8,128)(2,1)S(1)} %get-tuple-element.6.refs_0_), channel_id=1, source_target_pairs={{0,120},{8,0},{16,8},{24,16},{32,24},{40,32},{48,40},{56,48},{64,5... | collective-permute-start | bytes 1572872 | tf_op jit(solution)/shard_map/ppermute | solution.py:21
  24.5 15.8 %collective-permute-start = (bf16[2,4,4,64,128]{4,3,2,1,0:T(8,128)(2,1)S(1)}, bf16[2,4,4,64,128]{4,3,2,1,0:T(8,128)(2,1)S(1)}, u32[]{:S(2)}, u32[]{:S(2)}) collective-permute-start(bf16[2,4,4,64,128]{4,3,2,1,0:T(8,128)(2,1)S(1)} %get-tuple-element.7.refs_1_), channel_id=1, source_target_pairs={{0,8},{8,16},{16,24},{24,32},{32,40},{40,48},{48,56},{56,64},{64,7... | collective-permute-start | bytes 1572872 | tf_op jit(solution)/shard_map/ppermute | solution.py:21
  24.5 18.3 %collective-permute-start.11 = (f32[8,2,128]{2,1,0:T(2,128)S(1)}, f32[8,2,128]{2,1,0:T(2,128)S(1)}, u32[]{:S(2)}, u32[]{:S(2)}) collective-permute-start(f32[8,2,128]{2,1,0:T(2,128)S(1)} %get-tuple-element.14), channel_id=1, source_target_pairs={{0,7},{1,0},{2,1},{3,2},{4,3},{5,4},{6,5},{7,6},{8,15},{9,8},{10,9... | collective-permute-start | bytes 24584 | tf_op jit(solution)/shard_map/ppermute | solution.py:21
  36.2 7.1 %collective-permute-start.10 = (f32[8,2,128]{2,1,0:T(2,128)S(1)}, f32[8,2,128]{2,1,0:T(2,128)S(1)}, u32[]{:S(2)}, u32[]{:S(2)}) collective-permute-start(f32[8,2,128]{2,1,0:T(2,128)S(1)} %get-tuple-element.15), channel_id=1, source_target_pairs={{0,1},{1,2},{2,3},{3,4},{4,5},{5,6},{6,7},{7,0},{8,9},{9,10},{10,1... | collective-permute-start | bytes 24584 | tf_op jit(solution)/shard_map/ppermute | solution.py:21
  40.2 7.4 %collective-permute-start.7 = (bf16[4,4,64,128]{3,2,1,0:T(8,128)(2,1)S(1)}, bf16[4,4,64,128]{3,2,1,0:T(8,128)(2,1)S(1)}, u32[]{:S(2)}, u32[]{:S(2)}) collective-permute-start(bf16[4,4,64,128]{3,2,1,0:T(8,128)(2,1)S(1)} %get-tuple-element.10), channel_id=1, source_target_pairs={{0,7},{1,0},{2,1},{3,2},{4,3},{5,4},{6,5},{7,6},{8,15},{9,8},{10,9... | collective-permute-start | bytes 786440 | tf_op jit(solution)/shard_map/ppermute | solution.py:21
  42.8 4.8 %collective-permute-start.6 = (bf16[4,4,64,128]{3,2,1,0:T(8,128)(2,1)S(1)}, bf16[4,4,64,128]{3,2,1,0:T(8,128)(2,1)S(1)}, u32[]{:S(2)}, u32[]{:S(2)}) collective-permute-start(bf16[4,4,64,128]{3,2,1,0:T(8,128)(2,1)S(1)} %get-tuple-element.11), channel_id=1, source_target_pairs={{0,1},{1,2},{2,3},{3,4},{4,5},{5,6},{6,7},{7,0},{8,9},{9,10},{10,1... | collective-permute-start | bytes 786440 | tf_op jit(solution)/shard_map/ppermute | solution.py:21
  43.3 7.1 %collective-permute-start.5 = (bf16[4,4,64,128]{3,2,1,0:T(8,128)(2,1)S(1)}, bf16[4,4,64,128]{3,2,1,0:T(8,128)(2,1)S(1)}, u32[]{:S(2)}, u32[]{:S(2)}) collective-permute-start(bf16[4,4,64,128]{3,2,1,0:T(8,128)(2,1)S(1)} %get-tuple-element.12), channel_id=1, source_target_pairs={{0,7},{1,0},{2,1},{3,2},{4,3},{5,4},{6,5},{7,6},{8,15},{9,8},{10,9... | collective-permute-start | bytes 786440 | tf_op jit(solution)/shard_map/ppermute | solution.py:21
  43.3 7.1 %collective-permute-start.4 = (bf16[4,4,64,128]{3,2,1,0:T(8,128)(2,1)S(1)}, bf16[4,4,64,128]{3,2,1,0:T(8,128)(2,1)S(1)}, u32[]{:S(2)}, u32[]{:S(2)}) collective-permute-start(bf16[4,4,64,128]{3,2,1,0:T(8,128)(2,1)S(1)} %get-tuple-element.13), channel_id=1, source_target_pairs={{0,1},{1,2},{2,3},{3,4},{4,5},{5,6},{6,7},{7,0},{8,9},{9,10},{10,1... | collective-permute-start | bytes 786440 | tf_op jit(solution)/shard_map/ppermute | solution.py:21
  45.1 9.7 %copy-start = (bf16[2,4,4,64,128]{4,3,2,1,0:T(8,128)(2,1)}, bf16[2,4,4,64,128]{4,3,2,1,0:T(8,128)(2,1)S(1)}, u32[]{:S(2)}) copy-start(bf16[2,4,4,64,128]{4,3,2,1,0:T(8,128)(2,1)S(1)} %collective-permute-done.3.refs_5_) | copy-start | bytes 1572868
  47.6 7.2 %copy-start.2 = (bf16[4,4,64,128]{3,2,1,0:T(8,128)(2,1)}, bf16[4,4,64,128]{3,2,1,0:T(8,128)(2,1)S(1)}, u32[]{:S(2)}) copy-start(bf16[4,4,64,128]{3,2,1,0:T(8,128)(2,1)S(1)} %collective-permute-done.6.refs_8_) | copy-start | bytes 786436
  50.4 4.4 %copy-start.4 = (bf16[4,4,64,128]{3,2,1,0:T(8,128)(2,1)}, bf16[4,4,64,128]{3,2,1,0:T(8,128)(2,1)S(1)}, u32[]{:S(2)}) copy-start(bf16[4,4,64,128]{3,2,1,0:T(8,128)(2,1)S(1)} %collective-permute-done.5.refs_7_) | copy-start | bytes 786436
  50.4 4.4 %copy-start.6 = (bf16[4,4,64,128]{3,2,1,0:T(8,128)(2,1)}, bf16[4,4,64,128]{3,2,1,0:T(8,128)(2,1)S(1)}, u32[]{:S(2)}) copy-start(bf16[4,4,64,128]{3,2,1,0:T(8,128)(2,1)S(1)} %collective-permute-done.4.refs_6_) | copy-start | bytes 786436
  58.5 29.5 %all-to-all-start = ((f16[256,2,1280]{2,1,0:T(2,128)(2,1)}), f16[256,2,1280]{2,1,0:T(2,128)(2,1)}, u32[]{:S(2)}, u32[]{:S(2)}) async-start(f16[256,2,1280]{2,1,0:T(2,128)(2,1)} %convert_element_type.9), calls=%async_computation | async-start | bytes 2621440 | tf_op jit(solution)/shard_map/all_to_all | solution.py:283
  66.1 1.0 %copy-start.1 = (bf16[2,4,4,64,128]{4,3,2,1,0:T(8,128)(2,1)S(1)}, bf16[2,4,4,64,128]{4,3,2,1,0:T(8,128)(2,1)}, u32[]{:S(2)}) copy-start(bf16[2,4,4,64,128]{4,3,2,1,0:T(8,128)(2,1)} %copy-done) | copy-start | bytes 1572868
  67.2 0.9 %copy-start.3 = (bf16[4,4,64,128]{3,2,1,0:T(8,128)(2,1)S(1)}, bf16[4,4,64,128]{3,2,1,0:T(8,128)(2,1)}, u32[]{:S(2)}) copy-start(bf16[4,4,64,128]{3,2,1,0:T(8,128)(2,1)} %copy-done.2) | copy-start | bytes 786436
  68.1 0.9 %copy-start.5 = (bf16[4,4,64,128]{3,2,1,0:T(8,128)(2,1)S(1)}, bf16[4,4,64,128]{3,2,1,0:T(8,128)(2,1)}, u32[]{:S(2)}) copy-start(bf16[4,4,64,128]{3,2,1,0:T(8,128)(2,1)} %copy-done.4) | copy-start | bytes 786436
  69.1 0.9 %copy-start.7 = (bf16[4,4,64,128]{3,2,1,0:T(8,128)(2,1)S(1)}, bf16[4,4,64,128]{3,2,1,0:T(8,128)(2,1)}, u32[]{:S(2)}) copy-start(bf16[4,4,64,128]{3,2,1,0:T(8,128)(2,1)} %copy-done.6) | copy-start | bytes 786436

commit v2 on v1

v2 whole, which is shorter than its diff:
```python
import functools

import jax
import jax.numpy as jnp
from jax import lax
from jax.experimental import pallas as pl
from jax.experimental.pallas import tpu as pltpu
from jax.sharding import PartitionSpec as P

AT_X = {1: 1, 0: 2}
AT_Y = {1: 3, 0: 4}
AT_XY = {(1, 1): 5, (1, 0): 6, (0, 1): 7, (0, 0): 8}
SIDES = ((0, 0), (0, 1), (1, 0), (1, 1))
STEPS = 64.0
TOP = 32700.0
SMALLEST = 1e-33
VMEM = pl.BlockSpec(memory_space=pltpu.VMEM)
SMEM = pl.BlockSpec(memory_space=pltpu.SMEM)


def shifted(shard, axis, by):
    size = lax.axis_size(axis)
    return lax.ppermute(shard, axis, [(i, (i + by) % size) for i in range(size)])


def params(mib=16):
    return pltpu.CompilerParams(vmem_limit_bytes=mib << 20)


def packed_rows(rows, func_count):
    value = jnp.concatenate(rows, axis=0)
    pieces = []
    for _ in range(3):
        piece = value.astype(jnp.bfloat16).astype(jnp.float32)
        pieces.append(piece)
        value = value - piece
    count = func_count - 3 * len(rows)
    pieces.append(jnp.zeros((count, value.shape[1]), jnp.float32))
    return jnp.concatenate(pieces, axis=0).astype(jnp.bfloat16)


def unpacked_rows(block, count):
    block = block.astype(jnp.float32)
    return block[:count] + block[count : 2 * count] + block[2 * count : 3 * count]


def split_x_kernel(half, f_ref, pot_ref, *out_refs):
    count = half * half
    func_count = f_ref.shape[0]
    inner = pot_ref.shape[0]
    margin = half - inner // 2
    for x in range(2 * half):
        rows = jnp.swapaxes(f_ref[:, x], 0, 1)
        side, at = divmod(x, half)
        for y in (0, 1):
            start = y * (count + 1) + at * half
            out_refs[side][start : start + half] = rows[y * half : (y + 1) * half]
    for side in (0, 1):
        first = side * (inner - margin)
        out_refs[side][count] = packed_rows(
            [pot_ref[first + i, j : j + 1] for i in range(margin) for j in range(inner)], func_count
        )


def split_y_kernel(half, x0_ref, x1_ref, pot_ref, *out_refs):
    count = half * half
    func_count = x0_ref.shape[1]
    inner = pot_ref.shape[0]
    margin = half - inner // 2
    for side in (0, 1):
        for side_x, x_ref in enumerate((x0_ref, x1_ref)):
            start, taken = side_x * (count + 1), side * (count + 1)
            out_refs[side][start : start + count] = x_ref[taken : taken + count]
        first = side * (inner - margin)
        out_refs[side][count] = packed_rows(
            [pot_ref[i, first + j : first + j + 1] for i in range(inner) for j in range(margin)], func_count
        )


class Boxes:
    def __init__(self, half, refs, pot_ref):
        self.half, self.count = half, half * half
        self.own, self.x, self.y, self.xy = refs[0:2], refs[2:4], refs[4:6], dict(zip(SIDES, refs[6:10]))
        self.pot = pot_ref
        self.inner = pot_ref.shape[0]
        self.margin = half - self.inner // 2
        self.edge = {}

    def columns(self, sides, at_x, at_y):
        side_x, side_y = sides
        at = at_x * self.half + at_y
        return [
            self.own[side_x][side_y * (self.count + 1) + at],
            self.x[side_x][side_y * (self.count + 1) + at],
            self.y[side_y][side_x * (self.count + 1) + at],
            self.xy[sides][1 - side_y + at],
        ]

    def edge_row(self, key, row):
        if key not in self.edge:
            ref = self.xy[key] if isinstance(key, tuple) and key in self.xy else getattr(self, key[0])[key[1]]
            at = self.count
            if key in self.xy:
                at = self.count * key[1]
            self.edge[key] = unpacked_rows(ref[at], self.margin * self.inner)
        return self.edge[key][row : row + 1]

    def potential(self, x, y):
        inner, margin = self.inner, self.margin
        in_x, in_y = (margin <= v < margin + inner for v in (x, y))
        side_x, side_y = x // self.half, y // self.half
        near_x, near_y = x - side_x * (margin + inner), y - side_y * (margin + inner)
        if in_x and in_y:
            return self.pot[x - margin, y - margin : y - margin + 1]
        if in_y:
            return self.edge_row(("x", side_x), near_x * inner + y - margin)
        if in_x:
            return self.edge_row(("y", side_y), (x - margin) * margin + near_y)
        column = near_y if side_y else inner - margin + near_y
        return self.edge_row((side_x, side_y), near_x * inner + column)


def pair_kernel(k_ref, o_ref):
    o_ref[...] = k_ref[...].reshape(o_ref.shape)


def stencil(cell, potential_row, half, x, y, zero_low, zero_high):
    value = cell(x, y)
    beside = jnp.where(zero_high, 0.0, pltpu.roll(value, value.shape[1] - 1, 1)) + jnp.where(
        zero_low, 0.0, pltpu.roll(value, 1, 1)
    )
    for near_x, near_y in ((x + 1, y), (x - 1, y), (x, y + 1), (x, y - 1)):
        if 0 <= near_x < 2 * half and 0 <= near_y < 2 * half:
            beside = beside + cell(near_x, near_y)
    return (3.0 + potential_row(x, y)) * value - 0.5 * beside


def edges(func_count, depth):
    lane = lax.broadcasted_iota(jnp.int32, (func_count, depth), 1)
    return lane == 0, lane == depth - 1


def ranks(owner_ref, count_ref):
    def clear(i, carry):
        count_ref[owner_ref[i]] = 0
        return carry

    lax.fori_loop(0, owner_ref.shape[0], clear, 0)
    found = []
    for a in range(owner_ref.shape[0]):
        owner = owner_ref[a]
        rank = count_ref[owner]
        count_ref[owner] = rank + 1
        found.append((owner, rank))
    return found


def pairs_kernel(half, cap, owner_ref, pot_ref, *refs):
    out_ref, wide_ref, sums_ref, count_ref = refs[10:14]
    boxes = Boxes(half, refs[0:10], pot_ref)
    func_count, depth = refs[0].shape[-2:]
    atoms = owner_ref.shape[0]
    low_edge, high_edge = edges(func_count, depth)

    def cell(x, y):
        side_x, at_x = divmod(x, half)
        side_y, at_y = divmod(y, half)
        return boxes.columns((side_x, side_y), at_x, at_y)[0].astype(jnp.float32)

    wide_ref[...] = jnp.zeros(wide_ref.shape, wide_ref.dtype)
    block = {}
    for side_x, side_y in SIDES:
        total = jnp.zeros((2 * func_count, 4 * func_count), jnp.float32)
        for at_x in range(half):
            left, right = [], []
            for at_y in range(half):
                columns = boxes.columns((side_x, side_y), at_x, at_y)
                applied = stencil(
                    cell, boxes.potential, half, side_x * half + at_x, side_y * half + at_y, low_edge, high_edge
                ).astype(jnp.bfloat16)
                left.append(jnp.concatenate([columns[0], applied], axis=0))
                right.append(jnp.concatenate(columns, axis=0))
            total = total + lax.dot_general(
                jnp.concatenate(left, axis=1),
                jnp.concatenate(right, axis=1),
                (((1,), (1,)), ((), ())),
                preferred_element_type=jnp.float32,
            )
        block[side_x, side_y] = total

    def summed(part, *sides):
        return functools.reduce(
            jnp.add, [block[s][:, part * func_count : (part + 1) * func_count] for s in sides]
        )

    parts = [summed(0, *SIDES)] + [None] * 8
    for side in (0, 1):
        parts[AT_X[side]] = summed(1, (side, 0), (side, 1))
        parts[AT_Y[side]] = summed(2, (0, side), (1, side))
    for sides in SIDES:
        parts[AT_XY[sides]] = summed(3, sides)
    width = 9 * func_count
    volume = 1.0 / (4 * half * half * depth)
    sums = jnp.concatenate(parts, axis=1) * volume
    for t in range(0, width, depth):
        sums_ref[t // depth, :, : min(depth, width - t)] = sums[:, t : t + depth]

    def atom_rows(start):
        picked = []
        for i in (0, 1):
            tiles = [sums_ref[t, pl.ds(start + i, atoms, stride=2), :] for t in range(sums_ref.shape[0])]
            picked.append(jnp.concatenate(tiles, axis=1)[:, :width])
        return jnp.concatenate(picked, axis=1)

    coded = []
    for start in (0, func_count):
        row = atom_rows(start)
        largest = jnp.maximum(jnp.max(jnp.abs(row), axis=1, keepdims=True), SMALLEST)
        power = jnp.ceil(STEPS * jnp.log2(largest))
        coded.append((row * (TOP * jnp.exp2(-power / STEPS)), jnp.broadcast_to(power, (atoms, depth))))
    tiles = 2 * width // depth
    for a, (owner, rank) in enumerate(ranks(owner_ref, count_ref)):
        for m, (row, power) in enumerate(coded):
            for t in range(tiles):
                wide_ref[owner, pl.ds(rank * (2 * tiles) + 2 * t + m, 1), :] = row[
                    a : a + 1, t * depth : (t + 1) * depth
                ]
            wide_ref[owner, pl.ds(cap * 2 * tiles + 2 * rank + m, 1), :] = power[a : a + 1]
    for owner in range(out_ref.shape[0]):
        out_ref[owner] = jnp.round(wide_ref[owner]).astype(jnp.int32).astype(jnp.int16)


def unpack_kernel(cap, in_ref, out_ref):
    chunks, rows, depth = in_ref.shape
    data = rows - 2 * cap
    line = lax.broadcasted_iota(jnp.int32, (data, depth), 0)
    even = line % 2 == 0
    for c in range(chunks):
        values = in_ref[c].astype(jnp.int32).astype(jnp.float32)
        scale = jnp.exp2(values[data:] * (1.0 / STEPS)) * (1.0 / TOP)
        spread = jnp.where(even, scale[0:1], scale[1:2])
        for rank in range(1, cap):
            spread = jnp.where(
                line >= rank * (data // cap),
                jnp.where(even, scale[2 * rank : 2 * rank + 1], scale[2 * rank + 1 : 2 * rank + 2]),
                spread,
            )
        values = values[:data] * spread
        for rank in range(cap):
            for t in range(data // (2 * cap)):
                start = rank * (data // cap) + 2 * t
                out_ref[c * cap + rank, :, t * depth : (t + 1) * depth] = values[start : start + 2]


def mix_kernel(half, owner_ref, kernel_ref, pot_ref, *refs):
    out_ref, rows_ref, mixed_ref, count_ref, sems = refs[10:15]
    held = refs[15:25]
    copies = [pltpu.make_async_copy(refs[i], held[i], sems.at[i]) for i in range(10)]
    for copy in copies:
        copy.start()
    boxes = Boxes(half, held, pot_ref)
    func_count, depth = refs[0].shape[-2:]
    atoms = owner_ref.shape[0]
    low_edge, high_edge = edges(func_count, depth)
    for a, (owner, rank) in enumerate(ranks(owner_ref, count_ref)):
        both = kernel_ref[owner].astype(jnp.float32)
        rows_ref[a : a + 1, :] = jnp.where(rank == 0, both[0:1], both[1:2])
    width = 9 * func_count
    matrix = jnp.concatenate([rows_ref[:, :width], rows_ref[:, width:]], axis=0)
    for copy in copies:
        copy.wait()
    for side_x, side_y in SIDES:
        at = (0, AT_X[side_x], AT_Y[side_y], AT_XY[side_x, side_y])
        left = jnp.concatenate(
            [matrix[:, k * func_count : (k + 1) * func_count] for k in at], axis=1
        ).astype(jnp.bfloat16)
        for at_x in range(half):
            for at_y in range(0, half, 2):
                right = jnp.concatenate(
                    [
                        jnp.concatenate(boxes.columns((side_x, side_y), at_x, y), axis=0)
                        for y in (at_y, at_y + 1)
                    ],
                    axis=1,
                )
                got = jnp.dot(left, right, preferred_element_type=jnp.float32)
                for i in (0, 1):
                    mixed_ref[side_x * half + at_x, side_y * half + at_y + i] = got[
                        :, i * depth : (i + 1) * depth
                    ]

    def cell(x, y):
        return mixed_ref[x, y]

    for x in range(2 * half):
        made = [
            stencil(cell, boxes.potential, half, x, y, low_edge, high_edge) for y in range(2 * half)
        ]
        for odd in (0, 1):
            stacked = jnp.stack([m[odd * atoms : (odd + 1) * atoms] for m in made], axis=0)
            out_ref[:, odd, x] = jnp.swapaxes(stacked, 0, 1).astype(out_ref.dtype)


def body(potential, functions, kernel_store, owners):
    own_funcs = functions[0, 0]
    func_count, ext_x, ext_y, depth = own_funcs.shape
    half = ext_x // 2
    margin = (ext_x - potential.shape[0]) // 2
    device_count = lax.axis_size("brick") * lax.axis_size("narrow")
    owner_col = owners[:, 0]
    atoms = owner_col.shape[0]
    slot_count, row_width = kernel_store.shape
    slot_cap = slot_count // device_count
    bf16 = jnp.bfloat16
    struct = jax.ShapeDtypeStruct

    band = struct((2 * half * half + 1, func_count, depth), bf16)

    def split(kernel, *operands):
        return pl.pallas_call(
            functools.partial(kernel, half),
            out_shape=(band,) * 2,
            in_specs=[VMEM] * len(operands),
            out_specs=(VMEM,) * 2,
            compiler_params=params(),
            cost_estimate=pl.CostEstimate(flops=0, transcendentals=0, bytes_accessed=2 << 20),
        )(*operands)

    own_x = split(split_x_kernel, own_funcs, potential)
    from_x = (shifted(own_x[1], "brick", 1), shifted(own_x[0], "brick", -1))
    own_y = split(split_y_kernel, *own_x, potential)
    from_y = (shifted(own_y[1], "narrow", 1), shifted(own_y[0], "narrow", -1))
    kernel_store, *_ = lax.optimization_barrier((kernel_store, *own_y))
    kernel_out = pl.pallas_call(
        pair_kernel,
        out_shape=struct((device_count, slot_cap, row_width), bf16),
        in_specs=[VMEM],
        out_specs=VMEM,
        compiler_params=params(),
        cost_estimate=pl.CostEstimate(flops=0, transcendentals=0, bytes_accessed=1 << 20),
    )(kernel_store)
    kernel_in = lax.all_to_all(
        kernel_out, ("brick", "narrow"), split_axis=0, concat_axis=0, tiled=True
    )

    count = half * half
    bands = lax.optimization_barrier((*from_x, *own_y, kernel_out))[:2]
    corners = [bands[sx][: count + 1] if sy else bands[sx][count:] for sx, sy in SIDES]
    from_xy = [shifted(c, "narrow", -1 if sy else 1) for c, (sx, sy) in zip(corners, SIDES)]

    boxes = (*own_x, *bands, *from_y, *from_xy)
    anywhere = pl.BlockSpec(memory_space=pltpu.HBM)
    cells = ext_x * ext_y * depth
    lines = 2 * slot_cap * (row_width // depth + 1)
    outgoing = pl.pallas_call(
        functools.partial(pairs_kernel, half, slot_cap),
        out_shape=struct((device_count, lines, depth), jnp.int16),
        in_specs=[SMEM] + [VMEM] * 11,
        out_specs=VMEM,
        scratch_shapes=[
            pltpu.VMEM((device_count, lines, depth), jnp.float32),
            pltpu.VMEM((pl.cdiv(9 * func_count, depth), 2 * func_count, depth), jnp.float32),
            pltpu.SMEM((device_count,), jnp.int32),
        ],
        compiler_params=params(60),
        cost_estimate=pl.CostEstimate(
            flops=16 * func_count * func_count * cells, transcendentals=0, bytes_accessed=7 << 20
        ),
    )(owner_col, potential, *boxes)
    blocks = lax.all_to_all(outgoing, ("brick", "narrow"), split_axis=0, concat_axis=0, tiled=True)
    steps = 8
    chunk = device_count // steps
    blocks = pl.pallas_call(
        functools.partial(unpack_kernel, slot_cap),
        grid=(steps,),
        out_shape=struct((slot_count, 2, row_width), jnp.float32),
        in_specs=[pl.BlockSpec((chunk, lines, depth), lambda i: (i, 0, 0))],
        out_specs=pl.BlockSpec((chunk * slot_cap, 2, row_width), lambda i: (i, 0, 0)),
        compiler_params=params(),
    )(blocks)

    gradient = pl.pallas_call(
        functools.partial(mix_kernel, half),
        out_shape=struct((atoms, 2, ext_x, ext_y, depth), bf16),
        in_specs=[SMEM, VMEM, VMEM] + [anywhere] * 10,
        out_specs=VMEM,
        scratch_shapes=[
            pltpu.VMEM((atoms, row_width), jnp.float32),
            pltpu.VMEM((ext_x, ext_y, func_count, depth), jnp.float32),
            pltpu.SMEM((device_count,), jnp.int32),
            pltpu.SemaphoreType.DMA((10,)),
        ]
        + [pltpu.VMEM(box.shape, box.dtype) for box in boxes],
        compiler_params=params(60),
        cost_estimate=pl.CostEstimate(
            flops=8 * func_count * func_count * cells, transcendentals=0, bytes_accessed=7 << 20
        ),
    )(owner_col, kernel_in, potential, *boxes)
    return (blocks, gradient.reshape(functions.shape))


def solution(mesh):
    in_specs = (
        P("brick", "narrow", None),
        P("brick", "narrow", None, None, None, None),
        P(("brick", "narrow"), None),
        P(("brick", "narrow"), None),
    )
    out_specs = (P(("brick", "narrow"), None, None), P("brick", "narrow", None, None, None, None))
    return jax.shard_map(body, mesh=mesh, in_specs=in_specs, out_specs=out_specs, check_vma=False)
```

time: 93.5 us -> 77.9 us (0.83)
  other arithmetic: 8.38 us -> 0 us
  Pallas kernels: 9.4 us -> 16.8 us
  waiting for transfers between devices: 31.5 us -> 25.3 us
  starting transfers between devices: 36.8 us -> 31.9 us
  local copies, waits for them, and re-layouts: 6.14 us -> 2.8 us
    ppermute x12 -> x8, starting transfers between devices: 22.7 us -> 14.5 us  [shifted(): lax.ppermute(shard, axis, [(i, (i + by) % size) for i in range(size)])]
    ppermute x12 -> x8, waiting for transfers between devices: 17.1 us -> 9.28 us  [shifted(): lax.ppermute(shard, axis, [(i, (i + by) % size) for i in range(size)])]
    convert_element_type x1 -> x0, other arithmetic: 3.7 us -> none  [body(): outgoing.astype(jnp.float16)]
    mul x1 -> x0, other arithmetic: 3.6 us -> none  [body(): blocks = blocks[:, :, :row_width].astype(jnp.float32) * jnp.exp2(power)]
    pallas_call x1 -> x3, Pallas kernels: 0.46 us -> 4.01 us  [the longest x1 3.48 us: body(): pl.pallas_call(functools.partial(unpack_kernel, slot_cap), grid=(steps,),...]
    all_to_all x1, starting transfers between devices: 6.48 us -> 9.52 us  [body(): lax.all_to_all(kernel_out, ('brick', 'narrow'), split_axis=0, concat_axis...]
    pallas_call x1, Pallas kernels: 3.65 us -> 6.08 us  [body(): pl.pallas_call(functools.partial(mix_kernel, half), out_shape=struct((ato...]
    unnamed x26 -> x22, local copies, waits for them, and re-layouts: 4.98 us -> 2.71 us
  transfers between devices with their start and end apart: 14 -> 10, of which waited for: 5 -> 4; matrix products, arithmetic and copies ran while one was open for 4% -> 0% of each run, Pallas kernels for 10% -> 17%
where the time goes in v2:
time: 77.9 us; the launch traced here: 77.6 us
  starting transfers between devices  31.9 us (41%)
  waiting for transfers between devices  25.3 us (32%)
  Pallas kernels  16.8 us (22%)
  local copies, waits for them, and re-layouts  2.8 us (4%)
    all_to_all x1, waiting for transfers between devices, body(): lax.all_to_all(outgoing, ('brick', 'narrow'), split_axis=0, concat_axis=0...  16.1 us
    ppermute x8, starting transfers between devices, shifted(): lax.ppermute(shard, axis, [(i, (i + by) % size) for i in range(size)])  14.5 us
    all_to_all x1, starting transfers between devices, body(): lax.all_to_all(kernel_out, ('brick', 'narrow'), split_axis=0, concat_axis...  9.52 us
    ppermute x8, waiting for transfers between devices, shifted(): lax.ppermute(shard, axis, [(i, (i + by) % size) for i in range(size)])  9.28 us
    all_to_all x1, starting transfers between devices, body(): lax.all_to_all(outgoing, ('brick', 'narrow'), split_axis=0, concat_axis=0...  7.89 us
    pallas_call x1, Pallas kernels, body(): pl.pallas_call(functools.partial(mix_kernel, half), out_shape=struct((ato...  6.08 us
    pallas_call x1, Pallas kernels, body(): pl.pallas_call(functools.partial(pairs_kernel, half, slot_cap), out_shape...  5.76 us
    pallas_call x1, Pallas kernels, body(): pl.pallas_call(functools.partial(unpack_kernel, slot_cap), grid=(steps,),...  3.48 us
  transfers between devices with their start and end apart: 10, of which 4 were waited for; matrix products, arithmetic and copies ran while one was open for 0% of the time, Pallas kernels for 17%

profile of v2, /device:TPU:1, one launch (start us, length us, event | category | flops | bytes accessed | tf_op | source)
XLA Modules:
  0.0 77.6 jit_solution(10899501212497063667)
XLA Ops:
  0.6 1.2 %copy-done.2 = bf16[1,1,64,8,8,128]{5,4,3,2,1,0:T(8,128)(2,1)S(1)} copy-done((bf16[1,1,64,8,8,128]{5,4,3,2,1,0:T(8,128)(2,1)S(1)}, bf16[1,1,64,8,8,128]{5,4,3,2,1,0:T(8,128)(2,1)}, u32[]{:S(2)}) %copy-start.2) | copy-done | bytes 1048600
  1.9 0.7 copy-done.4
  2.6 0.4 shard_map.59
  3.0 0.0 copy-start.1
  3.0 7.1 %collective-permute-start.1 = (bf16[33,64,128]{2,1,0:T(8,128)(2,1)S(1)}, bf16[33,64,128]{2,1,0:T(8,128)(2,1)S(1)}, u32[]{:S(2)}, u32[]{:S(2)}) collective-permute-start(bf16[33,64,128]{2,1,0:T(8,128)(2,1)S(1)} %get-tuple-element.9.x0_ref.refs_0_), channel_id=1, source_target_pairs={{0,120},{8,0},{16,8},{24,16},{32,24},{40,32},{48,40},{56,48},{64,5... | collective-permute-start | bytes 1622024 | tf_op jit(solution)/shard_map/ppermute | solution.py:23
  10.1 0.0 collective-permute-start
  10.1 0.1 shard_map.60
  10.2 1.0 %collective-permute-start.3 = (bf16[33,64,128]{2,1,0:T(8,128)(2,1)S(1)}, bf16[33,64,128]{2,1,0:T(8,128)(2,1)}, u32[]{:S(2)}, u32[]{:S(2)}) collective-permute-start(bf16[33,64,128]{2,1,0:T(8,128)(2,1)S(1)} %get-tuple-element.11), channel_id=1, source_target_pairs={{0,7},{1,0},{2,1},{3,2},{4,3},{5,4},{6,5},{7,6},{8,15},{9,8},{10,9... | collective-permute-start | bytes 1622024 | tf_op jit(solution)/shard_map/ppermute | solution.py:23
  11.2 1.1 %collective-permute-start.2 = (bf16[33,64,128]{2,1,0:T(8,128)(2,1)S(1)}, bf16[33,64,128]{2,1,0:T(8,128)(2,1)}, u32[]{:S(2)}, u32[]{:S(2)}) collective-permute-start(bf16[33,64,128]{2,1,0:T(8,128)(2,1)S(1)} %get-tuple-element.12), channel_id=1, source_target_pairs={{0,1},{1,2},{2,3},{3,4},{4,5},{5,6},{6,7},{7,0},{8,9},{9,10},{10,1... | collective-permute-start | bytes 1622024 | tf_op jit(solution)/shard_map/ppermute | solution.py:23
  12.3 0.9 %shard_map.61 = bf16[128,2,1152]{2,1,0:T(2,128)(2,1)} custom-call(bf16[256,1152]{1,0:T(8,128)(2,1)S(1)} %copy-done.3), custom_call_target="tpu_custom_call" | custom-call | bytes 1048576 | tf_op jit(solution)/shard_map/pallas_call | solution.py:334
  13.2 0.0 copy-done
  13.2 9.5 %all-to-all-start.1 = ((bf16[128,2,1152]{2,1,0:T(2,128)(2,1)}), bf16[128,2,1152]{2,1,0:T(2,128)(2,1)}, u32[]{:S(2)}, u32[]{:S(2)}) async-start(bf16[128,2,1152]{2,1,0:T(2,128)(2,1)} %shard_map.61), calls=%async_computation.1 | async-start | bytes 1179648 | tf_op jit(solution)/shard_map/all_to_all | solution.py:342
  22.8 0.0 collective-permute-done.1.refs_3_
  22.8 3.5 %collective-permute-done.refs_2_ = bf16[33,64,128]{2,1,0:T(8,128)(2,1)S(1)} collective-permute-done((bf16[33,64,128]{2,1,0:T(8,128)(2,1)S(1)}, bf16[33,64,128]{2,1,0:T(8,128)(2,1)S(1)}, u32[]{:S(2)}, u32[]{:S(2)}) %collective-permute-start) | collective-permute-done | bytes 540704 | tf_op jit(solution)/shard_map/ppermute | solution.py:23
  26.3 2.3 %collective-permute-start.5 = (bf16[17,64,128]{2,1,0:T(8,128)(2,1)S(1)}, bf16[17,64,128]{2,1,0:T(8,128)(2,1)S(1)}, u32[]{:S(2)}, u32[]{:S(2)}) collective-permute-start(bf16[17,64,128]{2,1,0:T(8,128)(2,1)S(1)} %get-tuple-element.18), channel_id=1, source_target_pairs={{0,7},{1,0},{2,1},{3,2},{4,3},{5,4},{6,5},{7,6},{8,15},{9,8},{10,9... | collective-permute-start | bytes 835592 | tf_op jit(solution)/shard_map/ppermute | solution.py:23
  28.6 1.2 %collective-permute-start.4 = (bf16[17,64,128]{2,1,0:T(8,128)(2,1)S(1)}, bf16[17,64,128]{2,1,0:T(8,128)(2,1)S(1)}, u32[]{:S(2)}, u32[]{:S(2)}) collective-permute-start(bf16[17,64,128]{2,1,0:T(8,128)(2,1)S(1)} %get-tuple-element.19), channel_id=1, source_target_pairs={{0,1},{1,2},{2,3},{3,4},{4,5},{5,6},{6,7},{7,0},{8,9},{9,10},{10,1... | collective-permute-start | bytes 835592 | tf_op jit(solution)/shard_map/ppermute | solution.py:23
  29.9 0.0 collective-permute-start.7
  29.9 0.0 collective-permute-done.3.refs_5_
  29.9 1.7 %collective-permute-start.6 = (bf16[17,64,128]{2,1,0:T(8,128)(2,1)S(1)}, bf16[17,64,128]{2,1,0:T(8,128)(2,1)S(1)}, u32[]{:S(2)}, u32[]{:S(2)}) collective-permute-start(bf16[17,64,128]{2,1,0:T(8,128)(2,1)S(1)} %get-tuple-element.17), channel_id=1, source_target_pairs={{0,1},{1,2},{2,3},{3,4},{4,5},{5,6},{6,7},{7,0},{8,9},{9,10},{10,1... | collective-permute-start | bytes 835592 | tf_op jit(solution)/shard_map/ppermute | solution.py:23
  31.7 0.0 collective-permute-done.2.refs_4_
  31.7 2.8 %collective-permute-done.5.refs_7_ = bf16[17,64,128]{2,1,0:T(8,128)(2,1)S(1)} collective-permute-done((bf16[17,64,128]{2,1,0:T(8,128)(2,1)S(1)}, bf16[17,64,128]{2,1,0:T(8,128)(2,1)S(1)}, u32[]{:S(2)}, u32[]{:S(2)}) %collective-permute-start.5) | collective-permute-done | bytes 278560 | tf_op jit(solution)/shard_map/ppermute | solution.py:23
  34.5 0.0 collective-permute-done.4.refs_6_
  34.5 3.0 %collective-permute-done.7.refs_9_ = bf16[17,64,128]{2,1,0:T(8,128)(2,1)S(1)} collective-permute-done((bf16[17,64,128]{2,1,0:T(8,128)(2,1)S(1)}, bf16[17,64,128]{2,1,0:T(8,128)(2,1)S(1)}, u32[]{:S(2)}, u32[]{:S(2)}) %collective-permute-start.7) | collective-permute-done | bytes 278560 | tf_op jit(solution)/shard_map/ppermute | solution.py:23
  37.5 0.0 collective-permute-done.6.refs_8_
  37.5 0.7 copy-done.9
  38.1 0.1 copy-done.10
  38.3 5.8 %shard_map.62 = s16[128,40,128]{2,1,0:T(8,128)(2,1)} custom-call(s32[32]{0:T(128)} %bitcast.5, f32[4,4,128]{2,1,0:T(4,128)} %pot_ref.7, bf16[33,64,128]{2,1,0:T(8,128)(2,1)} %copy-done, bf16[33,64,128]{2,1,0:T(8,128)(2,1)} %copy-done.1, bf16[33,64,128]{2,1,0:T(8,128)(2,1)} %copy-done.6, bf16[33,64,128]{2,1,0:T(8,128)(2,1)} %copy-done.5, ...), custom_call_target="tpu_custom_call" | custom-call | flops 536870912 | bytes 7340032 | tf_op jit(solution)/shard_map/pallas_call | solution.py:355
  44.0 0.0 all-to-all-done.1.kernel_ref
  44.0 7.9 %all-to-all-start = ((s16[128,40,128]{2,1,0:T(8,128)(2,1)}), s16[128,40,128]{2,1,0:T(8,128)(2,1)S(1)}, u32[]{:S(2)}, u32[]{:S(2)}) async-start(s16[128,40,128]{2,1,0:T(8,128)(2,1)} %shard_map.62), calls=%async_computation | async-start | bytes 2621440 | tf_op jit(solution)/shard_map/all_to_all | solution.py:370
  51.9 6.1 %shard_map.64 = bf16[32,2,8,8,128]{4,3,2,1,0:T(8,128)(2,1)} custom-call(s32[32]{0:T(128)} %bitcast.6, bf16[128,2,1152]{2,1,0:T(2,128)(2,1)} %all-to-all-done.1.kernel_ref, f32[4,4,128]{2,1,0:T(4,128)} %pot_ref.7, bf16[33,64,128]{2,1,0:T(8,128)(2,1)} %copy-done, bf16[33,64,128]{2,1,0:T(8,128)(2,1)} %copy-done.1, bf16[33,64,128]{2,1,0:T(8,128)(2,1)} %copy-done.6, ...), custom_call_target="tpu_custom_call" | custom-call | flops 268435456 | bytes 7340032 | tf_op jit(solution)/shard_map/pallas_call | solution.py:382
  58.0 16.1 %all-to-all-done.in_ref = s16[128,40,128]{2,1,0:T(8,128)(2,1)S(1)} async-done(((s16[128,40,128]{2,1,0:T(8,128)(2,1)}), s16[128,40,128]{2,1,0:T(8,128)(2,1)S(1)}, u32[]{:S(2)}, u32[]{:S(2)}) %all-to-all-start) | async-done | bytes 1310752 | tf_op jit(solution)/shard_map/all_to_all | solution.py:370
  74.1 3.5 %shard_map.63 = f32[256,2,1152]{2,1,0:T(2,128)} custom-call(s16[128,40,128]{2,1,0:T(8,128)(2,1)S(1)} %all-to-all-done.in_ref), custom_call_target="tpu_custom_call" | custom-call | tf_op jit(solution)/shard_map/pallas_call | solution.py:373
  (18 shorter events, 0.1 us)
Async XLA Ops:
  0.6 1.2 %copy-start.2 = (bf16[1,1,64,8,8,128]{5,4,3,2,1,0:T(8,128)(2,1)S(1)}, bf16[1,1,64,8,8,128]{5,4,3,2,1,0:T(8,128)(2,1)}, u32[]{:S(2)}) copy-start(bf16[1,1,64,8,8,128]{5,4,3,2,1,0:T(8,128)(2,1)} %param.5) | copy-start | bytes 3145732
  1.9 0.7 copy-start.4
  2.6 9.7 %copy-start.3 = (bf16[256,1152]{1,0:T(8,128)(2,1)S(1)}, bf16[256,1152]{1,0:T(8,128)(2,1)}, u32[]{:S(2)}) copy-start(bf16[256,1152]{1,0:T(8,128)(2,1)} %k_ref) | copy-start | bytes 1769476
  3.0 10.2 %copy-start = (bf16[33,64,128]{2,1,0:T(8,128)(2,1)}, bf16[33,64,128]{2,1,0:T(8,128)(2,1)S(1)}, u32[]{:S(2)}) copy-start(bf16[33,64,128]{2,1,0:T(8,128)(2,1)S(1)} %get-tuple-element.9.x0_ref.refs_0_) | copy-start | bytes 1622020
  3.0 10.2 %copy-start.1 = (bf16[33,64,128]{2,1,0:T(8,128)(2,1)}, bf16[33,64,128]{2,1,0:T(8,128)(2,1)S(1)}, u32[]{:S(2)}) copy-start(bf16[33,64,128]{2,1,0:T(8,128)(2,1)S(1)} %get-tuple-element.10.x1_ref.refs_1_) | copy-start | bytes 1622020
  3.0 19.7 %collective-permute-start.1 = (bf16[33,64,128]{2,1,0:T(8,128)(2,1)S(1)}, bf16[33,64,128]{2,1,0:T(8,128)(2,1)S(1)}, u32[]{:S(2)}, u32[]{:S(2)}) collective-permute-start(bf16[33,64,128]{2,1,0:T(8,128)(2,1)S(1)} %get-tuple-element.9.x0_ref.refs_0_), channel_id=1, source_target_pairs={{0,120},{8,0},{16,8},{24,16},{32,24},{40,32},{48,40},{56,48},{64,5... | collective-permute-start | bytes 1622024 | tf_op jit(solution)/shard_map/ppermute | solution.py:23
  10.1 16.1 %collective-permute-start = (bf16[33,64,128]{2,1,0:T(8,128)(2,1)S(1)}, bf16[33,64,128]{2,1,0:T(8,128)(2,1)S(1)}, u32[]{:S(2)}, u32[]{:S(2)}) collective-permute-start(bf16[33,64,128]{2,1,0:T(8,128)(2,1)S(1)} %get-tuple-element.10.x1_ref.refs_1_), channel_id=1, source_target_pairs={{0,8},{8,16},{16,24},{24,32},{32,40},{40,48},{48,56},{56,64},{64,7... | collective-permute-start | bytes 1622024 | tf_op jit(solution)/shard_map/ppermute | solution.py:23
  10.2 19.7 %collective-permute-start.3 = (bf16[33,64,128]{2,1,0:T(8,128)(2,1)S(1)}, bf16[33,64,128]{2,1,0:T(8,128)(2,1)}, u32[]{:S(2)}, u32[]{:S(2)}) collective-permute-start(bf16[33,64,128]{2,1,0:T(8,128)(2,1)S(1)} %get-tuple-element.11), channel_id=1, source_target_pairs={{0,7},{1,0},{2,1},{3,2},{4,3},{5,4},{6,5},{7,6},{8,15},{9,8},{10,9... | collective-permute-start | bytes 1622024 | tf_op jit(solution)/shard_map/ppermute | solution.py:23
  11.2 20.5 %collective-permute-start.2 = (bf16[33,64,128]{2,1,0:T(8,128)(2,1)S(1)}, bf16[33,64,128]{2,1,0:T(8,128)(2,1)}, u32[]{:S(2)}, u32[]{:S(2)}) collective-permute-start(bf16[33,64,128]{2,1,0:T(8,128)(2,1)S(1)} %get-tuple-element.12), channel_id=1, source_target_pairs={{0,1},{1,2},{2,3},{3,4},{4,5},{5,6},{6,7},{7,0},{8,9},{9,10},{10,1... | collective-permute-start | bytes 1622024 | tf_op jit(solution)/shard_map/ppermute | solution.py:23
  13.2 30.8 %all-to-all-start.1 = ((bf16[128,2,1152]{2,1,0:T(2,128)(2,1)}), bf16[128,2,1152]{2,1,0:T(2,128)(2,1)}, u32[]{:S(2)}, u32[]{:S(2)}) async-start(bf16[128,2,1152]{2,1,0:T(2,128)(2,1)} %shard_map.61), calls=%async_computation.1 | async-start | bytes 1179648 | tf_op jit(solution)/shard_map/all_to_all | solution.py:342
  22.8 14.7 %copy-start.5 = (bf16[33,64,128]{2,1,0:T(8,128)(2,1)}, bf16[33,64,128]{2,1,0:T(8,128)(2,1)S(1)}, u32[]{:S(2)}) copy-start(bf16[33,64,128]{2,1,0:T(8,128)(2,1)S(1)} %collective-permute-done.1.refs_3_) | copy-start | bytes 1622020
  26.3 11.2 %copy-start.6 = (bf16[33,64,128]{2,1,0:T(8,128)(2,1)}, bf16[33,64,128]{2,1,0:T(8,128)(2,1)S(1)}, u32[]{:S(2)}) copy-start(bf16[33,64,128]{2,1,0:T(8,128)(2,1)S(1)} %collective-permute-done.refs_2_) | copy-start | bytes 1622020
  26.3 8.1 %collective-permute-start.5 = (bf16[17,64,128]{2,1,0:T(8,128)(2,1)S(1)}, bf16[17,64,128]{2,1,0:T(8,128)(2,1)S(1)}, u32[]{:S(2)}, u32[]{:S(2)}) collective-permute-start(bf16[17,64,128]{2,1,0:T(8,128)(2,1)S(1)} %get-tuple-element.18), channel_id=1, source_target_pairs={{0,7},{1,0},{2,1},{3,2},{4,3},{5,4},{6,5},{7,6},{8,15},{9,8},{10,9... | collective-permute-start | bytes 835592 | tf_op jit(solution)/shard_map/ppermute | solution.py:23
  28.6 5.8 %collective-permute-start.4 = (bf16[17,64,128]{2,1,0:T(8,128)(2,1)S(1)}, bf16[17,64,128]{2,1,0:T(8,128)(2,1)S(1)}, u32[]{:S(2)}, u32[]{:S(2)}) collective-permute-start(bf16[17,64,128]{2,1,0:T(8,128)(2,1)S(1)} %get-tuple-element.19), channel_id=1, source_target_pairs={{0,1},{1,2},{2,3},{3,4},{4,5},{5,6},{6,7},{7,0},{8,9},{9,10},{10,1... | collective-permute-start | bytes 835592 | tf_op jit(solution)/shard_map/ppermute | solution.py:23
  29.9 7.5 %collective-permute-start.7 = (bf16[17,64,128]{2,1,0:T(8,128)(2,1)S(1)}, bf16[17,64,128]{2,1,0:T(8,128)(2,1)S(1)}, u32[]{:S(2)}, u32[]{:S(2)}) collective-permute-start(bf16[17,64,128]{2,1,0:T(8,128)(2,1)S(1)} %get-tuple-element.16), channel_id=1, source_target_pairs={{0,7},{1,0},{2,1},{3,2},{4,3},{5,4},{6,5},{7,6},{8,15},{9,8},{10,9... | collective-permute-start | bytes 835592 | tf_op jit(solution)/shard_map/ppermute | solution.py:23
  29.9 7.5 %collective-permute-start.6 = (bf16[17,64,128]{2,1,0:T(8,128)(2,1)S(1)}, bf16[17,64,128]{2,1,0:T(8,128)(2,1)S(1)}, u32[]{:S(2)}, u32[]{:S(2)}) collective-permute-start(bf16[17,64,128]{2,1,0:T(8,128)(2,1)S(1)} %get-tuple-element.17), channel_id=1, source_target_pairs={{0,1},{1,2},{2,3},{3,4},{4,5},{5,6},{6,7},{7,0},{8,9},{9,10},{10,1... | collective-permute-start | bytes 835592 | tf_op jit(solution)/shard_map/ppermute | solution.py:23
  34.5 3.0 %copy-start.7 = (bf16[17,64,128]{2,1,0:T(8,128)(2,1)}, bf16[17,64,128]{2,1,0:T(8,128)(2,1)S(1)}, u32[]{:S(2)}) copy-start(bf16[17,64,128]{2,1,0:T(8,128)(2,1)S(1)} %collective-permute-done.5.refs_7_) | copy-start | bytes 835588
  34.5 3.0 %copy-start.8 = (bf16[17,64,128]{2,1,0:T(8,128)(2,1)}, bf16[17,64,128]{2,1,0:T(8,128)(2,1)S(1)}, u32[]{:S(2)}) copy-start(bf16[17,64,128]{2,1,0:T(8,128)(2,1)S(1)} %collective-permute-done.4.refs_6_) | copy-start | bytes 835588
  37.4 0.7 copy-start.9
  37.5 0.8 %copy-start.10 = (bf16[17,64,128]{2,1,0:T(8,128)(2,1)}, bf16[17,64,128]{2,1,0:T(8,128)(2,1)S(1)}, u32[]{:S(2)}) copy-start(bf16[17,64,128]{2,1,0:T(8,128)(2,1)S(1)} %collective-permute-done.6.refs_8_) | copy-start | bytes 835588
  44.0 30.1 %all-to-all-start = ((s16[128,40,128]{2,1,0:T(8,128)(2,1)}), s16[128,40,128]{2,1,0:T(8,128)(2,1)S(1)}, u32[]{:S(2)}, u32[]{:S(2)}) async-start(s16[128,40,128]{2,1,0:T(8,128)(2,1)} %shard_map.62), calls=%async_computation | async-start | bytes 2621440 | tf_op jit(solution)/shard_map/all_to_all | solution.py:370

commit v3 on v2

--- a/solution.py
+++ b/solution.py
@@ -5,6 +5,7 @@
 from jax import lax
 from jax.experimental import pallas as pl
 from jax.experimental.pallas import tpu as pltpu
+from jax.sharding import Mesh
 from jax.sharding import PartitionSpec as P
 
 AT_X = {1: 1, 0: 2}
@@ -16,6 +17,19 @@
 SMALLEST = 1e-33
 VMEM = pl.BlockSpec(memory_space=pltpu.VMEM)
 SMEM = pl.BlockSpec(memory_space=pltpu.SMEM)
+
+
+BRICK, NARROW = ("z", "y"), ("x", "core")
+ORDER = ("core", "x", "y", "z")
+
+
+def place(device, sizes):
+    z_bits, y_bits, x_bits, core_bits = (size.bit_length() - 1 for size in sizes)
+    core = device & (sizes[3] - 1)
+    x = (device >> core_bits) & (sizes[2] - 1)
+    y = (device >> (core_bits + x_bits)) & (sizes[1] - 1)
+    z = device >> (core_bits + x_bits + y_bits)
+    return (((((core << x_bits) + x) << y_bits) + y) << z_bits) + z
 
 
 def shifted(shard, axis, by):
@@ -120,8 +134,14 @@
         return self.edge_row((side_x, side_y), near_x * inner + column)
 
 
-def pair_kernel(k_ref, o_ref):
-    o_ref[...] = k_ref[...].reshape(o_ref.shape)
+def pair_kernel(sizes, k_ref, o_ref):
+    z_size, y_size, x_size, core_size = sizes
+    rows = k_ref[...].reshape(*sizes, *o_ref.shape[1:])
+    for core in range(core_size):
+        for x in range(x_size):
+            for y in range(y_size):
+                at = ((core * x_size + x) * y_size + y) * z_size
+                o_ref[at : at + z_size] = rows[:, y, x, core]
 
 
 def stencil(cell, potential_row, half, x, y, zero_low, zero_high):
@@ -140,7 +160,7 @@
     return lane == 0, lane == depth - 1
 
 
-def ranks(owner_ref, count_ref):
+def ranks(owner_ref, count_ref, sizes):
     def clear(i, carry):
         count_ref[owner_ref[i]] = 0
         return carry
@@ -151,11 +171,11 @@
         owner = owner_ref[a]
         rank = count_ref[owner]
         count_ref[owner] = rank + 1
-        found.append((owner, rank))
+        found.append((place(owner, sizes), rank))
     return found
 
 
-def pairs_kernel(half, cap, owner_ref, pot_ref, *refs):
+def pairs_kernel(half, cap, sizes, owner_ref, pot_ref, *refs):
     out_ref, wide_ref, sums_ref, count_ref = refs[10:14]
     boxes = Boxes(half, refs[0:10], pot_ref)
     func_count, depth = refs[0].shape[-2:]
@@ -219,7 +239,7 @@
         power = jnp.ceil(STEPS * jnp.log2(largest))
         coded.append((row * (TOP * jnp.exp2(-power / STEPS)), jnp.broadcast_to(power, (atoms, depth))))
     tiles = 2 * width // depth
-    for a, (owner, rank) in enumerate(ranks(owner_ref, count_ref)):
+    for a, (owner, rank) in enumerate(ranks(owner_ref, count_ref, sizes)):
         for m, (row, power) in enumerate(coded):
             for t in range(tiles):
                 wide_ref[owner, pl.ds(rank * (2 * tiles) + 2 * t + m, 1), :] = row[
@@ -230,13 +250,15 @@
         out_ref[owner] = jnp.round(wide_ref[owner]).astype(jnp.int32).astype(jnp.int16)
 
 
-def unpack_kernel(cap, in_ref, out_ref):
-    chunks, rows, depth = in_ref.shape
+def unpack_kernel(cap, sizes, in_ref, out_ref):
+    chunks = out_ref.shape[0] // cap
+    _, rows, depth = in_ref.shape
     data = rows - 2 * cap
     line = lax.broadcasted_iota(jnp.int32, (data, depth), 0)
     even = line % 2 == 0
     for c in range(chunks):
-        values = in_ref[c].astype(jnp.int32).astype(jnp.float32)
+        at = place(c, sizes) + pl.program_id(0) * (chunks * sizes[0] // in_ref.shape[0])
+        values = in_ref[at].astype(jnp.int32).astype(jnp.float32)
         scale = jnp.exp2(values[data:] * (1.0 / STEPS)) * (1.0 / TOP)
         spread = jnp.where(even, scale[0:1], scale[1:2])
         for rank in range(1, cap):
@@ -252,7 +274,7 @@
                 out_ref[c * cap + rank, :, t * depth : (t + 1) * depth] = values[start : start + 2]
 
 
-def mix_kernel(half, owner_ref, kernel_ref, pot_ref, *refs):
+def mix_kernel(half, sizes, owner_ref, kernel_ref, pot_ref, *refs):
     out_ref, rows_ref, mixed_ref, count_ref, sems = refs[10:15]
     held = refs[15:25]
     copies = [pltpu.make_async_copy(refs[i], held[i], sems.at[i]) for i in range(10)]
@@ -262,7 +284,7 @@
     func_count, depth = refs[0].shape[-2:]
     atoms = owner_ref.shape[0]
     low_edge, high_edge = edges(func_count, depth)
-    for a, (owner, rank) in enumerate(ranks(owner_ref, count_ref)):
+    for a, (owner, rank) in enumerate(ranks(owner_ref, count_ref, sizes)):
         both = kernel_ref[owner].astype(jnp.float32)
         rows_ref[a : a + 1, :] = jnp.where(rank == 0, both[0:1], both[1:2])
     width = 9 * func_count
@@ -301,12 +323,12 @@
             out_ref[:, odd, x] = jnp.swapaxes(stacked, 0, 1).astype(out_ref.dtype)
 
 
-def body(potential, functions, kernel_store, owners):
+def body(sizes, potential, functions, kernel_store, owners):
     own_funcs = functions[0, 0]
     func_count, ext_x, ext_y, depth = own_funcs.shape
     half = ext_x // 2
     margin = (ext_x - potential.shape[0]) // 2
-    device_count = lax.axis_size("brick") * lax.axis_size("narrow")
+    device_count = sizes[0] * sizes[1] * sizes[2] * sizes[3]
     owner_col = owners[:, 0]
     atoms = owner_col.shape[0]
     slot_count, row_width = kernel_store.shape
@@ -327,12 +349,12 @@
         )(*operands)
 
     own_x = split(split_x_kernel, own_funcs, potential)
-    from_x = (shifted(own_x[1], "brick", 1), shifted(own_x[0], "brick", -1))
+    from_x = (shifted(own_x[1], BRICK, 1), shifted(own_x[0], BRICK, -1))
     own_y = split(split_y_kernel, *own_x, potential)
-    from_y = (shifted(own_y[1], "narrow", 1), shifted(own_y[0], "narrow", -1))
+    from_y = (shifted(own_y[1], NARROW, 1), shifted(own_y[0], NARROW, -1))
     kernel_store, *_ = lax.optimization_barrier((kernel_store, *own_y))
     kernel_out = pl.pallas_call(
-        pair_kernel,
+        functools.partial(pair_kernel, sizes),
         out_shape=struct((device_count, slot_cap, row_width), bf16),
         in_specs=[VMEM],
         out_specs=VMEM,
@@ -340,20 +362,20 @@
         cost_estimate=pl.CostEstimate(flops=0, transcendentals=0, bytes_accessed=1 << 20),
     )(kernel_store)
     kernel_in = lax.all_to_all(
-        kernel_out, ("brick", "narrow"), split_axis=0, concat_axis=0, tiled=True
+        kernel_out, ORDER, split_axis=0, concat_axis=0, tiled=True
     )
 
     count = half * half
     bands = lax.optimization_barrier((*from_x, *own_y, kernel_out))[:2]
     corners = [bands[sx][: count + 1] if sy else bands[sx][count:] for sx, sy in SIDES]
-    from_xy = [shifted(c, "narrow", -1 if sy else 1) for c, (sx, sy) in zip(corners, SIDES)]
+    from_xy = [shifted(c, NARROW, -1 if sy else 1) for c, (sx, sy) in zip(corners, SIDES)]
 
     boxes = (*own_x, *bands, *from_y, *from_xy)
     anywhere = pl.BlockSpec(memory_space=pltpu.HBM)
     cells = ext_x * ext_y * depth
     lines = 2 * slot_cap * (row_width // depth + 1)
     outgoing = pl.pallas_call(
-        functools.partial(pairs_kernel, half, slot_cap),
+        functools.partial(pairs_kernel, half, slot_cap, sizes),
         out_shape=struct((device_count, lines, depth), jnp.int16),
         in_specs=[SMEM] + [VMEM] * 11,
         out_specs=VMEM,
@@ -367,20 +389,20 @@
             flops=16 * func_count * func_count * cells, transcendentals=0, bytes_accessed=7 << 20
         ),
     )(owner_col, potential, *boxes)
-    blocks = lax.all_to_all(outgoing, ("brick", "narrow"), split_axis=0, concat_axis=0, tiled=True)
-    steps = 8
+    blocks = lax.all_to_all(outgoing, ORDER, split_axis=0, concat_axis=0, tiled=True)
+    steps = 2
     chunk = device_count // steps
     blocks = pl.pallas_call(
-        functools.partial(unpack_kernel, slot_cap),
+        functools.partial(unpack_kernel, slot_cap, sizes),
         grid=(steps,),
         out_shape=struct((slot_count, 2, row_width), jnp.float32),
-        in_specs=[pl.BlockSpec((chunk, lines, depth), lambda i: (i, 0, 0))],
+        in_specs=[VMEM],
         out_specs=pl.BlockSpec((chunk * slot_cap, 2, row_width), lambda i: (i, 0, 0)),
         compiler_params=params(),
     )(blocks)
 
     gradient = pl.pallas_call(
-        functools.partial(mix_kernel, half),
+        functools.partial(mix_kernel, half, sizes),
         out_shape=struct((atoms, 2, ext_x, ext_y, depth), bf16),
         in_specs=[SMEM, VMEM, VMEM] + [anywhere] * 10,
         out_specs=VMEM,
@@ -400,11 +422,11 @@
 
 
 def solution(mesh):
-    in_specs = (
-        P("brick", "narrow", None),
-        P("brick", "narrow", None, None, None, None),
-        P(("brick", "narrow"), None),
-        P(("brick", "narrow"), None),
+    sizes = (mesh.shape["brick"] // 4, 4, mesh.shape["narrow"] // 2, 2)
+    mesh = Mesh(mesh.devices.reshape(sizes), BRICK + NARROW)
+    every = BRICK + NARROW
+    in_specs = (P(BRICK, NARROW, None), P(BRICK, NARROW, None, None, None, None), P(every, None), P(every, None))
+    out_specs = (P(every, None, None), P(BRICK, NARROW, None, None, None, None))
+    return jax.shard_map(
+        functools.partial(body, sizes), mesh=mesh, in_specs=in_specs, out_specs=out_specs, check_vma=False
     )
-    out_specs = (P(("brick", "narrow"), None, None), P("brick", "narrow", None, None, None, None))
-    return jax.shard_map(body, mesh=mesh, in_specs=in_specs, out_specs=out_specs, check_vma=False)

time: 77.9 us -> 74.5 us (0.956)
  waiting for transfers between devices: 25.3 us -> 23.2 us
  Pallas kernels: 16.8 us -> 15.4 us
    all_to_all x2, waiting for transfers between devices: 16.1 us -> 14 us  [the longest x1 14 us: body(): lax.all_to_all(outgoing, ORDER, split_axis=0, concat_axis=0, tiled=True)]
    pallas_call x4, Pallas kernels: 16.2 us -> 14.9 us  [the longest x1 6.09 us: body(): pl.pallas_call(functools.partial(mix_kernel, half, sizes), out_shape=stru...]
  transfers between devices with their start and end apart: 10 -> 10, of which waited for: 4 -> 4; matrix products, arithmetic and copies ran while one was open for 0% -> 0% of each run, Pallas kernels for 17% -> 18%
where the time goes in v3:
time: 74.5 us; the launch traced here: 74.1 us
  starting transfers between devices  32 us (43%)
  waiting for transfers between devices  23.2 us (31%)
  Pallas kernels  15.4 us (21%)
  local copies, waits for them, and re-layouts  2.8 us (4%)
  between operations  0.77 us (1%)
    ppermute x8, starting transfers between devices, shifted(): lax.ppermute(shard, axis, [(i, (i + by) % size) for i in range(size)])  14.6 us
    all_to_all x1, waiting for transfers between devices, body(): lax.all_to_all(outgoing, ORDER, split_axis=0, concat_axis=0, tiled=True)  14 us
    all_to_all x1, starting transfers between devices, body(): lax.all_to_all(kernel_out, ORDER, split_axis=0, concat_axis=0, tiled=True)  9.52 us
    ppermute x8, waiting for transfers between devices, shifted(): lax.ppermute(shard, axis, [(i, (i + by) % size) for i in range(size)])  9.16 us
    all_to_all x1, starting transfers between devices, body(): lax.all_to_all(outgoing, ORDER, split_axis=0, concat_axis=0, tiled=True)  7.86 us
    pallas_call x1, Pallas kernels, body(): pl.pallas_call(functools.partial(mix_kernel, half, sizes), out_shape=stru...  6.09 us
    pallas_call x1, Pallas kernels, body(): pl.pallas_call(functools.partial(pairs_kernel, half, slot_cap, sizes), ou...  5.9 us
    unnamed x22, local copies, waits for them, and re-layouts  2.71 us
  transfers between devices with their start and end apart: 10, of which 4 were waited for; matrix products, arithmetic and copies ran while one was open for 0% of the time, Pallas kernels for 18%

profile of v3, /device:TPU:1, one launch (start us, length us, event | category | flops | bytes accessed | tf_op | source)
XLA Modules:
  0.0 74.1 jit_solution(7126742496780403563)
XLA Ops:
  0.6 0.0 copy-start.2
  0.6 1.2 %copy-done.2 = bf16[1,1,64,8,8,128]{5,4,3,2,1,0:T(8,128)(2,1)S(1)} copy-done((bf16[1,1,64,8,8,128]{5,4,3,2,1,0:T(8,128)(2,1)S(1)}, bf16[1,1,64,8,8,128]{5,4,3,2,1,0:T(8,128)(2,1)}, u32[]{:S(2)}) %copy-start.2) | copy-done | bytes 1048600
  1.9 0.7 copy-done.4
  2.6 0.4 shard_map.59
  3.0 7.1 %collective-permute-start.1 = (bf16[33,64,128]{2,1,0:T(8,128)(2,1)S(1)}, bf16[33,64,128]{2,1,0:T(8,128)(2,1)S(1)}, u32[]{:S(2)}, u32[]{:S(2)}) collective-permute-start(bf16[33,64,128]{2,1,0:T(8,128)(2,1)S(1)} %get-tuple-element.9.x0_ref.refs_0_), channel_id=1, source_target_pairs={{0,120},{8,0},{16,8},{24,16},{32,24},{40,32},{48,40},{56,48},{64,5... | collective-permute-start | bytes 1622024 | tf_op jit(solution)/shard_map/ppermute | solution.py:37
  10.1 0.0 collective-permute-start
  10.1 0.1 shard_map.60
  10.2 1.0 %collective-permute-start.3 = (bf16[33,64,128]{2,1,0:T(8,128)(2,1)S(1)}, bf16[33,64,128]{2,1,0:T(8,128)(2,1)}, u32[]{:S(2)}, u32[]{:S(2)}) collective-permute-start(bf16[33,64,128]{2,1,0:T(8,128)(2,1)S(1)} %get-tuple-element.11), channel_id=1, source_target_pairs={{0,7},{1,0},{2,1},{3,2},{4,3},{5,4},{6,5},{7,6},{8,15},{9,8},{10,9... | collective-permute-start | bytes 1622024 | tf_op jit(solution)/shard_map/ppermute | solution.py:37
  11.2 1.1 %collective-permute-start.2 = (bf16[33,64,128]{2,1,0:T(8,128)(2,1)S(1)}, bf16[33,64,128]{2,1,0:T(8,128)(2,1)}, u32[]{:S(2)}, u32[]{:S(2)}) collective-permute-start(bf16[33,64,128]{2,1,0:T(8,128)(2,1)S(1)} %get-tuple-element.12), channel_id=1, source_target_pairs={{0,1},{1,2},{2,3},{3,4},{4,5},{5,6},{6,7},{7,0},{8,9},{9,10},{10,1... | collective-permute-start | bytes 1622024 | tf_op jit(solution)/shard_map/ppermute | solution.py:37
  12.3 0.9 %shard_map.61 = bf16[128,2,1152]{2,1,0:T(2,128)(2,1)} custom-call(bf16[256,1152]{1,0:T(8,128)(2,1)S(1)} %copy-done.3), custom_call_target="tpu_custom_call" | custom-call | bytes 1048576 | tf_op jit(solution)/shard_map/pallas_call | solution.py:356
  13.2 0.0 copy-done.1
  13.2 9.5 %all-to-all-start.1 = ((bf16[128,2,1152]{2,1,0:T(2,128)(2,1)}), bf16[128,2,1152]{2,1,0:T(2,128)(2,1)}, u32[]{:S(2)}, u32[]{:S(2)}) async-start(bf16[128,2,1152]{2,1,0:T(2,128)(2,1)} %shard_map.61), calls=%async_computation.1 | async-start | bytes 1179648 | tf_op jit(solution)/shard_map/all_to_all | solution.py:364
  22.8 0.0 collective-permute-done.1.refs_3_
  22.8 3.5 %collective-permute-done.refs_2_ = bf16[33,64,128]{2,1,0:T(8,128)(2,1)S(1)} collective-permute-done((bf16[33,64,128]{2,1,0:T(8,128)(2,1)S(1)}, bf16[33,64,128]{2,1,0:T(8,128)(2,1)S(1)}, u32[]{:S(2)}, u32[]{:S(2)}) %collective-permute-start) | collective-permute-done | bytes 540704 | tf_op jit(solution)/shard_map/ppermute | solution.py:37
  26.3 2.4 %collective-permute-start.5 = (bf16[17,64,128]{2,1,0:T(8,128)(2,1)S(1)}, bf16[17,64,128]{2,1,0:T(8,128)(2,1)S(1)}, u32[]{:S(2)}, u32[]{:S(2)}) collective-permute-start(bf16[17,64,128]{2,1,0:T(8,128)(2,1)S(1)} %get-tuple-element.18), channel_id=1, source_target_pairs={{0,7},{1,0},{2,1},{3,2},{4,3},{5,4},{6,5},{7,6},{8,15},{9,8},{10,9... | collective-permute-start | bytes 835592 | tf_op jit(solution)/shard_map/ppermute | solution.py:37
  28.7 1.3 %collective-permute-start.4 = (bf16[17,64,128]{2,1,0:T(8,128)(2,1)S(1)}, bf16[17,64,128]{2,1,0:T(8,128)(2,1)S(1)}, u32[]{:S(2)}, u32[]{:S(2)}) collective-permute-start(bf16[17,64,128]{2,1,0:T(8,128)(2,1)S(1)} %get-tuple-element.19), channel_id=1, source_target_pairs={{0,1},{1,2},{2,3},{3,4},{4,5},{5,6},{6,7},{7,0},{8,9},{9,10},{10,1... | collective-permute-start | bytes 835592 | tf_op jit(solution)/shard_map/ppermute | solution.py:37
  30.1 0.0 collective-permute-start.7
  30.1 0.0 collective-permute-done.3.refs_5_
  30.1 1.7 %collective-permute-start.6 = (bf16[17,64,128]{2,1,0:T(8,128)(2,1)S(1)}, bf16[17,64,128]{2,1,0:T(8,128)(2,1)S(1)}, u32[]{:S(2)}, u32[]{:S(2)}) collective-permute-start(bf16[17,64,128]{2,1,0:T(8,128)(2,1)S(1)} %get-tuple-element.17), channel_id=1, source_target_pairs={{0,1},{1,2},{2,3},{3,4},{4,5},{5,6},{6,7},{7,0},{8,9},{9,10},{10,1... | collective-permute-start | bytes 835592 | tf_op jit(solution)/shard_map/ppermute | solution.py:37
  31.8 0.0 collective-permute-done.2.refs_4_
  31.8 2.8 %collective-permute-done.5.refs_7_ = bf16[17,64,128]{2,1,0:T(8,128)(2,1)S(1)} collective-permute-done((bf16[17,64,128]{2,1,0:T(8,128)(2,1)S(1)}, bf16[17,64,128]{2,1,0:T(8,128)(2,1)S(1)}, u32[]{:S(2)}, u32[]{:S(2)}) %collective-permute-start.5) | collective-permute-done | bytes 278560 | tf_op jit(solution)/shard_map/ppermute | solution.py:37
  34.6 0.0 collective-permute-done.4.refs_6_
  34.6 2.9 %collective-permute-done.7.refs_9_ = bf16[17,64,128]{2,1,0:T(8,128)(2,1)S(1)} collective-permute-done((bf16[17,64,128]{2,1,0:T(8,128)(2,1)S(1)}, bf16[17,64,128]{2,1,0:T(8,128)(2,1)S(1)}, u32[]{:S(2)}, u32[]{:S(2)}) %collective-permute-start.7) | collective-permute-done | bytes 278560 | tf_op jit(solution)/shard_map/ppermute | solution.py:37
  37.5 0.0 collective-permute-done.6.refs_8_
  37.5 0.7 copy-done.9
  38.2 0.1 copy-done.10
  38.3 5.9 %shard_map.62 = s16[128,40,128]{2,1,0:T(8,128)(2,1)} custom-call(s32[32]{0:T(128)} %bitcast.5, f32[4,4,128]{2,1,0:T(4,128)} %pot_ref.7, bf16[33,64,128]{2,1,0:T(8,128)(2,1)} %copy-done, bf16[33,64,128]{2,1,0:T(8,128)(2,1)} %copy-done.1, bf16[33,64,128]{2,1,0:T(8,128)(2,1)} %copy-done.6, bf16[33,64,128]{2,1,0:T(8,128)(2,1)} %copy-done.5, ...), custom_call_target="tpu_custom_call" | custom-call | flops 536870912 | bytes 7340032 | tf_op jit(solution)/shard_map/pallas_call | solution.py:377
  44.2 0.0 all-to-all-done.1.kernel_ref
  44.2 7.9 %all-to-all-start = ((s16[128,40,128]{2,1,0:T(8,128)(2,1)}), s16[128,40,128]{2,1,0:T(8,128)(2,1)S(1)}, u32[]{:S(2)}, u32[]{:S(2)}) async-start(s16[128,40,128]{2,1,0:T(8,128)(2,1)} %shard_map.62), calls=%async_computation | async-start | bytes 2621440 | tf_op jit(solution)/shard_map/all_to_all | solution.py:392
  52.1 6.1 %shard_map.64 = bf16[32,2,8,8,128]{4,3,2,1,0:T(8,128)(2,1)} custom-call(s32[32]{0:T(128)} %bitcast.6, bf16[128,2,1152]{2,1,0:T(2,128)(2,1)} %all-to-all-done.1.kernel_ref, f32[4,4,128]{2,1,0:T(4,128)} %pot_ref.7, bf16[33,64,128]{2,1,0:T(8,128)(2,1)} %copy-done, bf16[33,64,128]{2,1,0:T(8,128)(2,1)} %copy-done.1, bf16[33,64,128]{2,1,0:T(8,128)(2,1)} %copy-done.6, ...), custom_call_target="tpu_custom_call" | custom-call | flops 268435456 | bytes 7340032 | tf_op jit(solution)/shard_map/pallas_call | solution.py:404
  58.2 14.0 %all-to-all-done.in_ref = s16[128,40,128]{2,1,0:T(8,128)(2,1)S(1)} async-done(((s16[128,40,128]{2,1,0:T(8,128)(2,1)}), s16[128,40,128]{2,1,0:T(8,128)(2,1)S(1)}, u32[]{:S(2)}, u32[]{:S(2)}) %all-to-all-start) | async-done | bytes 1310752 | tf_op jit(solution)/shard_map/all_to_all | solution.py:392
  72.2 2.0 %shard_map.63 = f32[256,2,1152]{2,1,0:T(2,128)} custom-call(s16[128,40,128]{2,1,0:T(8,128)(2,1)S(1)} %all-to-all-done.in_ref), custom_call_target="tpu_custom_call" | custom-call | tf_op jit(solution)/shard_map/pallas_call | solution.py:395
  (18 shorter events, 0.1 us)
Async XLA Ops:
  0.6 1.2 %copy-start.2 = (bf16[1,1,64,8,8,128]{5,4,3,2,1,0:T(8,128)(2,1)S(1)}, bf16[1,1,64,8,8,128]{5,4,3,2,1,0:T(8,128)(2,1)}, u32[]{:S(2)}) copy-start(bf16[1,1,64,8,8,128]{5,4,3,2,1,0:T(8,128)(2,1)} %param.5) | copy-start | bytes 3145732
  1.9 0.7 copy-start.4
  2.6 9.7 %copy-start.3 = (bf16[256,1152]{1,0:T(8,128)(2,1)S(1)}, bf16[256,1152]{1,0:T(8,128)(2,1)}, u32[]{:S(2)}) copy-start(bf16[256,1152]{1,0:T(8,128)(2,1)} %k_ref) | copy-start | bytes 1769476
  3.0 10.2 %copy-start = (bf16[33,64,128]{2,1,0:T(8,128)(2,1)}, bf16[33,64,128]{2,1,0:T(8,128)(2,1)S(1)}, u32[]{:S(2)}) copy-start(bf16[33,64,128]{2,1,0:T(8,128)(2,1)S(1)} %get-tuple-element.9.x0_ref.refs_0_) | copy-start | bytes 1622020
  3.0 10.2 %copy-start.1 = (bf16[33,64,128]{2,1,0:T(8,128)(2,1)}, bf16[33,64,128]{2,1,0:T(8,128)(2,1)S(1)}, u32[]{:S(2)}) copy-start(bf16[33,64,128]{2,1,0:T(8,128)(2,1)S(1)} %get-tuple-element.10.x1_ref.refs_1_) | copy-start | bytes 1622020
  3.0 19.8 %collective-permute-start.1 = (bf16[33,64,128]{2,1,0:T(8,128)(2,1)S(1)}, bf16[33,64,128]{2,1,0:T(8,128)(2,1)S(1)}, u32[]{:S(2)}, u32[]{:S(2)}) collective-permute-start(bf16[33,64,128]{2,1,0:T(8,128)(2,1)S(1)} %get-tuple-element.9.x0_ref.refs_0_), channel_id=1, source_target_pairs={{0,120},{8,0},{16,8},{24,16},{32,24},{40,32},{48,40},{56,48},{64,5... | collective-permute-start | bytes 1622024 | tf_op jit(solution)/shard_map/ppermute | solution.py:37
  10.1 16.1 %collective-permute-start = (bf16[33,64,128]{2,1,0:T(8,128)(2,1)S(1)}, bf16[33,64,128]{2,1,0:T(8,128)(2,1)S(1)}, u32[]{:S(2)}, u32[]{:S(2)}) collective-permute-start(bf16[33,64,128]{2,1,0:T(8,128)(2,1)S(1)} %get-tuple-element.10.x1_ref.refs_1_), channel_id=1, source_target_pairs={{0,8},{8,16},{16,24},{24,32},{32,40},{40,48},{48,56},{56,64},{64,7... | collective-permute-start | bytes 1622024 | tf_op jit(solution)/shard_map/ppermute | solution.py:37
  10.2 19.9 %collective-permute-start.3 = (bf16[33,64,128]{2,1,0:T(8,128)(2,1)S(1)}, bf16[33,64,128]{2,1,0:T(8,128)(2,1)}, u32[]{:S(2)}, u32[]{:S(2)}) collective-permute-start(bf16[33,64,128]{2,1,0:T(8,128)(2,1)S(1)} %get-tuple-element.11), channel_id=1, source_target_pairs={{0,7},{1,0},{2,1},{3,2},{4,3},{5,4},{6,5},{7,6},{8,15},{9,8},{10,9... | collective-permute-start | bytes 1622024 | tf_op jit(solution)/shard_map/ppermute | solution.py:37
  11.2 20.7 %collective-permute-start.2 = (bf16[33,64,128]{2,1,0:T(8,128)(2,1)S(1)}, bf16[33,64,128]{2,1,0:T(8,128)(2,1)}, u32[]{:S(2)}, u32[]{:S(2)}) collective-permute-start(bf16[33,64,128]{2,1,0:T(8,128)(2,1)S(1)} %get-tuple-element.12), channel_id=1, source_target_pairs={{0,1},{1,2},{2,3},{3,4},{4,5},{5,6},{6,7},{7,0},{8,9},{9,10},{10,1... | collective-permute-start | bytes 1622024 | tf_op jit(solution)/shard_map/ppermute | solution.py:37
  13.2 31.0 %all-to-all-start.1 = ((bf16[128,2,1152]{2,1,0:T(2,128)(2,1)}), bf16[128,2,1152]{2,1,0:T(2,128)(2,1)}, u32[]{:S(2)}, u32[]{:S(2)}) async-start(bf16[128,2,1152]{2,1,0:T(2,128)(2,1)} %shard_map.61), calls=%async_computation.1 | async-start | bytes 1179648 | tf_op jit(solution)/shard_map/all_to_all | solution.py:364
  22.8 14.7 %copy-start.5 = (bf16[33,64,128]{2,1,0:T(8,128)(2,1)}, bf16[33,64,128]{2,1,0:T(8,128)(2,1)S(1)}, u32[]{:S(2)}) copy-start(bf16[33,64,128]{2,1,0:T(8,128)(2,1)S(1)} %collective-permute-done.1.refs_3_) | copy-start | bytes 1622020
  26.3 11.2 %copy-start.6 = (bf16[33,64,128]{2,1,0:T(8,128)(2,1)}, bf16[33,64,128]{2,1,0:T(8,128)(2,1)S(1)}, u32[]{:S(2)}) copy-start(bf16[33,64,128]{2,1,0:T(8,128)(2,1)S(1)} %collective-permute-done.refs_2_) | copy-start | bytes 1622020
  26.3 8.3 %collective-permute-start.5 = (bf16[17,64,128]{2,1,0:T(8,128)(2,1)S(1)}, bf16[17,64,128]{2,1,0:T(8,128)(2,1)S(1)}, u32[]{:S(2)}, u32[]{:S(2)}) collective-permute-start(bf16[17,64,128]{2,1,0:T(8,128)(2,1)S(1)} %get-tuple-element.18), channel_id=1, source_target_pairs={{0,7},{1,0},{2,1},{3,2},{4,3},{5,4},{6,5},{7,6},{8,15},{9,8},{10,9... | collective-permute-start | bytes 835592 | tf_op jit(solution)/shard_map/ppermute | solution.py:37
  28.7 5.9 %collective-permute-start.4 = (bf16[17,64,128]{2,1,0:T(8,128)(2,1)S(1)}, bf16[17,64,128]{2,1,0:T(8,128)(2,1)S(1)}, u32[]{:S(2)}, u32[]{:S(2)}) collective-permute-start(bf16[17,64,128]{2,1,0:T(8,128)(2,1)S(1)} %get-tuple-element.19), channel_id=1, source_target_pairs={{0,1},{1,2},{2,3},{3,4},{4,5},{5,6},{6,7},{7,0},{8,9},{9,10},{10,1... | collective-permute-start | bytes 835592 | tf_op jit(solution)/shard_map/ppermute | solution.py:37
  30.1 7.4 %collective-permute-start.7 = (bf16[17,64,128]{2,1,0:T(8,128)(2,1)S(1)}, bf16[17,64,128]{2,1,0:T(8,128)(2,1)S(1)}, u32[]{:S(2)}, u32[]{:S(2)}) collective-permute-start(bf16[17,64,128]{2,1,0:T(8,128)(2,1)S(1)} %get-tuple-element.16), channel_id=1, source_target_pairs={{0,7},{1,0},{2,1},{3,2},{4,3},{5,4},{6,5},{7,6},{8,15},{9,8},{10,9... | collective-permute-start | bytes 835592 | tf_op jit(solution)/shard_map/ppermute | solution.py:37
  30.1 7.4 %collective-permute-start.6 = (bf16[17,64,128]{2,1,0:T(8,128)(2,1)S(1)}, bf16[17,64,128]{2,1,0:T(8,128)(2,1)S(1)}, u32[]{:S(2)}, u32[]{:S(2)}) collective-permute-start(bf16[17,64,128]{2,1,0:T(8,128)(2,1)S(1)} %get-tuple-element.17), channel_id=1, source_target_pairs={{0,1},{1,2},{2,3},{3,4},{4,5},{5,6},{6,7},{7,0},{8,9},{9,10},{10,1... | collective-permute-start | bytes 835592 | tf_op jit(solution)/shard_map/ppermute | solution.py:37
  34.6 2.9 %copy-start.7 = (bf16[17,64,128]{2,1,0:T(8,128)(2,1)}, bf16[17,64,128]{2,1,0:T(8,128)(2,1)S(1)}, u32[]{:S(2)}) copy-start(bf16[17,64,128]{2,1,0:T(8,128)(2,1)S(1)} %collective-permute-done.5.refs_7_) | copy-start | bytes 835588
  34.6 2.9 %copy-start.8 = (bf16[17,64,128]{2,1,0:T(8,128)(2,1)}, bf16[17,64,128]{2,1,0:T(8,128)(2,1)S(1)}, u32[]{:S(2)}) copy-start(bf16[17,64,128]{2,1,0:T(8,128)(2,1)S(1)} %collective-permute-done.4.refs_6_) | copy-start | bytes 835588
  37.5 0.7 copy-start.9
  37.5 0.8 %copy-start.10 = (bf16[17,64,128]{2,1,0:T(8,128)(2,1)}, bf16[17,64,128]{2,1,0:T(8,128)(2,1)S(1)}, u32[]{:S(2)}) copy-start(bf16[17,64,128]{2,1,0:T(8,128)(2,1)S(1)} %collective-permute-done.6.refs_8_) | copy-start | bytes 835588
  44.2 28.0 %all-to-all-start = ((s16[128,40,128]{2,1,0:T(8,128)(2,1)}), s16[128,40,128]{2,1,0:T(8,128)(2,1)S(1)}, u32[]{:S(2)}, u32[]{:S(2)}) async-start(s16[128,40,128]{2,1,0:T(8,128)(2,1)} %shard_map.62), calls=%async_computation | async-start | bytes 2621440 | tf_op jit(solution)/shard_map/all_to_all | solution.py:392

commit v4 on v3

--- a/solution.py
+++ b/solution.py
@@ -21,6 +21,7 @@
 
 BRICK, NARROW = ("z", "y"), ("x", "core")
 ORDER = ("core", "x", "y", "z")
+ROWS_ORDER = ("y", "core", "x", "z")
 
 
 def place(device, sizes):
@@ -30,6 +31,15 @@
     y = (device >> (core_bits + x_bits)) & (sizes[1] - 1)
     z = device >> (core_bits + x_bits + y_bits)
     return (((((core << x_bits) + x) << y_bits) + y) << z_bits) + z
+
+
+def rows_place(device, sizes):
+    z_bits, y_bits, x_bits, core_bits = (size.bit_length() - 1 for size in sizes)
+    core = device & (sizes[3] - 1)
+    x = (device >> core_bits) & (sizes[2] - 1)
+    y = (device >> (core_bits + x_bits)) & (sizes[1] - 1)
+    z = device >> (core_bits + x_bits + y_bits)
+    return (((((y << core_bits) + core) << x_bits) + x) << z_bits) + z
 
 
 def shifted(shard, axis, by):
@@ -140,7 +150,7 @@
     for core in range(core_size):
         for x in range(x_size):
             for y in range(y_size):
-                at = ((core * x_size + x) * y_size + y) * z_size
+                at = ((y * core_size + core) * x_size + x) * z_size
                 o_ref[at : at + z_size] = rows[:, y, x, core]
 
 
@@ -160,7 +170,7 @@
     return lane == 0, lane == depth - 1
 
 
-def ranks(owner_ref, count_ref, sizes):
+def ranks(owner_ref, count_ref):
     def clear(i, carry):
         count_ref[owner_ref[i]] = 0
         return carry
@@ -171,7 +181,7 @@
         owner = owner_ref[a]
         rank = count_ref[owner]
         count_ref[owner] = rank + 1
-        found.append((place(owner, sizes), rank))
+        found.append((owner, rank))
     return found
 
 
@@ -239,13 +249,14 @@
         power = jnp.ceil(STEPS * jnp.log2(largest))
         coded.append((row * (TOP * jnp.exp2(-power / STEPS)), jnp.broadcast_to(power, (atoms, depth))))
     tiles = 2 * width // depth
-    for a, (owner, rank) in enumerate(ranks(owner_ref, count_ref, sizes)):
+    for a, (owner, rank) in enumerate(ranks(owner_ref, count_ref)):
+        at = place(owner, sizes)
         for m, (row, power) in enumerate(coded):
             for t in range(tiles):
-                wide_ref[owner, pl.ds(rank * (2 * tiles) + 2 * t + m, 1), :] = row[
+                wide_ref[at, pl.ds(rank * (2 * tiles) + 2 * t + m, 1), :] = row[
                     a : a + 1, t * depth : (t + 1) * depth
                 ]
-            wide_ref[owner, pl.ds(cap * 2 * tiles + 2 * rank + m, 1), :] = power[a : a + 1]
+            wide_ref[at, pl.ds(cap * 2 * tiles + 2 * rank + m, 1), :] = power[a : a + 1]
     for owner in range(out_ref.shape[0]):
         out_ref[owner] = jnp.round(wide_ref[owner]).astype(jnp.int32).astype(jnp.int16)
 
@@ -274,6 +285,12 @@
                 out_ref[c * cap + rank, :, t * depth : (t + 1) * depth] = values[start : start + 2]
 
 
+def keep_kernel(*refs):
+    number = len(refs) // 2
+    for given, kept in zip(refs[:number], refs[number:]):
+        kept[...] = given[...]
+
+
 def mix_kernel(half, sizes, owner_ref, kernel_ref, pot_ref, *refs):
     out_ref, rows_ref, mixed_ref, count_ref, sems = refs[10:15]
     held = refs[15:25]
@@ -284,8 +301,8 @@
     func_count, depth = refs[0].shape[-2:]
     atoms = owner_ref.shape[0]
     low_edge, high_edge = edges(func_count, depth)
-    for a, (owner, rank) in enumerate(ranks(owner_ref, count_ref, sizes)):
-        both = kernel_ref[owner].astype(jnp.float32)
+    for a, (owner, rank) in enumerate(ranks(owner_ref, count_ref)):
+        both = kernel_ref[rows_place(owner, sizes)].astype(jnp.float32)
         rows_ref[a : a + 1, :] = jnp.where(rank == 0, both[0:1], both[1:2])
     width = 9 * func_count
     matrix = jnp.concatenate([rows_ref[:, :width], rows_ref[:, width:]], axis=0)
@@ -362,7 +379,7 @@
         cost_estimate=pl.CostEstimate(flops=0, transcendentals=0, bytes_accessed=1 << 20),
     )(kernel_store)
     kernel_in = lax.all_to_all(
-        kernel_out, ORDER, split_axis=0, concat_axis=0, tiled=True
+        kernel_out, ROWS_ORDER, split_axis=0, concat_axis=0, tiled=True
     )
 
     count = half * half
@@ -374,6 +391,18 @@
     anywhere = pl.BlockSpec(memory_space=pltpu.HBM)
     cells = ext_x * ext_y * depth
     lines = 2 * slot_cap * (row_width // depth + 1)
+    kept = [
+        pl.pallas_call(
+            keep_kernel,
+            out_shape=struct(box.shape, box.dtype),
+            in_specs=[VMEM],
+            out_specs=VMEM,
+            compiler_params=params(24),
+            cost_estimate=pl.CostEstimate(flops=0, transcendentals=0, bytes_accessed=1 << 19),
+        )(box)
+        for box in from_xy
+    ]
+    owner_first, *kept = lax.optimization_barrier((owner_col, *kept))
     outgoing = pl.pallas_call(
         functools.partial(pairs_kernel, half, slot_cap, sizes),
         out_shape=struct((device_count, lines, depth), jnp.int16),
@@ -384,11 +413,11 @@
             pltpu.VMEM((pl.cdiv(9 * func_count, depth), 2 * func_count, depth), jnp.float32),
             pltpu.SMEM((device_count,), jnp.int32),
         ],
-        compiler_params=params(60),
+        compiler_params=params(24),
         cost_estimate=pl.CostEstimate(
             flops=16 * func_count * func_count * cells, transcendentals=0, bytes_accessed=7 << 20
         ),
-    )(owner_col, potential, *boxes)
+    )(owner_first, potential, *boxes)
     blocks = lax.all_to_all(outgoing, ORDER, split_axis=0, concat_axis=0, tiled=True)
     steps = 2
     chunk = device_count // steps
@@ -417,7 +446,7 @@
         cost_estimate=pl.CostEstimate(
             flops=8 * func_count * func_count * cells, transcendentals=0, bytes_accessed=7 << 20
         ),
-    )(owner_col, kernel_in, potential, *boxes)
+    )(owner_col, kernel_in, potential, *boxes[:6], *kept)
     return (blocks, gradient.reshape(functions.shape))
 
 

time: 74.5 us -> 85.5 us (1.15)
  waiting for transfers between devices: 23.2 us -> 31.6 us
  local copies, waits for them, and re-layouts: 2.8 us -> 5.65 us
  starting transfers between devices: 32 us -> 30.7 us
  Pallas kernels: 15.4 us -> 16.3 us
    ppermute x8, waiting for transfers between devices: 9.16 us -> 17.6 us  [shifted(): lax.ppermute(shard, axis, [(i, (i + by) % size) for i in range(size)])]
    unnamed x22 -> x30, local copies, waits for them, and re-layouts: 2.71 us -> 4.76 us
    ppermute x8, starting transfers between devices: 14.6 us -> 13.1 us  [shifted(): lax.ppermute(shard, axis, [(i, (i + by) % size) for i in range(size)])]
    pallas_call x1, Pallas kernels: 5.9 us -> 4.78 us  [body(): pl.pallas_call(functools.partial(pairs_kernel, half, slot_cap, sizes), ou...]
    pallas_call x0 -> x4, Pallas kernels: none -> 1.03 us  [body(): pl.pallas_call(keep_kernel, out_shape=struct(box.shape, box.dtype), in_sp...]
    pallas_call x2, Pallas kernels: 0.53 us -> 1.48 us  [split(): pl.pallas_call(functools.partial(kernel, half), out_shape=(band,) * 2, in...]
  transfers between devices with their start and end apart: 10 -> 10, of which waited for: 4 -> 4; matrix products, arithmetic and copies ran while one was open for 0% -> 0% of each run, Pallas kernels for 18% -> 16%
where the time goes in v4:
time: 85.5 us; the launch traced here: 85.1 us
  waiting for transfers between devices  31.6 us (37%)
  starting transfers between devices  30.7 us (36%)
  Pallas kernels  16.3 us (19%)
  local copies, waits for them, and re-layouts  5.65 us (7%)
    ppermute x8, waiting for transfers between devices, shifted(): lax.ppermute(shard, axis, [(i, (i + by) % size) for i in range(size)])  17.6 us
    all_to_all x1, waiting for transfers between devices, body(): lax.all_to_all(outgoing, ORDER, split_axis=0, concat_axis=0, tiled=True)  14 us
    ppermute x8, starting transfers between devices, shifted(): lax.ppermute(shard, axis, [(i, (i + by) % size) for i in range(size)])  13.1 us
    all_to_all x1, starting transfers between devices, body(): lax.all_to_all(kernel_out, ROWS_ORDER, split_axis=0, concat_axis=0, tiled...  9.01 us
    all_to_all x1, starting transfers between devices, body(): lax.all_to_all(outgoing, ORDER, split_axis=0, concat_axis=0, tiled=True)  8.64 us
    pallas_call x1, Pallas kernels, body(): pl.pallas_call(functools.partial(mix_kernel, half, sizes), out_shape=stru...  6.08 us
    pallas_call x1, Pallas kernels, body(): pl.pallas_call(functools.partial(pairs_kernel, half, slot_cap, sizes), ou...  4.78 us
    unnamed x30, local copies, waits for them, and re-layouts  4.76 us
  transfers between devices with their start and end apart: 10, of which 4 were waited for; matrix products, arithmetic and copies ran while one was open for 0% of the time, Pallas kernels for 16%

profile of v4, /device:TPU:1, one launch (start us, length us, event | category | flops | bytes accessed | tf_op | source)
XLA Modules:
  0.0 85.1 jit_solution(6117094142794993142)
XLA Ops:
  0.6 1.2 %copy-done.10 = bf16[1,1,64,8,8,128]{5,4,3,2,1,0:T(8,128)(2,1)S(1)} copy-done((bf16[1,1,64,8,8,128]{5,4,3,2,1,0:T(8,128)(2,1)S(1)}, bf16[1,1,64,8,8,128]{5,4,3,2,1,0:T(8,128)(2,1)}, u32[]{:S(2)}) %copy-start.10) | copy-done | bytes 1048600
  1.9 0.7 copy-done.12
  2.6 0.4 shard_map.59
  3.0 2.2 %collective-permute-start = (bf16[33,64,128]{2,1,0:T(8,128)(2,1)S(1)}, bf16[33,64,128]{2,1,0:T(8,128)(2,1)S(1)}, u32[]{:S(2)}, u32[]{:S(2)}) collective-permute-start(bf16[33,64,128]{2,1,0:T(8,128)(2,1)S(1)} %get-tuple-element.14.x1_ref.refs_1_), channel_id=1, source_target_pairs={{0,8},{8,16},{16,24},{24,32},{32,40},{40,48},{48,56},{56,64},{64,7... | collective-permute-start | bytes 1622024 | tf_op jit(solution)/shard_map/ppermute | solution.py:47
  5.2 5.0 %collective-permute-start.1 = (bf16[33,64,128]{2,1,0:T(8,128)(2,1)S(1)}, bf16[33,64,128]{2,1,0:T(8,128)(2,1)S(1)}, u32[]{:S(2)}, u32[]{:S(2)}) collective-permute-start(bf16[33,64,128]{2,1,0:T(8,128)(2,1)S(1)} %get-tuple-element.15.x0_ref.refs_0_), channel_id=1, source_target_pairs={{0,120},{8,0},{16,8},{24,16},{32,24},{40,32},{48,40},{56,48},{64,5... | collective-permute-start | bytes 1622024 | tf_op jit(solution)/shard_map/ppermute | solution.py:47
  10.2 1.0 %shard_map.60 = (bf16[33,64,128]{2,1,0:T(8,128)(2,1)}, bf16[33,64,128]{2,1,0:T(8,128)(2,1)}) custom-call(bf16[33,64,128]{2,1,0:T(8,128)(2,1)S(1)} %get-tuple-element.15.x0_ref.refs_0_, bf16[33,64,128]{2,1,0:T(8,128)(2,1)S(1)} %get-tuple-element.14.x1_ref.refs_1_, f32[4,4,128]{2,1,0:T(4,128)S(1)} %copy-done.12), custom_call_target="tpu_custom_call" | custom-call | bytes 2097152 | tf_op jit(solution)/shard_map/pallas_call | solution.py:359
  11.2 0.9 %shard_map.61 = bf16[128,2,1152]{2,1,0:T(2,128)(2,1)} custom-call(bf16[256,1152]{1,0:T(8,128)(2,1)S(1)} %copy-done.11), custom_call_target="tpu_custom_call" | custom-call | bytes 1048576 | tf_op jit(solution)/shard_map/pallas_call | solution.py:373
  12.2 9.9 %collective-permute-done.refs_2_ = bf16[33,64,128]{2,1,0:T(8,128)(2,1)S(1)} collective-permute-done((bf16[33,64,128]{2,1,0:T(8,128)(2,1)S(1)}, bf16[33,64,128]{2,1,0:T(8,128)(2,1)S(1)}, u32[]{:S(2)}, u32[]{:S(2)}) %collective-permute-start) | collective-permute-done | bytes 540704 | tf_op jit(solution)/shard_map/ppermute | solution.py:47
  22.1 0.0 collective-permute-done.1.refs_3_
  22.1 0.8 fusion.1
  23.0 2.3 %collective-permute-start.2 = (bf16[17,64,128]{2,1,0:T(8,128)(2,1)}, bf16[17,64,128]{2,1,0:T(8,128)(2,1)}, u32[]{:S(2)}, u32[]{:S(2)}) collective-permute-start(bf16[17,64,128]{2,1,0:T(8,128)(2,1)} %get-tuple-element.29), channel_id=1, source_target_pairs={{0,1},{1,2},{2,3},{3,4},{4,5},{5,6},{6,7},{7,0},{8,9},{9,10},{10,1... | collective-permute-start | bytes 835592 | tf_op jit(solution)/shard_map/ppermute | solution.py:47
  25.3 0.0 collective-permute-start.6
  25.3 0.5 collective-permute-start.7
  25.8 9.0 %all-to-all-start.1 = ((bf16[128,2,1152]{2,1,0:T(2,128)(2,1)}), bf16[128,2,1152]{2,1,0:T(2,128)(2,1)}, u32[]{:S(2)}, u32[]{:S(2)}) async-start(bf16[128,2,1152]{2,1,0:T(2,128)(2,1)} %shard_map.61), calls=%async_computation.1 | async-start | bytes 1179648 | tf_op jit(solution)/shard_map/all_to_all | solution.py:381
  34.8 1.1 %collective-permute-start.3 = (bf16[17,64,128]{2,1,0:T(8,128)(2,1)S(1)}, bf16[17,64,128]{2,1,0:T(8,128)(2,1)S(1)}, u32[]{:S(2)}, u32[]{:S(2)}) collective-permute-start(bf16[17,64,128]{2,1,0:T(8,128)(2,1)S(1)} %get-tuple-element.28), channel_id=1, source_target_pairs={{0,7},{1,0},{2,1},{3,2},{4,3},{5,4},{6,5},{7,6},{8,15},{9,8},{10,9... | collective-permute-start | bytes 835592 | tf_op jit(solution)/shard_map/ppermute | solution.py:47
  36.0 0.0 copy-start.13
  36.0 0.0 copy-start.14
  36.0 0.6 collective-permute-start.4
  36.7 1.3 %collective-permute-start.5 = (bf16[17,64,128]{2,1,0:T(8,128)(2,1)S(1)}, bf16[17,64,128]{2,1,0:T(8,128)(2,1)S(1)}, u32[]{:S(2)}, u32[]{:S(2)}) collective-permute-start(bf16[17,64,128]{2,1,0:T(8,128)(2,1)S(1)} %get-tuple-element.26), channel_id=1, source_target_pairs={{0,7},{1,0},{2,1},{3,2},{4,3},{5,4},{6,5},{7,6},{8,15},{9,8},{10,9... | collective-permute-start | bytes 835592 | tf_op jit(solution)/shard_map/ppermute | solution.py:47
  38.0 1.0 %shard_map.62.refs_6_ = bf16[17,64,128]{2,1,0:T(8,128)(2,1)S(1)} custom-call(bf16[17,64,128]{2,1,0:T(8,128)(2,1)} %collective-permute-done.2.refs_0_.refs_6_), custom_call_target="tpu_custom_call" | custom-call | bytes 524288 | tf_op jit(solution)/shard_map/pallas_call | solution.py:395
  38.9 0.7 copy-done.6
  39.6 6.2 %collective-permute-done.3.refs_0_.refs_7_ = bf16[17,64,128]{2,1,0:T(8,128)(2,1)S(1)} collective-permute-done((bf16[17,64,128]{2,1,0:T(8,128)(2,1)S(1)}, bf16[17,64,128]{2,1,0:T(8,128)(2,1)S(1)}, u32[]{:S(2)}, u32[]{:S(2)}) %collective-permute-start.3) | collective-permute-done | bytes 278560 | tf_op jit(solution)/shard_map/ppermute | solution.py:47
  45.8 0.7 copy-done.7
  46.6 0.7 copy-done.8
  47.3 1.5 %collective-permute-done.5.refs_0_.refs_9_ = bf16[17,64,128]{2,1,0:T(8,128)(2,1)S(1)} collective-permute-done((bf16[17,64,128]{2,1,0:T(8,128)(2,1)S(1)}, bf16[17,64,128]{2,1,0:T(8,128)(2,1)S(1)}, u32[]{:S(2)}, u32[]{:S(2)}) %collective-permute-start.5) | collective-permute-done | bytes 278560 | tf_op jit(solution)/shard_map/ppermute | solution.py:47
  48.8 0.7 copy-done.9
  49.6 4.8 %shard_map.66 = s16[128,40,128]{2,1,0:T(8,128)(2,1)} custom-call(s32[32]{0:T(128)S(1)} %bitcast.5, f32[4,4,128]{2,1,0:T(4,128)S(1)} %copy-done.13, bf16[33,64,128]{2,1,0:T(8,128)(2,1)S(1)} %get-tuple-element.15.x0_ref.refs_0_, bf16[33,64,128]{2,1,0:T(8,128)(2,1)S(1)} %get-tuple-element.14.x1_ref.refs_1_, ...), custom_call_target="tpu_custom_call" | custom-call | flops 536870912 | bytes 7340032 | tf_op jit(solution)/shard_map/pallas_call | solution.py:406
  54.4 0.0 all-to-all-done.1.kernel_ref
  54.4 8.6 %all-to-all-start = ((s16[128,40,128]{2,1,0:T(8,128)(2,1)}), s16[128,40,128]{2,1,0:T(8,128)(2,1)S(1)}, u32[]{:S(2)}, u32[]{:S(2)}) async-start(s16[128,40,128]{2,1,0:T(8,128)(2,1)} %shard_map.66), calls=%async_computation | async-start | bytes 2621440 | tf_op jit(solution)/shard_map/all_to_all | solution.py:421
  63.0 6.1 %shard_map.68 = bf16[32,2,8,8,128]{4,3,2,1,0:T(8,128)(2,1)} custom-call(s32[32]{0:T(128)} %bitcast.4, bf16[128,2,1152]{2,1,0:T(2,128)(2,1)} %all-to-all-done.1.kernel_ref, f32[4,4,128]{2,1,0:T(4,128)} %pot_ref.7, bf16[33,64,128]{2,1,0:T(8,128)(2,1)} %copy-done.2, bf16[33,64,128]{2,1,0:T(8,128)(2,1)} %copy-done.3, bf16[33,64,128]{2,1,0:T(8,128)(2,1)} %copy-done, ...), custom_call_target="tpu_custom_call" | custom-call | flops 268435456 | bytes 7340032 | tf_op jit(solution)/shard_map/pallas_call | solution.py:433
  69.1 14.0 %all-to-all-done.in_ref = s16[128,40,128]{2,1,0:T(8,128)(2,1)S(1)} async-done(((s16[128,40,128]{2,1,0:T(8,128)(2,1)}), s16[128,40,128]{2,1,0:T(8,128)(2,1)S(1)}, u32[]{:S(2)}, u32[]{:S(2)}) %all-to-all-start) | async-done | bytes 1310752 | tf_op jit(solution)/shard_map/all_to_all | solution.py:421
  83.1 2.0 %shard_map.67 = f32[256,2,1152]{2,1,0:T(2,128)} custom-call(s16[128,40,128]{2,1,0:T(8,128)(2,1)S(1)} %all-to-all-done.in_ref), custom_call_target="tpu_custom_call" | custom-call | tf_op jit(solution)/shard_map/pallas_call | solution.py:424
  (30 shorter events, 0.2 us)
Async XLA Ops:
  0.6 1.2 %copy-start.10 = (bf16[1,1,64,8,8,128]{5,4,3,2,1,0:T(8,128)(2,1)S(1)}, bf16[1,1,64,8,8,128]{5,4,3,2,1,0:T(8,128)(2,1)}, u32[]{:S(2)}) copy-start(bf16[1,1,64,8,8,128]{5,4,3,2,1,0:T(8,128)(2,1)} %param.5) | copy-start | bytes 3145732
  1.9 0.7 copy-start.12
  2.6 8.7 %copy-start.11 = (bf16[256,1152]{1,0:T(8,128)(2,1)S(1)}, bf16[256,1152]{1,0:T(8,128)(2,1)}, u32[]{:S(2)}) copy-start(bf16[256,1152]{1,0:T(8,128)(2,1)} %k_ref) | copy-start | bytes 1769476
  3.0 46.5 %copy-start.2 = (bf16[33,64,128]{2,1,0:T(8,128)(2,1)}, bf16[33,64,128]{2,1,0:T(8,128)(2,1)S(1)}, u32[]{:S(2)}) copy-start(bf16[33,64,128]{2,1,0:T(8,128)(2,1)S(1)} %get-tuple-element.15.x0_ref.refs_0_) | copy-start | bytes 1622020
  3.0 46.5 %copy-start.3 = (bf16[33,64,128]{2,1,0:T(8,128)(2,1)}, bf16[33,64,128]{2,1,0:T(8,128)(2,1)S(1)}, u32[]{:S(2)}) copy-start(bf16[33,64,128]{2,1,0:T(8,128)(2,1)S(1)} %get-tuple-element.14.x1_ref.refs_1_) | copy-start | bytes 1622020
  3.0 19.1 %collective-permute-start = (bf16[33,64,128]{2,1,0:T(8,128)(2,1)S(1)}, bf16[33,64,128]{2,1,0:T(8,128)(2,1)S(1)}, u32[]{:S(2)}, u32[]{:S(2)}) collective-permute-start(bf16[33,64,128]{2,1,0:T(8,128)(2,1)S(1)} %get-tuple-element.14.x1_ref.refs_1_), channel_id=1, source_target_pairs={{0,8},{8,16},{16,24},{24,32},{32,40},{40,48},{48,56},{56,64},{64,7... | collective-permute-start | bytes 1622024 | tf_op jit(solution)/shard_map/ppermute | solution.py:47
  5.2 16.9 %collective-permute-start.1 = (bf16[33,64,128]{2,1,0:T(8,128)(2,1)S(1)}, bf16[33,64,128]{2,1,0:T(8,128)(2,1)S(1)}, u32[]{:S(2)}, u32[]{:S(2)}) collective-permute-start(bf16[33,64,128]{2,1,0:T(8,128)(2,1)S(1)} %get-tuple-element.15.x0_ref.refs_0_), channel_id=1, source_target_pairs={{0,120},{8,0},{16,8},{24,16},{32,24},{40,32},{48,40},{56,48},{64,5... | collective-permute-start | bytes 1622024 | tf_op jit(solution)/shard_map/ppermute | solution.py:47
  22.1 27.4 %copy-start = (bf16[33,64,128]{2,1,0:T(8,128)(2,1)}, bf16[33,64,128]{2,1,0:T(8,128)(2,1)S(1)}, u32[]{:S(2)}) copy-start(bf16[33,64,128]{2,1,0:T(8,128)(2,1)S(1)} %collective-permute-done.refs_2_) | copy-start | bytes 1622020
  22.1 27.4 %copy-start.1 = (bf16[33,64,128]{2,1,0:T(8,128)(2,1)}, bf16[33,64,128]{2,1,0:T(8,128)(2,1)S(1)}, u32[]{:S(2)}) copy-start(bf16[33,64,128]{2,1,0:T(8,128)(2,1)S(1)} %collective-permute-done.1.refs_3_) | copy-start | bytes 1622020
  23.0 13.7 %collective-permute-start.2 = (bf16[17,64,128]{2,1,0:T(8,128)(2,1)}, bf16[17,64,128]{2,1,0:T(8,128)(2,1)}, u32[]{:S(2)}, u32[]{:S(2)}) collective-permute-start(bf16[17,64,128]{2,1,0:T(8,128)(2,1)} %get-tuple-element.29), channel_id=1, source_target_pairs={{0,1},{1,2},{2,3},{3,4},{4,5},{5,6},{6,7},{7,0},{8,9},{9,10},{10,1... | collective-permute-start | bytes 835592 | tf_op jit(solution)/shard_map/ppermute | solution.py:47
  25.3 24.2 %collective-permute-start.6 = (bf16[33,64,128]{2,1,0:T(8,128)(2,1)}, bf16[33,64,128]{2,1,0:T(8,128)(2,1)S(1)}, u32[]{:S(2)}, u32[]{:S(2)}) collective-permute-start(bf16[33,64,128]{2,1,0:T(8,128)(2,1)} %get-tuple-element.17), channel_id=1, source_target_pairs={{0,1},{1,2},{2,3},{3,4},{4,5},{5,6},{6,7},{7,0},{8,9},{9,10},{10,1... | collective-permute-start | bytes 1622024 | tf_op jit(solution)/shard_map/ppermute | solution.py:47
  25.3 24.2 %collective-permute-start.7 = (bf16[33,64,128]{2,1,0:T(8,128)(2,1)}, bf16[33,64,128]{2,1,0:T(8,128)(2,1)S(1)}, u32[]{:S(2)}, u32[]{:S(2)}) collective-permute-start(bf16[33,64,128]{2,1,0:T(8,128)(2,1)} %get-tuple-element.16), channel_id=1, source_target_pairs={{0,7},{1,0},{2,1},{3,2},{4,3},{5,4},{6,5},{7,6},{8,15},{9,8},{10,9... | collective-permute-start | bytes 1622024 | tf_op jit(solution)/shard_map/ppermute | solution.py:47
  25.8 28.6 %all-to-all-start.1 = ((bf16[128,2,1152]{2,1,0:T(2,128)(2,1)}), bf16[128,2,1152]{2,1,0:T(2,128)(2,1)}, u32[]{:S(2)}, u32[]{:S(2)}) async-start(bf16[128,2,1152]{2,1,0:T(2,128)(2,1)} %shard_map.61), calls=%async_computation.1 | async-start | bytes 1179648 | tf_op jit(solution)/shard_map/all_to_all | solution.py:381
  34.8 11.0 %collective-permute-start.3 = (bf16[17,64,128]{2,1,0:T(8,128)(2,1)S(1)}, bf16[17,64,128]{2,1,0:T(8,128)(2,1)S(1)}, u32[]{:S(2)}, u32[]{:S(2)}) collective-permute-start(bf16[17,64,128]{2,1,0:T(8,128)(2,1)S(1)} %get-tuple-element.28), channel_id=1, source_target_pairs={{0,7},{1,0},{2,1},{3,2},{4,3},{5,4},{6,5},{7,6},{8,15},{9,8},{10,9... | collective-permute-start | bytes 835592 | tf_op jit(solution)/shard_map/ppermute | solution.py:47
  36.0 13.5 %copy-start.13 = (f32[4,4,128]{2,1,0:T(4,128)S(1)}, f32[4,4,128]{2,1,0:T(4,128)}, u32[]{:S(2)}) copy-start(f32[4,4,128]{2,1,0:T(4,128)} %pot_ref.7) | copy-start | bytes 24580
  36.0 13.5 %copy-start.14 = (s32[32,1]{0,1:T(1,128)S(1)}, s32[32,1]{0,1:T(1,128)}, u32[]{:S(2)}) copy-start(s32[32,1]{0,1:T(1,128)} %param.7) | copy-start | bytes 388
  36.0 10.5 %collective-permute-start.4 = (bf16[17,64,128]{2,1,0:T(8,128)(2,1)S(1)}, bf16[17,64,128]{2,1,0:T(8,128)(2,1)S(1)}, u32[]{:S(2)}, u32[]{:S(2)}) collective-permute-start(bf16[17,64,128]{2,1,0:T(8,128)(2,1)S(1)} %get-tuple-element.27), channel_id=1, source_target_pairs={{0,1},{1,2},{2,3},{3,4},{4,5},{5,6},{6,7},{7,0},{8,9},{9,10},{10,1... | collective-permute-start | bytes 835592 | tf_op jit(solution)/shard_map/ppermute | solution.py:47
  36.7 12.1 %collective-permute-start.5 = (bf16[17,64,128]{2,1,0:T(8,128)(2,1)S(1)}, bf16[17,64,128]{2,1,0:T(8,128)(2,1)S(1)}, u32[]{:S(2)}, u32[]{:S(2)}) collective-permute-start(bf16[17,64,128]{2,1,0:T(8,128)(2,1)S(1)} %get-tuple-element.26), channel_id=1, source_target_pairs={{0,7},{1,0},{2,1},{3,2},{4,3},{5,4},{6,5},{7,6},{8,15},{9,8},{10,9... | collective-permute-start | bytes 835592 | tf_op jit(solution)/shard_map/ppermute | solution.py:47
  38.9 0.7 copy-start.6
  45.8 0.7 copy-start.7
  46.6 0.7 copy-start.8
  48.8 0.7 copy-start.9
  49.5 4.9 %copy-start.4 = (bf16[33,64,128]{2,1,0:T(8,128)(2,1)}, bf16[33,64,128]{2,1,0:T(8,128)(2,1)S(1)}, u32[]{:S(2)}) copy-start(bf16[33,64,128]{2,1,0:T(8,128)(2,1)S(1)} %collective-permute-done.6.refs_4_) | copy-start | bytes 1622020
  49.6 4.8 %copy-start.5 = (bf16[33,64,128]{2,1,0:T(8,128)(2,1)}, bf16[33,64,128]{2,1,0:T(8,128)(2,1)S(1)}, u32[]{:S(2)}) copy-start(bf16[33,64,128]{2,1,0:T(8,128)(2,1)S(1)} %collective-permute-done.7.refs_5_) | copy-start | bytes 1622020
  54.4 28.8 %all-to-all-start = ((s16[128,40,128]{2,1,0:T(8,128)(2,1)}), s16[128,40,128]{2,1,0:T(8,128)(2,1)S(1)}, u32[]{:S(2)}, u32[]{:S(2)}) async-start(s16[128,40,128]{2,1,0:T(8,128)(2,1)} %shard_map.66), calls=%async_computation | async-start | bytes 2621440 | tf_op jit(solution)/shard_map/all_to_all | solution.py:421

commit v5 on v4

--- a/solution.py
+++ b/solution.py
@@ -283,12 +283,6 @@
             for t in range(data // (2 * cap)):
                 start = rank * (data // cap) + 2 * t
                 out_ref[c * cap + rank, :, t * depth : (t + 1) * depth] = values[start : start + 2]
-
-
-def keep_kernel(*refs):
-    number = len(refs) // 2
-    for given, kept in zip(refs[:number], refs[number:]):
-        kept[...] = given[...]
 
 
 def mix_kernel(half, sizes, owner_ref, kernel_ref, pot_ref, *refs):
@@ -391,18 +385,6 @@
     anywhere = pl.BlockSpec(memory_space=pltpu.HBM)
     cells = ext_x * ext_y * depth
     lines = 2 * slot_cap * (row_width // depth + 1)
-    kept = [
-        pl.pallas_call(
-            keep_kernel,
-            out_shape=struct(box.shape, box.dtype),
-            in_specs=[VMEM],
-            out_specs=VMEM,
-            compiler_params=params(24),
-            cost_estimate=pl.CostEstimate(flops=0, transcendentals=0, bytes_accessed=1 << 19),
-        )(box)
-        for box in from_xy
-    ]
-    owner_first, *kept = lax.optimization_barrier((owner_col, *kept))
     outgoing = pl.pallas_call(
         functools.partial(pairs_kernel, half, slot_cap, sizes),
         out_shape=struct((device_count, lines, depth), jnp.int16),
@@ -413,11 +395,11 @@
             pltpu.VMEM((pl.cdiv(9 * func_count, depth), 2 * func_count, depth), jnp.float32),
             pltpu.SMEM((device_count,), jnp.int32),
         ],
-        compiler_params=params(24),
+        compiler_params=params(60),
         cost_estimate=pl.CostEstimate(
             flops=16 * func_count * func_count * cells, transcendentals=0, bytes_accessed=7 << 20
         ),
-    )(owner_first, potential, *boxes)
+    )(owner_col, potential, *boxes)
     blocks = lax.all_to_all(outgoing, ORDER, split_axis=0, concat_axis=0, tiled=True)
     steps = 2
     chunk = device_count // steps
@@ -446,7 +428,7 @@
         cost_estimate=pl.CostEstimate(
             flops=8 * func_count * func_count * cells, transcendentals=0, bytes_accessed=7 << 20
         ),
-    )(owner_col, kernel_in, potential, *boxes[:6], *kept)
+    )(owner_col, kernel_in, potential, *boxes)
     return (blocks, gradient.reshape(functions.shape))
 
 

time: 85.5 us -> 74.4 us (0.87)
  waiting for transfers between devices: 31.6 us -> 23.3 us
  local copies, waits for them, and re-layouts: 5.65 us -> 2.8 us
  starting transfers between devices: 30.7 us -> 31.9 us
  Pallas kernels: 16.3 us -> 15.3 us
    ppermute x8, waiting for transfers between devices: 17.6 us -> 9.26 us  [shifted(): lax.ppermute(shard, axis, [(i, (i + by) % size) for i in range(size)])]
    unnamed x30 -> x22, local copies, waits for them, and re-layouts: 4.76 us -> 2.71 us
    ppermute x8, starting transfers between devices: 13.1 us -> 14.6 us  [shifted(): lax.ppermute(shard, axis, [(i, (i + by) % size) for i in range(size)])]
    pallas_call x4 -> x0, Pallas kernels: 1.03 us -> none  [body(): pl.pallas_call(keep_kernel, out_shape=struct(box.shape, box.dtype), in_sp...]
    pallas_call x1, Pallas kernels: 4.78 us -> 5.79 us  [body(): pl.pallas_call(functools.partial(pairs_kernel, half, slot_cap, sizes), ou...]
    pallas_call x2, Pallas kernels: 1.48 us -> 0.53 us  [split(): pl.pallas_call(functools.partial(kernel, half), out_shape=(band,) * 2, in...]
    all_to_all x1, starting transfers between devices: 8.64 us -> 7.74 us  [body(): lax.all_to_all(outgoing, ORDER, split_axis=0, concat_axis=0, tiled=True)]
  transfers between devices with their start and end apart: 10 -> 10, of which waited for: 4 -> 4; matrix products, arithmetic and copies ran while one was open for 0% -> 0% of each run, Pallas kernels for 16% -> 17%
where the time goes in v5:
time: 74.4 us; the launch traced here: 74 us
  starting transfers between devices  31.9 us (43%)
  waiting for transfers between devices  23.3 us (31%)
  Pallas kernels  15.3 us (21%)
  local copies, waits for them, and re-layouts  2.8 us (4%)
  between operations  0.77 us (1%)
    ppermute x8, starting transfers between devices, shifted(): lax.ppermute(shard, axis, [(i, (i + by) % size) for i in range(size)])  14.6 us
    all_to_all x1, waiting for transfers between devices, body(): lax.all_to_all(outgoing, ORDER, split_axis=0, concat_axis=0, tiled=True)  14 us
    all_to_all x1, starting transfers between devices, body(): lax.all_to_all(kernel_out, ROWS_ORDER, split_axis=0, concat_axis=0, tiled...  9.52 us
    ppermute x8, waiting for transfers between devices, shifted(): lax.ppermute(shard, axis, [(i, (i + by) % size) for i in range(size)])  9.26 us
    all_to_all x1, starting transfers between devices, body(): lax.all_to_all(outgoing, ORDER, split_axis=0, concat_axis=0, tiled=True)  7.74 us
    pallas_call x1, Pallas kernels, body(): pl.pallas_call(functools.partial(mix_kernel, half, sizes), out_shape=stru...  6.09 us
    pallas_call x1, Pallas kernels, body(): pl.pallas_call(functools.partial(pairs_kernel, half, slot_cap, sizes), ou...  5.79 us
    unnamed x22, local copies, waits for them, and re-layouts  2.71 us
  transfers between devices with their start and end apart: 10, of which 4 were waited for; matrix products, arithmetic and copies ran while one was open for 0% of the time, Pallas kernels for 17%

profile of v5, /device:TPU:1, one launch (start us, length us, event | category | flops | bytes accessed | tf_op | source)
XLA Modules:
  0.0 74.0 jit_solution(17124170360303061745)
XLA Ops:
  0.6 0.0 copy-start.2
  0.6 1.2 %copy-done.2 = bf16[1,1,64,8,8,128]{5,4,3,2,1,0:T(8,128)(2,1)S(1)} copy-done((bf16[1,1,64,8,8,128]{5,4,3,2,1,0:T(8,128)(2,1)S(1)}, bf16[1,1,64,8,8,128]{5,4,3,2,1,0:T(8,128)(2,1)}, u32[]{:S(2)}) %copy-start.2) | copy-done | bytes 1048600
  1.9 0.7 copy-done.4
  2.6 0.4 shard_map.59
  3.0 7.1 %collective-permute-start.1 = (bf16[33,64,128]{2,1,0:T(8,128)(2,1)S(1)}, bf16[33,64,128]{2,1,0:T(8,128)(2,1)S(1)}, u32[]{:S(2)}, u32[]{:S(2)}) collective-permute-start(bf16[33,64,128]{2,1,0:T(8,128)(2,1)S(1)} %get-tuple-element.9.x0_ref.refs_0_), channel_id=1, source_target_pairs={{0,120},{8,0},{16,8},{24,16},{32,24},{40,32},{48,40},{56,48},{64,5... | collective-permute-start | bytes 1622024 | tf_op jit(solution)/shard_map/ppermute | solution.py:47
  10.1 0.0 collective-permute-start
  10.1 0.1 shard_map.60
  10.2 1.0 %collective-permute-start.3 = (bf16[33,64,128]{2,1,0:T(8,128)(2,1)S(1)}, bf16[33,64,128]{2,1,0:T(8,128)(2,1)}, u32[]{:S(2)}, u32[]{:S(2)}) collective-permute-start(bf16[33,64,128]{2,1,0:T(8,128)(2,1)S(1)} %get-tuple-element.11), channel_id=1, source_target_pairs={{0,7},{1,0},{2,1},{3,2},{4,3},{5,4},{6,5},{7,6},{8,15},{9,8},{10,9... | collective-permute-start | bytes 1622024 | tf_op jit(solution)/shard_map/ppermute | solution.py:47
  11.2 1.1 %collective-permute-start.2 = (bf16[33,64,128]{2,1,0:T(8,128)(2,1)S(1)}, bf16[33,64,128]{2,1,0:T(8,128)(2,1)}, u32[]{:S(2)}, u32[]{:S(2)}) collective-permute-start(bf16[33,64,128]{2,1,0:T(8,128)(2,1)S(1)} %get-tuple-element.12), channel_id=1, source_target_pairs={{0,1},{1,2},{2,3},{3,4},{4,5},{5,6},{6,7},{7,0},{8,9},{9,10},{10,1... | collective-permute-start | bytes 1622024 | tf_op jit(solution)/shard_map/ppermute | solution.py:47
  12.3 0.9 %shard_map.61 = bf16[128,2,1152]{2,1,0:T(2,128)(2,1)} custom-call(bf16[256,1152]{1,0:T(8,128)(2,1)S(1)} %copy-done.3), custom_call_target="tpu_custom_call" | custom-call | bytes 1048576 | tf_op jit(solution)/shard_map/pallas_call | solution.py:367
  13.2 0.0 copy-done.1
  13.2 9.5 %all-to-all-start.1 = ((bf16[128,2,1152]{2,1,0:T(2,128)(2,1)}), bf16[128,2,1152]{2,1,0:T(2,128)(2,1)}, u32[]{:S(2)}, u32[]{:S(2)}) async-start(bf16[128,2,1152]{2,1,0:T(2,128)(2,1)} %shard_map.61), calls=%async_computation.1 | async-start | bytes 1179648 | tf_op jit(solution)/shard_map/all_to_all | solution.py:375
  22.8 0.0 collective-permute-done.1.refs_3_
  22.8 3.5 %collective-permute-done.refs_2_ = bf16[33,64,128]{2,1,0:T(8,128)(2,1)S(1)} collective-permute-done((bf16[33,64,128]{2,1,0:T(8,128)(2,1)S(1)}, bf16[33,64,128]{2,1,0:T(8,128)(2,1)S(1)}, u32[]{:S(2)}, u32[]{:S(2)}) %collective-permute-start) | collective-permute-done | bytes 540704 | tf_op jit(solution)/shard_map/ppermute | solution.py:47
  26.3 2.3 %collective-permute-start.5 = (bf16[17,64,128]{2,1,0:T(8,128)(2,1)S(1)}, bf16[17,64,128]{2,1,0:T(8,128)(2,1)S(1)}, u32[]{:S(2)}, u32[]{:S(2)}) collective-permute-start(bf16[17,64,128]{2,1,0:T(8,128)(2,1)S(1)} %get-tuple-element.18), channel_id=1, source_target_pairs={{0,7},{1,0},{2,1},{3,2},{4,3},{5,4},{6,5},{7,6},{8,15},{9,8},{10,9... | collective-permute-start | bytes 835592 | tf_op jit(solution)/shard_map/ppermute | solution.py:47
  28.6 1.4 %collective-permute-start.4 = (bf16[17,64,128]{2,1,0:T(8,128)(2,1)S(1)}, bf16[17,64,128]{2,1,0:T(8,128)(2,1)S(1)}, u32[]{:S(2)}, u32[]{:S(2)}) collective-permute-start(bf16[17,64,128]{2,1,0:T(8,128)(2,1)S(1)} %get-tuple-element.19), channel_id=1, source_target_pairs={{0,1},{1,2},{2,3},{3,4},{4,5},{5,6},{6,7},{7,0},{8,9},{9,10},{10,1... | collective-permute-start | bytes 835592 | tf_op jit(solution)/shard_map/ppermute | solution.py:47
  30.1 0.0 collective-permute-start.7
  30.1 0.0 collective-permute-done.3.refs_5_
  30.1 1.7 %collective-permute-start.6 = (bf16[17,64,128]{2,1,0:T(8,128)(2,1)S(1)}, bf16[17,64,128]{2,1,0:T(8,128)(2,1)S(1)}, u32[]{:S(2)}, u32[]{:S(2)}) collective-permute-start(bf16[17,64,128]{2,1,0:T(8,128)(2,1)S(1)} %get-tuple-element.17), channel_id=1, source_target_pairs={{0,1},{1,2},{2,3},{3,4},{4,5},{5,6},{6,7},{7,0},{8,9},{9,10},{10,1... | collective-permute-start | bytes 835592 | tf_op jit(solution)/shard_map/ppermute | solution.py:47
  31.8 0.0 collective-permute-done.2.refs_4_
  31.8 2.8 %collective-permute-done.5.refs_7_ = bf16[17,64,128]{2,1,0:T(8,128)(2,1)S(1)} collective-permute-done((bf16[17,64,128]{2,1,0:T(8,128)(2,1)S(1)}, bf16[17,64,128]{2,1,0:T(8,128)(2,1)S(1)}, u32[]{:S(2)}, u32[]{:S(2)}) %collective-permute-start.5) | collective-permute-done | bytes 278560 | tf_op jit(solution)/shard_map/ppermute | solution.py:47
  34.6 0.0 collective-permute-done.4.refs_6_
  34.6 3.0 %collective-permute-done.7.refs_9_ = bf16[17,64,128]{2,1,0:T(8,128)(2,1)S(1)} collective-permute-done((bf16[17,64,128]{2,1,0:T(8,128)(2,1)S(1)}, bf16[17,64,128]{2,1,0:T(8,128)(2,1)S(1)}, u32[]{:S(2)}, u32[]{:S(2)}) %collective-permute-start.7) | collective-permute-done | bytes 278560 | tf_op jit(solution)/shard_map/ppermute | solution.py:47
  37.6 0.0 collective-permute-done.6.refs_8_
  37.7 0.7 copy-done.9
  38.3 0.1 copy-done.10
  38.4 5.8 %shard_map.62 = s16[128,40,128]{2,1,0:T(8,128)(2,1)} custom-call(s32[32]{0:T(128)} %bitcast.5, f32[4,4,128]{2,1,0:T(4,128)} %pot_ref.7, bf16[33,64,128]{2,1,0:T(8,128)(2,1)} %copy-done, bf16[33,64,128]{2,1,0:T(8,128)(2,1)} %copy-done.1, bf16[33,64,128]{2,1,0:T(8,128)(2,1)} %copy-done.6, bf16[33,64,128]{2,1,0:T(8,128)(2,1)} %copy-done.5, ...), custom_call_target="tpu_custom_call" | custom-call | flops 536870912 | bytes 7340032 | tf_op jit(solution)/shard_map/pallas_call | solution.py:388
  44.2 0.0 all-to-all-done.1.kernel_ref
  44.2 7.7 %all-to-all-start = ((s16[128,40,128]{2,1,0:T(8,128)(2,1)}), s16[128,40,128]{2,1,0:T(8,128)(2,1)S(1)}, u32[]{:S(2)}, u32[]{:S(2)}) async-start(s16[128,40,128]{2,1,0:T(8,128)(2,1)} %shard_map.62), calls=%async_computation | async-start | bytes 2621440 | tf_op jit(solution)/shard_map/all_to_all | solution.py:403
  52.0 6.1 %shard_map.64 = bf16[32,2,8,8,128]{4,3,2,1,0:T(8,128)(2,1)} custom-call(s32[32]{0:T(128)} %bitcast.6, bf16[128,2,1152]{2,1,0:T(2,128)(2,1)} %all-to-all-done.1.kernel_ref, f32[4,4,128]{2,1,0:T(4,128)} %pot_ref.7, bf16[33,64,128]{2,1,0:T(8,128)(2,1)} %copy-done, bf16[33,64,128]{2,1,0:T(8,128)(2,1)} %copy-done.1, bf16[33,64,128]{2,1,0:T(8,128)(2,1)} %copy-done.6, ...), custom_call_target="tpu_custom_call" | custom-call | flops 268435456 | bytes 7340032 | tf_op jit(solution)/shard_map/pallas_call | solution.py:415
  58.1 14.0 %all-to-all-done.in_ref = s16[128,40,128]{2,1,0:T(8,128)(2,1)S(1)} async-done(((s16[128,40,128]{2,1,0:T(8,128)(2,1)}), s16[128,40,128]{2,1,0:T(8,128)(2,1)S(1)}, u32[]{:S(2)}, u32[]{:S(2)}) %all-to-all-start) | async-done | bytes 1310752 | tf_op jit(solution)/shard_map/all_to_all | solution.py:403
  72.1 2.0 %shard_map.63 = f32[256,2,1152]{2,1,0:T(2,128)} custom-call(s16[128,40,128]{2,1,0:T(8,128)(2,1)S(1)} %all-to-all-done.in_ref), custom_call_target="tpu_custom_call" | custom-call | tf_op jit(solution)/shard_map/pallas_call | solution.py:406
  (18 shorter events, 0.1 us)
Async XLA Ops:
  0.6 1.2 %copy-start.2 = (bf16[1,1,64,8,8,128]{5,4,3,2,1,0:T(8,128)(2,1)S(1)}, bf16[1,1,64,8,8,128]{5,4,3,2,1,0:T(8,128)(2,1)}, u32[]{:S(2)}) copy-start(bf16[1,1,64,8,8,128]{5,4,3,2,1,0:T(8,128)(2,1)} %param.5) | copy-start | bytes 3145732
  1.9 0.7 copy-start.4
  2.6 9.7 %copy-start.3 = (bf16[256,1152]{1,0:T(8,128)(2,1)S(1)}, bf16[256,1152]{1,0:T(8,128)(2,1)}, u32[]{:S(2)}) copy-start(bf16[256,1152]{1,0:T(8,128)(2,1)} %k_ref) | copy-start | bytes 1769476
  3.0 10.2 %copy-start = (bf16[33,64,128]{2,1,0:T(8,128)(2,1)}, bf16[33,64,128]{2,1,0:T(8,128)(2,1)S(1)}, u32[]{:S(2)}) copy-start(bf16[33,64,128]{2,1,0:T(8,128)(2,1)S(1)} %get-tuple-element.9.x0_ref.refs_0_) | copy-start | bytes 1622020
  3.0 10.2 %copy-start.1 = (bf16[33,64,128]{2,1,0:T(8,128)(2,1)}, bf16[33,64,128]{2,1,0:T(8,128)(2,1)S(1)}, u32[]{:S(2)}) copy-start(bf16[33,64,128]{2,1,0:T(8,128)(2,1)S(1)} %get-tuple-element.10.x1_ref.refs_1_) | copy-start | bytes 1622020
  3.0 19.8 %collective-permute-start.1 = (bf16[33,64,128]{2,1,0:T(8,128)(2,1)S(1)}, bf16[33,64,128]{2,1,0:T(8,128)(2,1)S(1)}, u32[]{:S(2)}, u32[]{:S(2)}) collective-permute-start(bf16[33,64,128]{2,1,0:T(8,128)(2,1)S(1)} %get-tuple-element.9.x0_ref.refs_0_), channel_id=1, source_target_pairs={{0,120},{8,0},{16,8},{24,16},{32,24},{40,32},{48,40},{56,48},{64,5... | collective-permute-start | bytes 1622024 | tf_op jit(solution)/shard_map/ppermute | solution.py:47
  10.1 16.1 %collective-permute-start = (bf16[33,64,128]{2,1,0:T(8,128)(2,1)S(1)}, bf16[33,64,128]{2,1,0:T(8,128)(2,1)S(1)}, u32[]{:S(2)}, u32[]{:S(2)}) collective-permute-start(bf16[33,64,128]{2,1,0:T(8,128)(2,1)S(1)} %get-tuple-element.10.x1_ref.refs_1_), channel_id=1, source_target_pairs={{0,8},{8,16},{16,24},{24,32},{32,40},{40,48},{48,56},{56,64},{64,7... | collective-permute-start | bytes 1622024 | tf_op jit(solution)/shard_map/ppermute | solution.py:47
  10.2 19.9 %collective-permute-start.3 = (bf16[33,64,128]{2,1,0:T(8,128)(2,1)S(1)}, bf16[33,64,128]{2,1,0:T(8,128)(2,1)}, u32[]{:S(2)}, u32[]{:S(2)}) collective-permute-start(bf16[33,64,128]{2,1,0:T(8,128)(2,1)S(1)} %get-tuple-element.11), channel_id=1, source_target_pairs={{0,7},{1,0},{2,1},{3,2},{4,3},{5,4},{6,5},{7,6},{8,15},{9,8},{10,9... | collective-permute-start | bytes 1622024 | tf_op jit(solution)/shard_map/ppermute | solution.py:47
  11.2 20.7 %collective-permute-start.2 = (bf16[33,64,128]{2,1,0:T(8,128)(2,1)S(1)}, bf16[33,64,128]{2,1,0:T(8,128)(2,1)}, u32[]{:S(2)}, u32[]{:S(2)}) collective-permute-start(bf16[33,64,128]{2,1,0:T(8,128)(2,1)S(1)} %get-tuple-element.12), channel_id=1, source_target_pairs={{0,1},{1,2},{2,3},{3,4},{4,5},{5,6},{6,7},{7,0},{8,9},{9,10},{10,1... | collective-permute-start | bytes 1622024 | tf_op jit(solution)/shard_map/ppermute | solution.py:47
  13.2 31.0 %all-to-all-start.1 = ((bf16[128,2,1152]{2,1,0:T(2,128)(2,1)}), bf16[128,2,1152]{2,1,0:T(2,128)(2,1)}, u32[]{:S(2)}, u32[]{:S(2)}) async-start(bf16[128,2,1152]{2,1,0:T(2,128)(2,1)} %shard_map.61), calls=%async_computation.1 | async-start | bytes 1179648 | tf_op jit(solution)/shard_map/all_to_all | solution.py:375
  22.8 14.9 %copy-start.5 = (bf16[33,64,128]{2,1,0:T(8,128)(2,1)}, bf16[33,64,128]{2,1,0:T(8,128)(2,1)S(1)}, u32[]{:S(2)}) copy-start(bf16[33,64,128]{2,1,0:T(8,128)(2,1)S(1)} %collective-permute-done.1.refs_3_) | copy-start | bytes 1622020
  26.3 11.4 %copy-start.6 = (bf16[33,64,128]{2,1,0:T(8,128)(2,1)}, bf16[33,64,128]{2,1,0:T(8,128)(2,1)S(1)}, u32[]{:S(2)}) copy-start(bf16[33,64,128]{2,1,0:T(8,128)(2,1)S(1)} %collective-permute-done.refs_2_) | copy-start | bytes 1622020
  26.3 8.3 %collective-permute-start.5 = (bf16[17,64,128]{2,1,0:T(8,128)(2,1)S(1)}, bf16[17,64,128]{2,1,0:T(8,128)(2,1)S(1)}, u32[]{:S(2)}, u32[]{:S(2)}) collective-permute-start(bf16[17,64,128]{2,1,0:T(8,128)(2,1)S(1)} %get-tuple-element.18), channel_id=1, source_target_pairs={{0,7},{1,0},{2,1},{3,2},{4,3},{5,4},{6,5},{7,6},{8,15},{9,8},{10,9... | collective-permute-start | bytes 835592 | tf_op jit(solution)/shard_map/ppermute | solution.py:47
  28.6 6.0 %collective-permute-start.4 = (bf16[17,64,128]{2,1,0:T(8,128)(2,1)S(1)}, bf16[17,64,128]{2,1,0:T(8,128)(2,1)S(1)}, u32[]{:S(2)}, u32[]{:S(2)}) collective-permute-start(bf16[17,64,128]{2,1,0:T(8,128)(2,1)S(1)} %get-tuple-element.19), channel_id=1, source_target_pairs={{0,1},{1,2},{2,3},{3,4},{4,5},{5,6},{6,7},{7,0},{8,9},{9,10},{10,1... | collective-permute-start | bytes 835592 | tf_op jit(solution)/shard_map/ppermute | solution.py:47
  30.1 7.5 %collective-permute-start.7 = (bf16[17,64,128]{2,1,0:T(8,128)(2,1)S(1)}, bf16[17,64,128]{2,1,0:T(8,128)(2,1)S(1)}, u32[]{:S(2)}, u32[]{:S(2)}) collective-permute-start(bf16[17,64,128]{2,1,0:T(8,128)(2,1)S(1)} %get-tuple-element.16), channel_id=1, source_target_pairs={{0,7},{1,0},{2,1},{3,2},{4,3},{5,4},{6,5},{7,6},{8,15},{9,8},{10,9... | collective-permute-start | bytes 835592 | tf_op jit(solution)/shard_map/ppermute | solution.py:47
  30.1 7.5 %collective-permute-start.6 = (bf16[17,64,128]{2,1,0:T(8,128)(2,1)S(1)}, bf16[17,64,128]{2,1,0:T(8,128)(2,1)S(1)}, u32[]{:S(2)}, u32[]{:S(2)}) collective-permute-start(bf16[17,64,128]{2,1,0:T(8,128)(2,1)S(1)} %get-tuple-element.17), channel_id=1, source_target_pairs={{0,1},{1,2},{2,3},{3,4},{4,5},{5,6},{6,7},{7,0},{8,9},{9,10},{10,1... | collective-permute-start | bytes 835592 | tf_op jit(solution)/shard_map/ppermute | solution.py:47
  34.6 3.0 %copy-start.7 = (bf16[17,64,128]{2,1,0:T(8,128)(2,1)}, bf16[17,64,128]{2,1,0:T(8,128)(2,1)S(1)}, u32[]{:S(2)}) copy-start(bf16[17,64,128]{2,1,0:T(8,128)(2,1)S(1)} %collective-permute-done.5.refs_7_) | copy-start | bytes 835588
  34.6 3.0 %copy-start.8 = (bf16[17,64,128]{2,1,0:T(8,128)(2,1)}, bf16[17,64,128]{2,1,0:T(8,128)(2,1)S(1)}, u32[]{:S(2)}) copy-start(bf16[17,64,128]{2,1,0:T(8,128)(2,1)S(1)} %collective-permute-done.4.refs_6_) | copy-start | bytes 835588
  37.6 0.7 copy-start.9
  37.6 0.8 %copy-start.10 = (bf16[17,64,128]{2,1,0:T(8,128)(2,1)}, bf16[17,64,128]{2,1,0:T(8,128)(2,1)S(1)}, u32[]{:S(2)}) copy-start(bf16[17,64,128]{2,1,0:T(8,128)(2,1)S(1)} %collective-permute-done.6.refs_8_) | copy-start | bytes 835588
  44.2 27.8 %all-to-all-start = ((s16[128,40,128]{2,1,0:T(8,128)(2,1)}), s16[128,40,128]{2,1,0:T(8,128)(2,1)S(1)}, u32[]{:S(2)}, u32[]{:S(2)}) async-start(s16[128,40,128]{2,1,0:T(8,128)(2,1)} %shard_map.62), calls=%async_computation | async-start | bytes 2621440 | tf_op jit(solution)/shard_map/all_to_all | solution.py:403

commit v6 on v5

--- a/solution.py
+++ b/solution.py
@@ -146,12 +146,14 @@
 
 def pair_kernel(sizes, k_ref, o_ref):
     z_size, y_size, x_size, core_size = sizes
-    rows = k_ref[...].reshape(*sizes, *o_ref.shape[1:])
-    for core in range(core_size):
-        for x in range(x_size):
-            for y in range(y_size):
-                at = ((y * core_size + core) * x_size + x) * z_size
-                o_ref[at : at + z_size] = rows[:, y, x, core]
+    _, cap, width = o_ref.shape
+    count = x_size * core_size * cap
+    for z in range(z_size):
+        start = pl.multiple_of((z * y_size + pl.program_id(0)) * count, count)
+        rows = k_ref[pl.ds(start, count)].reshape(x_size, core_size, cap, width)
+        for core in range(core_size):
+            for x in range(x_size):
+                o_ref[(core * x_size + x) * z_size + z] = rows[x, core]
 
 
 def stencil(cell, potential_row, half, x, y, zero_low, zero_high):
@@ -368,7 +370,8 @@
         functools.partial(pair_kernel, sizes),
         out_shape=struct((device_count, slot_cap, row_width), bf16),
         in_specs=[VMEM],
-        out_specs=VMEM,
+        out_specs=pl.BlockSpec((device_count // sizes[1], slot_cap, row_width), lambda i: (i, 0, 0)),
+        grid=(sizes[1],),
         compiler_params=params(),
         cost_estimate=pl.CostEstimate(flops=0, transcendentals=0, bytes_accessed=1 << 20),
     )(kernel_store)

time: 74.4 us -> 74.9 us (level)
    all_to_all x1, starting transfers between devices: 7.74 us -> 8.6 us  [body(): lax.all_to_all(outgoing, ORDER, split_axis=0, concat_axis=0, tiled=True)]
  transfers between devices with their start and end apart: 10 -> 10, of which waited for: 4 -> 4; matrix products, arithmetic and copies ran while one was open for 0% -> 0% of each run, Pallas kernels for 17% -> 18%
where the time goes in v6:
time: 74.9 us; the launch traced here: 74.5 us
  starting transfers between devices  32.4 us (43%)
  waiting for transfers between devices  22.8 us (30%)
  Pallas kernels  15.8 us (21%)
  local copies, waits for them, and re-layouts  2.8 us (4%)
  between operations  0.77 us (1%)
    ppermute x8, starting transfers between devices, shifted(): lax.ppermute(shard, axis, [(i, (i + by) % size) for i in range(size)])  14.3 us
    all_to_all x1, waiting for transfers between devices, body(): lax.all_to_all(outgoing, ORDER, split_axis=0, concat_axis=0, tiled=True)  14 us
    all_to_all x1, starting transfers between devices, body(): lax.all_to_all(kernel_out, ROWS_ORDER, split_axis=0, concat_axis=0, tiled...  9.52 us
    ppermute x8, waiting for transfers between devices, shifted(): lax.ppermute(shard, axis, [(i, (i + by) % size) for i in range(size)])  8.77 us
    all_to_all x1, starting transfers between devices, body(): lax.all_to_all(outgoing, ORDER, split_axis=0, concat_axis=0, tiled=True)  8.6 us
    pallas_call x1, Pallas kernels, body(): pl.pallas_call(functools.partial(mix_kernel, half, sizes), out_shape=stru...  6.08 us
    pallas_call x1, Pallas kernels, body(): pl.pallas_call(functools.partial(pairs_kernel, half, slot_cap, sizes), ou...  5.79 us
    unnamed x22, local copies, waits for them, and re-layouts  2.71 us
  transfers between devices with their start and end apart: 10, of which 4 were waited for; matrix products, arithmetic and copies ran while one was open for 0% of the time, Pallas kernels for 18%

profile of v6, /device:TPU:1, one launch (start us, length us, event | category | flops | bytes accessed | tf_op | source)
XLA Modules:
  0.0 74.5 jit_solution(7587517992795028777)
XLA Ops:
  0.6 0.0 copy-start.2
  0.6 1.2 %copy-done.2 = bf16[1,1,64,8,8,128]{5,4,3,2,1,0:T(8,128)(2,1)S(1)} copy-done((bf16[1,1,64,8,8,128]{5,4,3,2,1,0:T(8,128)(2,1)S(1)}, bf16[1,1,64,8,8,128]{5,4,3,2,1,0:T(8,128)(2,1)}, u32[]{:S(2)}) %copy-start.2) | copy-done | bytes 1048600
  1.9 0.7 copy-done.4
  2.6 0.4 shard_map.59
  3.0 7.1 %collective-permute-start.1 = (bf16[33,64,128]{2,1,0:T(8,128)(2,1)S(1)}, bf16[33,64,128]{2,1,0:T(8,128)(2,1)S(1)}, u32[]{:S(2)}, u32[]{:S(2)}) collective-permute-start(bf16[33,64,128]{2,1,0:T(8,128)(2,1)S(1)} %get-tuple-element.9.x0_ref.refs_0_), channel_id=1, source_target_pairs={{0,120},{8,0},{16,8},{24,16},{32,24},{40,32},{48,40},{56,48},{64,5... | collective-permute-start | bytes 1622024 | tf_op jit(solution)/shard_map/ppermute | solution.py:47
  10.1 0.0 collective-permute-start
  10.1 0.1 shard_map.60
  10.2 1.0 %collective-permute-start.3 = (bf16[33,64,128]{2,1,0:T(8,128)(2,1)S(1)}, bf16[33,64,128]{2,1,0:T(8,128)(2,1)}, u32[]{:S(2)}, u32[]{:S(2)}) collective-permute-start(bf16[33,64,128]{2,1,0:T(8,128)(2,1)S(1)} %get-tuple-element.11), channel_id=1, source_target_pairs={{0,7},{1,0},{2,1},{3,2},{4,3},{5,4},{6,5},{7,6},{8,15},{9,8},{10,9... | collective-permute-start | bytes 1622024 | tf_op jit(solution)/shard_map/ppermute | solution.py:47
  11.2 1.1 %collective-permute-start.2 = (bf16[33,64,128]{2,1,0:T(8,128)(2,1)S(1)}, bf16[33,64,128]{2,1,0:T(8,128)(2,1)}, u32[]{:S(2)}, u32[]{:S(2)}) collective-permute-start(bf16[33,64,128]{2,1,0:T(8,128)(2,1)S(1)} %get-tuple-element.12), channel_id=1, source_target_pairs={{0,1},{1,2},{2,3},{3,4},{4,5},{5,6},{6,7},{7,0},{8,9},{9,10},{10,1... | collective-permute-start | bytes 1622024 | tf_op jit(solution)/shard_map/ppermute | solution.py:47
  12.3 1.4 %shard_map.61 = bf16[128,2,1152]{2,1,0:T(2,128)(2,1)} custom-call(bf16[256,1152]{1,0:T(8,128)(2,1)S(1)} %copy-done.3), custom_call_target="tpu_custom_call" | custom-call | bytes 1048576 | tf_op jit(solution)/shard_map/pallas_call | solution.py:369
  13.7 9.5 %all-to-all-start.1 = ((bf16[128,2,1152]{2,1,0:T(2,128)(2,1)}), bf16[128,2,1152]{2,1,0:T(2,128)(2,1)}, u32[]{:S(2)}, u32[]{:S(2)}) async-start(bf16[128,2,1152]{2,1,0:T(2,128)(2,1)} %shard_map.61), calls=%async_computation.1 | async-start | bytes 1179648 | tf_op jit(solution)/shard_map/all_to_all | solution.py:378
  23.3 0.0 collective-permute-done.1.refs_3_
  23.3 0.0 copy-start.5
  23.3 3.0 %collective-permute-done.refs_2_ = bf16[33,64,128]{2,1,0:T(8,128)(2,1)S(1)} collective-permute-done((bf16[33,64,128]{2,1,0:T(8,128)(2,1)S(1)}, bf16[33,64,128]{2,1,0:T(8,128)(2,1)S(1)}, u32[]{:S(2)}, u32[]{:S(2)}) %collective-permute-start) | collective-permute-done | bytes 540704 | tf_op jit(solution)/shard_map/ppermute | solution.py:47
  26.3 2.1 %collective-permute-start.5 = (bf16[17,64,128]{2,1,0:T(8,128)(2,1)S(1)}, bf16[17,64,128]{2,1,0:T(8,128)(2,1)S(1)}, u32[]{:S(2)}, u32[]{:S(2)}) collective-permute-start(bf16[17,64,128]{2,1,0:T(8,128)(2,1)S(1)} %get-tuple-element.18), channel_id=1, source_target_pairs={{0,7},{1,0},{2,1},{3,2},{4,3},{5,4},{6,5},{7,6},{8,15},{9,8},{10,9... | collective-permute-start | bytes 835592 | tf_op jit(solution)/shard_map/ppermute | solution.py:47
  28.4 1.2 %collective-permute-start.4 = (bf16[17,64,128]{2,1,0:T(8,128)(2,1)S(1)}, bf16[17,64,128]{2,1,0:T(8,128)(2,1)S(1)}, u32[]{:S(2)}, u32[]{:S(2)}) collective-permute-start(bf16[17,64,128]{2,1,0:T(8,128)(2,1)S(1)} %get-tuple-element.19), channel_id=1, source_target_pairs={{0,1},{1,2},{2,3},{3,4},{4,5},{5,6},{6,7},{7,0},{8,9},{9,10},{10,1... | collective-permute-start | bytes 835592 | tf_op jit(solution)/shard_map/ppermute | solution.py:47
  29.7 0.0 collective-permute-start.7
  29.7 0.0 collective-permute-done.3.refs_5_
  29.8 1.7 %collective-permute-start.6 = (bf16[17,64,128]{2,1,0:T(8,128)(2,1)S(1)}, bf16[17,64,128]{2,1,0:T(8,128)(2,1)S(1)}, u32[]{:S(2)}, u32[]{:S(2)}) collective-permute-start(bf16[17,64,128]{2,1,0:T(8,128)(2,1)S(1)} %get-tuple-element.17), channel_id=1, source_target_pairs={{0,1},{1,2},{2,3},{3,4},{4,5},{5,6},{6,7},{7,0},{8,9},{9,10},{10,1... | collective-permute-start | bytes 835592 | tf_op jit(solution)/shard_map/ppermute | solution.py:47
  31.5 0.0 collective-permute-done.2.refs_4_
  31.5 2.8 %collective-permute-done.5.refs_7_ = bf16[17,64,128]{2,1,0:T(8,128)(2,1)S(1)} collective-permute-done((bf16[17,64,128]{2,1,0:T(8,128)(2,1)S(1)}, bf16[17,64,128]{2,1,0:T(8,128)(2,1)S(1)}, u32[]{:S(2)}, u32[]{:S(2)}) %collective-permute-start.5) | collective-permute-done | bytes 278560 | tf_op jit(solution)/shard_map/ppermute | solution.py:47
  34.3 0.0 collective-permute-done.4.refs_6_
  34.3 3.0 %collective-permute-done.7.refs_9_ = bf16[17,64,128]{2,1,0:T(8,128)(2,1)S(1)} collective-permute-done((bf16[17,64,128]{2,1,0:T(8,128)(2,1)S(1)}, bf16[17,64,128]{2,1,0:T(8,128)(2,1)S(1)}, u32[]{:S(2)}, u32[]{:S(2)}) %collective-permute-start.7) | collective-permute-done | bytes 278560 | tf_op jit(solution)/shard_map/ppermute | solution.py:47
  37.3 0.0 collective-permute-done.6.refs_8_
  37.3 0.7 copy-done.9
  38.0 0.1 copy-done.10
  38.1 5.8 %shard_map.62 = s16[128,40,128]{2,1,0:T(8,128)(2,1)} custom-call(s32[32]{0:T(128)} %bitcast.5, f32[4,4,128]{2,1,0:T(4,128)} %pot_ref.7, bf16[33,64,128]{2,1,0:T(8,128)(2,1)} %copy-done, bf16[33,64,128]{2,1,0:T(8,128)(2,1)} %copy-done.1, bf16[33,64,128]{2,1,0:T(8,128)(2,1)} %copy-done.6, bf16[33,64,128]{2,1,0:T(8,128)(2,1)} %copy-done.5, ...), custom_call_target="tpu_custom_call" | custom-call | flops 536870912 | bytes 7340032 | tf_op jit(solution)/shard_map/pallas_call | solution.py:391
  43.9 0.0 all-to-all-done.1.kernel_ref
  43.9 8.6 %all-to-all-start = ((s16[128,40,128]{2,1,0:T(8,128)(2,1)}), s16[128,40,128]{2,1,0:T(8,128)(2,1)S(1)}, u32[]{:S(2)}, u32[]{:S(2)}) async-start(s16[128,40,128]{2,1,0:T(8,128)(2,1)} %shard_map.62), calls=%async_computation | async-start | bytes 2621440 | tf_op jit(solution)/shard_map/all_to_all | solution.py:406
  52.5 6.1 %shard_map.64 = bf16[32,2,8,8,128]{4,3,2,1,0:T(8,128)(2,1)} custom-call(s32[32]{0:T(128)} %bitcast.6, bf16[128,2,1152]{2,1,0:T(2,128)(2,1)} %all-to-all-done.1.kernel_ref, f32[4,4,128]{2,1,0:T(4,128)} %pot_ref.7, bf16[33,64,128]{2,1,0:T(8,128)(2,1)} %copy-done, bf16[33,64,128]{2,1,0:T(8,128)(2,1)} %copy-done.1, bf16[33,64,128]{2,1,0:T(8,128)(2,1)} %copy-done.6, ...), custom_call_target="tpu_custom_call" | custom-call | flops 268435456 | bytes 7340032 | tf_op jit(solution)/shard_map/pallas_call | solution.py:418
  58.6 14.0 %all-to-all-done.in_ref = s16[128,40,128]{2,1,0:T(8,128)(2,1)S(1)} async-done(((s16[128,40,128]{2,1,0:T(8,128)(2,1)}), s16[128,40,128]{2,1,0:T(8,128)(2,1)S(1)}, u32[]{:S(2)}, u32[]{:S(2)}) %all-to-all-start) | async-done | bytes 1310752 | tf_op jit(solution)/shard_map/all_to_all | solution.py:406
  72.6 2.0 %shard_map.63 = f32[256,2,1152]{2,1,0:T(2,128)} custom-call(s16[128,40,128]{2,1,0:T(8,128)(2,1)S(1)} %all-to-all-done.in_ref), custom_call_target="tpu_custom_call" | custom-call | tf_op jit(solution)/shard_map/pallas_call | solution.py:409
  (18 shorter events, 0.1 us)
Async XLA Ops:
  0.6 1.2 %copy-start.2 = (bf16[1,1,64,8,8,128]{5,4,3,2,1,0:T(8,128)(2,1)S(1)}, bf16[1,1,64,8,8,128]{5,4,3,2,1,0:T(8,128)(2,1)}, u32[]{:S(2)}) copy-start(bf16[1,1,64,8,8,128]{5,4,3,2,1,0:T(8,128)(2,1)} %param.5) | copy-start | bytes 3145732
  1.9 0.7 copy-start.4
  2.6 9.7 %copy-start.3 = (bf16[256,1152]{1,0:T(8,128)(2,1)S(1)}, bf16[256,1152]{1,0:T(8,128)(2,1)}, u32[]{:S(2)}) copy-start(bf16[256,1152]{1,0:T(8,128)(2,1)} %k_ref) | copy-start | bytes 1769476
  3.0 10.7 %copy-start = (bf16[33,64,128]{2,1,0:T(8,128)(2,1)}, bf16[33,64,128]{2,1,0:T(8,128)(2,1)S(1)}, u32[]{:S(2)}) copy-start(bf16[33,64,128]{2,1,0:T(8,128)(2,1)S(1)} %get-tuple-element.9.x0_ref.refs_0_) | copy-start | bytes 1622020
  3.0 10.7 %copy-start.1 = (bf16[33,64,128]{2,1,0:T(8,128)(2,1)}, bf16[33,64,128]{2,1,0:T(8,128)(2,1)S(1)}, u32[]{:S(2)}) copy-start(bf16[33,64,128]{2,1,0:T(8,128)(2,1)S(1)} %get-tuple-element.10.x1_ref.refs_1_) | copy-start | bytes 1622020
  3.0 20.2 %collective-permute-start.1 = (bf16[33,64,128]{2,1,0:T(8,128)(2,1)S(1)}, bf16[33,64,128]{2,1,0:T(8,128)(2,1)S(1)}, u32[]{:S(2)}, u32[]{:S(2)}) collective-permute-start(bf16[33,64,128]{2,1,0:T(8,128)(2,1)S(1)} %get-tuple-element.9.x0_ref.refs_0_), channel_id=1, source_target_pairs={{0,120},{8,0},{16,8},{24,16},{32,24},{40,32},{48,40},{56,48},{64,5... | collective-permute-start | bytes 1622024 | tf_op jit(solution)/shard_map/ppermute | solution.py:47
  10.1 16.1 %collective-permute-start = (bf16[33,64,128]{2,1,0:T(8,128)(2,1)S(1)}, bf16[33,64,128]{2,1,0:T(8,128)(2,1)S(1)}, u32[]{:S(2)}, u32[]{:S(2)}) collective-permute-start(bf16[33,64,128]{2,1,0:T(8,128)(2,1)S(1)} %get-tuple-element.10.x1_ref.refs_1_), channel_id=1, source_target_pairs={{0,8},{8,16},{16,24},{24,32},{32,40},{40,48},{48,56},{56,64},{64,7... | collective-permute-start | bytes 1622024 | tf_op jit(solution)/shard_map/ppermute | solution.py:47
  10.2 19.5 %collective-permute-start.3 = (bf16[33,64,128]{2,1,0:T(8,128)(2,1)S(1)}, bf16[33,64,128]{2,1,0:T(8,128)(2,1)}, u32[]{:S(2)}, u32[]{:S(2)}) collective-permute-start(bf16[33,64,128]{2,1,0:T(8,128)(2,1)S(1)} %get-tuple-element.11), channel_id=1, source_target_pairs={{0,7},{1,0},{2,1},{3,2},{4,3},{5,4},{6,5},{7,6},{8,15},{9,8},{10,9... | collective-permute-start | bytes 1622024 | tf_op jit(solution)/shard_map/ppermute | solution.py:47
  11.2 20.3 %collective-permute-start.2 = (bf16[33,64,128]{2,1,0:T(8,128)(2,1)S(1)}, bf16[33,64,128]{2,1,0:T(8,128)(2,1)}, u32[]{:S(2)}, u32[]{:S(2)}) collective-permute-start(bf16[33,64,128]{2,1,0:T(8,128)(2,1)S(1)} %get-tuple-element.12), channel_id=1, source_target_pairs={{0,1},{1,2},{2,3},{3,4},{4,5},{5,6},{6,7},{7,0},{8,9},{9,10},{10,1... | collective-permute-start | bytes 1622024 | tf_op jit(solution)/shard_map/ppermute | solution.py:47
  13.7 30.1 %all-to-all-start.1 = ((bf16[128,2,1152]{2,1,0:T(2,128)(2,1)}), bf16[128,2,1152]{2,1,0:T(2,128)(2,1)}, u32[]{:S(2)}, u32[]{:S(2)}) async-start(bf16[128,2,1152]{2,1,0:T(2,128)(2,1)} %shard_map.61), calls=%async_computation.1 | async-start | bytes 1179648 | tf_op jit(solution)/shard_map/all_to_all | solution.py:378
  23.3 14.0 %copy-start.5 = (bf16[33,64,128]{2,1,0:T(8,128)(2,1)}, bf16[33,64,128]{2,1,0:T(8,128)(2,1)S(1)}, u32[]{:S(2)}) copy-start(bf16[33,64,128]{2,1,0:T(8,128)(2,1)S(1)} %collective-permute-done.1.refs_3_) | copy-start | bytes 1622020
  26.3 11.0 %copy-start.6 = (bf16[33,64,128]{2,1,0:T(8,128)(2,1)}, bf16[33,64,128]{2,1,0:T(8,128)(2,1)S(1)}, u32[]{:S(2)}) copy-start(bf16[33,64,128]{2,1,0:T(8,128)(2,1)S(1)} %collective-permute-done.refs_2_) | copy-start | bytes 1622020
  26.3 8.0 %collective-permute-start.5 = (bf16[17,64,128]{2,1,0:T(8,128)(2,1)S(1)}, bf16[17,64,128]{2,1,0:T(8,128)(2,1)S(1)}, u32[]{:S(2)}, u32[]{:S(2)}) collective-permute-start(bf16[17,64,128]{2,1,0:T(8,128)(2,1)S(1)} %get-tuple-element.18), channel_id=1, source_target_pairs={{0,7},{1,0},{2,1},{3,2},{4,3},{5,4},{6,5},{7,6},{8,15},{9,8},{10,9... | collective-permute-start | bytes 835592 | tf_op jit(solution)/shard_map/ppermute | solution.py:47
  28.4 5.8 %collective-permute-start.4 = (bf16[17,64,128]{2,1,0:T(8,128)(2,1)S(1)}, bf16[17,64,128]{2,1,0:T(8,128)(2,1)S(1)}, u32[]{:S(2)}, u32[]{:S(2)}) collective-permute-start(bf16[17,64,128]{2,1,0:T(8,128)(2,1)S(1)} %get-tuple-element.19), channel_id=1, source_target_pairs={{0,1},{1,2},{2,3},{3,4},{4,5},{5,6},{6,7},{7,0},{8,9},{9,10},{10,1... | collective-permute-start | bytes 835592 | tf_op jit(solution)/shard_map/ppermute | solution.py:47
  29.7 7.5 %collective-permute-start.7 = (bf16[17,64,128]{2,1,0:T(8,128)(2,1)S(1)}, bf16[17,64,128]{2,1,0:T(8,128)(2,1)S(1)}, u32[]{:S(2)}, u32[]{:S(2)}) collective-permute-start(bf16[17,64,128]{2,1,0:T(8,128)(2,1)S(1)} %get-tuple-element.16), channel_id=1, source_target_pairs={{0,7},{1,0},{2,1},{3,2},{4,3},{5,4},{6,5},{7,6},{8,15},{9,8},{10,9... | collective-permute-start | bytes 835592 | tf_op jit(solution)/shard_map/ppermute | solution.py:47
  29.8 7.5 %collective-permute-start.6 = (bf16[17,64,128]{2,1,0:T(8,128)(2,1)S(1)}, bf16[17,64,128]{2,1,0:T(8,128)(2,1)S(1)}, u32[]{:S(2)}, u32[]{:S(2)}) collective-permute-start(bf16[17,64,128]{2,1,0:T(8,128)(2,1)S(1)} %get-tuple-element.17), channel_id=1, source_target_pairs={{0,1},{1,2},{2,3},{3,4},{4,5},{5,6},{6,7},{7,0},{8,9},{9,10},{10,1... | collective-permute-start | bytes 835592 | tf_op jit(solution)/shard_map/ppermute | solution.py:47
  34.3 3.0 %copy-start.7 = (bf16[17,64,128]{2,1,0:T(8,128)(2,1)}, bf16[17,64,128]{2,1,0:T(8,128)(2,1)S(1)}, u32[]{:S(2)}) copy-start(bf16[17,64,128]{2,1,0:T(8,128)(2,1)S(1)} %collective-permute-done.5.refs_7_) | copy-start | bytes 835588
  34.3 3.0 %copy-start.8 = (bf16[17,64,128]{2,1,0:T(8,128)(2,1)}, bf16[17,64,128]{2,1,0:T(8,128)(2,1)S(1)}, u32[]{:S(2)}) copy-start(bf16[17,64,128]{2,1,0:T(8,128)(2,1)S(1)} %collective-permute-done.4.refs_6_) | copy-start | bytes 835588
  37.3 0.7 copy-start.9
  37.3 0.8 %copy-start.10 = (bf16[17,64,128]{2,1,0:T(8,128)(2,1)}, bf16[17,64,128]{2,1,0:T(8,128)(2,1)S(1)}, u32[]{:S(2)}) copy-start(bf16[17,64,128]{2,1,0:T(8,128)(2,1)S(1)} %collective-permute-done.6.refs_8_) | copy-start | bytes 835588
  43.9 28.7 %all-to-all-start = ((s16[128,40,128]{2,1,0:T(8,128)(2,1)}), s16[128,40,128]{2,1,0:T(8,128)(2,1)S(1)}, u32[]{:S(2)}, u32[]{:S(2)}) async-start(s16[128,40,128]{2,1,0:T(8,128)(2,1)} %shard_map.62), calls=%async_computation | async-start | bytes 2621440 | tf_op jit(solution)/shard_map/all_to_all | solution.py:406
